TPU v7x, 32 devices: a whole 2x2x4 slice. The times are simulated.
32 devices in a mesh: src: 4 (over y, x), dst: 8 (over z, core).
Axes of the slice: x: 2, y: 2, z: 4, core: 2. Of those that a mesh axis runs over, the one named last changes fastest.
Arguments:
- src_emb: float32 [32768, 256], P(('src', 'dst')), may hold values from -2 to 2
- src_acc: float32 [32768], P(('src', 'dst')), may hold values from 0.001 to 0.03
- dst_emb: float32 [16384, 256], P(('src', 'dst')), may hold values from -2 to 2
- dst_acc: float32 [16384], P(('src', 'dst')), may hold values from 0.001 to 0.03
- rel_emb: float32 [128, 256], replicated, may hold values from -4 to 4
- rel_acc: float32 [128], replicated, may hold values from 0.001 to 0.03
- edge_src: int32 [4, 8, 4, 8, 128], P('src', 'dst'), may hold values from 0 to 1023
- edge_dst: int32 [4, 8, 4, 8, 128], P('src', 'dst'), may hold values from 0 to 511
- edge_rel: int32 [4, 8, 4, 8, 128], P('src', 'dst'), may hold values from 0 to 127
- negatives: int32 [4, 8, 4, 8, 128], P('src', 'dst'), may hold values from 0 to 511
Outputs:
- src_out: float32 [32768, 256], P(('src', 'dst'))
- src_acc_out: float32 [32768], P(('src', 'dst'))
- dst_out: float32 [16384, 256], P(('src', 'dst'))
- dst_acc_out: float32 [16384], P(('src', 'dst'))
- rel_out: float32 [128, 256], replicated
- rel_acc_out: float32 [128], replicated
All inputs are finite; a program needn't handle non-finite values.
Results may differ from a plain program's by a relative error of at most 0.0003.
Values sent between devices are 32-bit elements; how exact they have to be, the bound alone decides.
No kernel may reach another device: no remote copies, remote signals or barrier semaphores. Data moves between devices by JAX's collectives and lax.ppermute only.
A program may use at most 64 MiB of HBM per device.

v0:
```python
import jax
import jax.numpy as jnp
from jax import lax
from jax.sharding import PartitionSpec as P

STEPS = 4


def shifted(value, axis, steps):
    count = lax.axis_size(axis)
    pairs = [(source, (source + steps) % count) for source in range(count)]
    return lax.ppermute(value, axis, pairs)


def bucket_grads(src_block, dst_block, rel_emb, src_ids, dst_ids, rel_ids, neg_ids):
    highest = lax.Precision.HIGHEST
    width = src_block.shape[-1]
    onehot = (rel_ids[..., None] == jnp.arange(rel_emb.shape[0], dtype=jnp.int32)).astype(
        src_block.dtype
    )
    rel_rows = jnp.einsum("cbr,rd->cbd", onehot, rel_emb, precision=highest)
    src_rows = src_block[src_ids]
    dst_rows = dst_block[dst_ids]
    neg_rows = dst_block[neg_ids]
    query = src_rows * rel_rows
    positive = jnp.sum(query * dst_rows, axis=-1)
    scores = jnp.einsum("cbd,ckd->cbk", query, neg_rows, precision=highest)
    pos_weight = -jax.nn.sigmoid(-positive)
    neg_weight = jax.nn.sigmoid(scores) / neg_ids.shape[-1]
    grad_query = pos_weight[..., None] * dst_rows + jnp.einsum(
        "cbk,ckd->cbd", neg_weight, neg_rows, precision=highest
    )
    grad_dst_pos = pos_weight[..., None] * query
    grad_neg = jnp.einsum("cbk,cbd->ckd", neg_weight, query, precision=highest)
    rel_grad = jnp.einsum("cbr,cbd->rd", onehot, grad_query * src_rows, precision=highest)
    src_grad = (
        jnp.zeros_like(src_block)
        .at[src_ids.reshape(-1)]
        .add((grad_query * rel_rows).reshape(-1, width))
    )
    dst_grad = (
        jnp.zeros_like(dst_block).at[dst_ids.reshape(-1)].add(grad_dst_pos.reshape(-1, width))
    )
    dst_grad = dst_grad.at[neg_ids.reshape(-1)].add(grad_neg.reshape(-1, width))
    return (src_grad, dst_grad, rel_grad)


def adagrad_rows(embedding, summed, grad):
    new_sum = summed + jnp.mean(grad * grad, axis=-1)
    return (embedding - 0.3 * grad / (jnp.sqrt(new_sum)[..., None] + 1e-10), new_sum)


def train_bucket(state, edge_pack, neg_ids):
    src_emb, src_acc, dst_emb, dst_acc, rel_emb, rel_acc = state
    src_grad, dst_grad, rel_part = bucket_grads(
        src_emb, dst_emb, rel_emb, edge_pack[0], edge_pack[1], edge_pack[2], neg_ids
    )
    rel_grad = lax.psum(rel_part, ("src", "dst"))
    src_emb, src_acc = adagrad_rows(src_emb, src_acc, src_grad)
    dst_emb, dst_acc = adagrad_rows(dst_emb, dst_acc, dst_grad)
    rel_emb, rel_acc = adagrad_rows(rel_emb, rel_acc, rel_grad)
    return (src_emb, src_acc, dst_emb, dst_acc, rel_emb, rel_acc)


def local(
    src_emb, src_acc, dst_emb, dst_acc, rel_emb, rel_acc, edge_src, edge_dst, edge_rel, negatives
):
    edge_pack = jnp.stack([edge_src[0, 0], edge_dst[0, 0], edge_rel[0, 0]])
    neg_pack = negatives[0, 0]
    state = (src_emb, src_acc, dst_emb, dst_acc, rel_emb, rel_acc)
    for step in range(STEPS):
        if step > 0:
            moved_emb, moved_acc = shifted((state[0], state[1]), "dst", -1)
            edge_pack, neg_pack = shifted((edge_pack, neg_pack), "dst", -1)
            state = (moved_emb, moved_acc, state[2], state[3], state[4], state[5])
        state = train_bucket(state, edge_pack[:, step], neg_pack[step])
    home_emb, home_acc = shifted((state[0], state[1]), "dst", STEPS - 1)
    state = (home_emb, home_acc, state[2], state[3], state[4], state[5])
    return state


def solution(mesh):
    return jax.shard_map(
        local,
        mesh=mesh,
        in_specs=(
            P(("src", "dst"), None),
            P(("src", "dst")),
            P(("src", "dst"), None),
            P(("src", "dst")),
            P(),
            P(),
            P("src", "dst", None, None, None),
            P("src", "dst", None, None, None),
            P("src", "dst", None, None, None),
            P("src", "dst", None, None, None),
        ),
        out_specs=(
            P(("src", "dst"), None),
            P(("src", "dst")),
            P(("src", "dst"), None),
            P(("src", "dst")),
            P(),
            P(),
        ),
        check_vma=False,
    )
```

profile of v0, /device:TPU:1, one launch (start us, length us, event | category | flops | bytes accessed | tf_op | source)
XLA Modules:
  0.0 621.1 jit_solution(4626486018556463571)
XLA Ops:
  18.0 4.7 gather_fusion.1
  22.7 4.7 gather_fusion
  34.7 6.8 %scatter_custom_fusion = f32[1024,256]{1,0:T(8,128)S(1)} fusion(s32[1024]{0:T(1024)S(1)} %bitcast.252, f32[1024,256]{1,0:T(8,128)} %bitcast.212, f32[]{:T(128)} %constant.16.clone.1), kind=kCustom, calls=%fused_computation.94 | custom fusion | flops 262144 | bytes 1049088 | tf_op jit(solution)/shard_map/scatter-add | solution.py:39
  48.2 6.7 %scatter_custom_fusion.1 = f32[512,256]{1,0:T(8,128)S(1)} fusion(s32[1024]{0:T(1024)S(1)} %bitcast.251, f32[1024,256]{1,0:T(8,128)} %bitcast.219, f32[]{:T(128)} %constant.16.clone.1), kind=kCustom, calls=%fused_computation.106 | custom fusion | flops 262144 | bytes 524800 | tf_op jit(solution)/shard_map/scatter-add | solution.py:42
  54.8 6.8 %scatter_fusion = f32[512,256]{1,0:T(8,128)S(1)} fusion(f32[512,256]{1,0:T(8,128)S(1)} %scatter_custom_fusion.1, s32[1024]{0:T(1024)S(1)} %bitcast.231, f32[1024,256]{1,0:T(8,128)} %bitcast.211), kind=kCustom, calls=%fused_computation.14 | custom fusion | flops 262144 | bytes 3149824 | tf_op jit(solution)/shard_map/scatter-add | solution.py:44
  63.0 4.7 gather_fusion.5
  75.7 79.5 %all-reduce.5.cloned.1.call-done = f32[128,256]{1,0:T(8,128)} async-done(((f32[128,256]{1,0:T(8,128)}), f32[128,256]{1,0:T(8,128)}) %all-reduce.5.cloned.1.call-update) | async-done | bytes 131088 | tf_op jit(solution)/shard_map/psum | solution.py:58
  163.8 4.7 gather_fusion.3
  178.6 6.8 %scatter_custom_fusion.3 = f32[1024,256]{1,0:T(8,128)S(1)} fusion(s32[1024]{0:T(1024)S(1)} %bitcast.250, f32[1024,256]{1,0:T(8,128)} %bitcast.213, f32[]{:T(128)} %constant.16.clone.1), kind=kCustom, calls=%fused_computation.92 | custom fusion | flops 262144 | bytes 1049088 | tf_op jit(solution)/shard_map/scatter-add | solution.py:39
  186.4 6.7 %scatter_custom_fusion.4 = f32[512,256]{1,0:T(8,128)S(1)} fusion(s32[1024]{0:T(1024)S(1)} %bitcast.249, f32[1024,256]{1,0:T(8,128)} %bitcast.217, f32[]{:T(128)} %constant.16.clone.1), kind=kCustom, calls=%fused_computation.104 | custom fusion | flops 262144 | bytes 524800 | tf_op jit(solution)/shard_map/scatter-add | solution.py:42
  193.0 6.9 %scatter_fusion.1 = f32[512,256]{1,0:T(8,128)S(1)} fusion(f32[512,256]{1,0:T(8,128)S(1)} %scatter_custom_fusion.4, s32[1024]{0:T(1024)S(1)} %bitcast.230, f32[1024,256]{1,0:T(8,128)} %bitcast.209), kind=kCustom, calls=%fused_computation.17 | custom fusion | flops 262144 | bytes 3149824 | tf_op jit(solution)/shard_map/scatter-add | solution.py:44
  208.8 4.7 gather_fusion.7
  213.5 87.4 %all-reduce.7.cloned.1.call-done = f32[128,256]{1,0:T(8,128)} async-done(((f32[128,256]{1,0:T(8,128)}), f32[128,256]{1,0:T(8,128)}) %all-reduce.7.cloned.1.call-update) | async-done | bytes 131088 | tf_op jit(solution)/shard_map/psum | solution.py:58
  303.9 4.7 gather_fusion.6
  318.0 6.8 %scatter_custom_fusion.6 = f32[1024,256]{1,0:T(8,128)S(1)} fusion(s32[1024]{0:T(1024)} %bitcast.248, f32[1024,256]{1,0:T(8,128)} %bitcast.215, f32[]{:T(128)} %constant.16.clone.1), kind=kCustom, calls=%fused_computation.90 | custom fusion | flops 262144 | bytes 1049088 | tf_op jit(solution)/shard_map/scatter-add | solution.py:39
  330.6 6.7 %scatter_custom_fusion.7 = f32[512,256]{1,0:T(8,128)S(1)} fusion(s32[1024]{0:T(1024)} %bitcast.247, f32[1024,256]{1,0:T(8,128)} %bitcast.216, f32[]{:T(128)} %constant.16.clone.1), kind=kCustom, calls=%fused_computation.102 | custom fusion | flops 262144 | bytes 524800 | tf_op jit(solution)/shard_map/scatter-add | solution.py:42
  337.2 6.8 %scatter_fusion.2 = f32[512,256]{1,0:T(8,128)S(1)} fusion(f32[512,256]{1,0:T(8,128)S(1)} %scatter_custom_fusion.7, s32[1024]{0:T(1024)S(1)} %bitcast.229, f32[1024,256]{1,0:T(8,128)} %bitcast.208), kind=kCustom, calls=%fused_computation.20 | custom fusion | flops 262144 | bytes 3149824 | tf_op jit(solution)/shard_map/scatter-add | solution.py:44
  344.9 4.7 gather_fusion.11
  353.0 97.7 %all-reduce.9.cloned.1.call-done = f32[128,256]{1,0:T(8,128)} async-done(((f32[128,256]{1,0:T(8,128)}), f32[128,256]{1,0:T(8,128)}) %all-reduce.9.cloned.1.call-update) | async-done | bytes 131088 | tf_op jit(solution)/shard_map/psum | solution.py:58
  452.4 4.7 gather_fusion.9
  467.1 6.8 %scatter_custom_fusion.9 = f32[1024,256]{1,0:T(8,128)S(1)} fusion(s32[1024]{0:T(1024)} %bitcast.246, f32[1024,256]{1,0:T(8,128)} %bitcast.214, f32[]{:T(128)} %constant.16.clone.1), kind=kCustom, calls=%fused_computation.88 | custom fusion | flops 262144 | bytes 1049088 | tf_op jit(solution)/shard_map/scatter-add | solution.py:39
  476.6 6.7 %scatter_custom_fusion.10 = f32[512,256]{1,0:T(8,128)S(1)} fusion(s32[1024]{0:T(1024)} %bitcast.245, f32[1024,256]{1,0:T(8,128)} %bitcast.218, f32[]{:T(128)} %constant.16.clone.1), kind=kCustom, calls=%fused_computation.100 | custom fusion | flops 262144 | bytes 524800 | tf_op jit(solution)/shard_map/scatter-add | solution.py:42
  483.2 7.0 %scatter_fusion.3 = f32[512,256]{1,0:T(8,128)S(1)} fusion(f32[512,256]{1,0:T(8,128)S(1)} %scatter_custom_fusion.10, s32[1024]{0:T(1024)S(1)} %bitcast.228, f32[1024,256]{1,0:T(8,128)} %bitcast.210), kind=kCustom, calls=%fused_computation.23 | custom fusion | flops 262144 | bytes 3149824 | tf_op jit(solution)/shard_map/scatter-add | solution.py:44
  493.1 117.0 %all-reduce.11.cloned.1.call-done = f32[128,256]{1,0:T(8,128)} async-done(((f32[128,256]{1,0:T(8,128)}), f32[128,256]{1,0:T(8,128)}) %all-reduce.11.cloned.1.call-update) | async-done | bytes 131088 | tf_op jit(solution)/shard_map/psum | solution.py:58
  (202 shorter events, 105.9 us)
Async XLA Ops:
  7.2 148.0 %all-reduce.5.cloned.1.call-start = ((), (), s32[]{:S(2)}) async-start(), calls=%async_computation | async-start | bytes 262144 | tf_op jit(solution)/shard_map/psum | solution.py:58
  7.2 55.2 %collective-permute-start.2 = (s32[4,8,128]{2,1,0:T(8,128)}, s32[4,8,128]{2,1,0:T(8,128)S(1)}, u32[]{:S(2)}, u32[]{:S(2)}) collective-permute-start(s32[4,8,128]{2,1,0:T(8,128)} %bitcast.244), channel_id=1, source_target_pairs={{0,7},{1,0},{2,1},{3,2},{4,3},{5,4},{6,5},{7,6},{8,15},{9,8},{10,9... | collective-permute-start | bytes 49160 | tf_op jit(solution)/shard_map/ppermute | solution.py:12
  7.3 6.0 copy-start.19
  7.3 6.0 copy-start.20
  8.1 64.0 %collective-permute-start.1 = (s32[3,4,8,128]{3,2,1,0:T(8,128)S(1)}, s32[3,4,8,128]{3,2,1,0:T(8,128)S(1)}, u32[]{:S(2)}, u32[]{:S(2)}) collective-permute-start(s32[3,4,8,128]{3,2,1,0:T(8,128)S(1)} %pad_add_fusion), channel_id=1, source_target_pairs={{0,7},{1,0},{2,1},{3,2},{4,3},{5,4},{6,5},{7,6},{8,15},{9,8},{10,9... | collective-permute-start | bytes 147464 | tf_op jit(solution)/shard_map/ppermute | solution.py:12
  34.6 266.3 %all-reduce.7.cloned.1.call-start = ((), (), s32[]{:S(2)}) async-start(), calls=%async_computation.1 | async-start | bytes 262144 | tf_op jit(solution)/shard_map/psum | solution.py:58
  42.8 142.9 %collective-permute-start.3 = (f32[1024]{0:T(1024)}, f32[1024]{0:T(1024)S(1)}, u32[]{:S(2)}, u32[]{:S(2)}) collective-permute-start(f32[1024]{0:T(1024)} %get-tuple-element.27), channel_id=1, source_target_pairs={{0,7},{1,0},{2,1},{3,2},{4,3},{5,4},{6,5},{7,6},{8,15},{9,8},{10,9... | collective-permute-start | bytes 12296 | tf_op jit(solution)/shard_map/ppermute | solution.py:12
  44.6 119.2 %collective-permute-start = (f32[1024,256]{1,0:T(8,128)}, f32[1024,256]{1,0:T(8,128)S(1)}, u32[]{:S(2)}, u32[]{:S(2)}) collective-permute-start(f32[1024,256]{1,0:T(8,128)} %divide_subtract_fusion.3), channel_id=1, source_target_pairs={{0,7},{1,0},{2,1},{3,2},{4,3},{5,4},{6,5},{7,6},{8,15},{9,8},{10,9... | collective-permute-start | bytes 3145736 | tf_op jit(solution)/shard_map/ppermute | solution.py:12
  62.5 5.2 collective-permute-start.6
  68.3 3.2 collective-permute-start.10
  75.6 80.6 %copy-start.32 = (f32[128]{0:T(128)S(1)}, f32[128]{0:T(128)}, u32[]{:S(2)}) copy-start(f32[128]{0:T(128)} %param.15) | copy-start | bytes 1540
  75.6 80.6 %collective-permute-start.5 = (s32[3,4,8,128]{3,2,1,0:T(8,128)S(1)}, s32[3,4,8,128]{3,2,1,0:T(8,128)S(1)}, u32[]{:S(2)}, u32[]{:S(2)}) collective-permute-start(s32[3,4,8,128]{3,2,1,0:T(8,128)S(1)} %collective-permute-done.1), channel_id=1, source_target_pairs={{0,7},{1,0},{2,1},{3,2},{4,3},{5,4},{6,5},{7,6},{8,15},{9,8},{10,9... | collective-permute-start | bytes 147464 | tf_op jit(solution)/shard_map/ppermute | solution.py:12
  156.2 12.3 %copy-start.30 = (f32[128]{0:T(128)}, f32[128]{0:T(128)S(1)}, u32[]{:S(2)}) copy-start(f32[128]{0:T(128)S(1)} %sqrt_add_fusion.11) | copy-start | bytes 1540
  157.5 4.6 collective-permute-start.9
  178.5 272.2 %all-reduce.9.cloned.1.call-start = ((), (), s32[]{:S(2)}) async-start(), calls=%async_computation.2 | async-start | bytes 262144 | tf_op jit(solution)/shard_map/psum | solution.py:58
  186.3 138.7 %collective-permute-start.7 = (f32[1024]{0:T(1024)}, f32[1024]{0:T(1024)}, u32[]{:S(2)}, u32[]{:S(2)}) collective-permute-start(f32[1024]{0:T(1024)} %get-tuple-element.23), channel_id=1, source_target_pairs={{0,7},{1,0},{2,1},{3,2},{4,3},{5,4},{6,5},{7,6},{8,15},{9,8},{10,9... | collective-permute-start | bytes 12296 | tf_op jit(solution)/shard_map/ppermute | solution.py:12
  202.5 100.8 %collective-permute-start.4 = (f32[1024,256]{1,0:T(8,128)}, f32[1024,256]{1,0:T(8,128)S(1)}, u32[]{:S(2)}, u32[]{:S(2)}) collective-permute-start(f32[1024,256]{1,0:T(8,128)} %divide_subtract_fusion.2), channel_id=1, source_target_pairs={{0,7},{1,0},{2,1},{3,2},{4,3},{5,4},{6,5},{7,6},{8,15},{9,8},{10,9... | collective-permute-start | bytes 3145736 | tf_op jit(solution)/shard_map/ppermute | solution.py:12
  326.9 124.8 %collective-permute-start.8 = (f32[1024,256]{1,0:T(8,128)}, f32[1024,256]{1,0:T(8,128)S(1)}, u32[]{:S(2)}, u32[]{:S(2)}) collective-permute-start(f32[1024,256]{1,0:T(8,128)} %divide_subtract_fusion.1), channel_id=1, source_target_pairs={{0,7},{1,0},{2,1},{3,2},{4,3},{5,4},{6,5},{7,6},{8,15},{9,8},{10,9... | collective-permute-start | bytes 3145736 | tf_op jit(solution)/shard_map/ppermute | solution.py:12
  329.6 280.6 %all-reduce.11.cloned.1.call-start = ((), (), s32[]{:S(2)}) async-start(), calls=%async_computation.3 | async-start | bytes 262144 | tf_op jit(solution)/shard_map/psum | solution.py:58
  329.6 144.4 %collective-permute-start.11 = (f32[1024]{0:T(1024)S(1)}, f32[1024]{0:T(1024)S(1)}, u32[]{:S(2)}, u32[]{:S(2)}) collective-permute-start(f32[1024]{0:T(1024)S(1)} %get-tuple-element.15), channel_id=1, source_target_pairs={{0,7},{1,0},{2,1},{3,2},{4,3},{5,4},{6,5},{7,6},{8,15},{9,8},{10,9... | collective-permute-start | bytes 12296 | tf_op jit(solution)/shard_map/ppermute | solution.py:12
  330.6 6.7 %copy-start.21 = (s32[1024,1]{0,1:T(1,128)S(1)}, s32[1024,1]{0,1:T(1,128)}, u32[]{:S(2)}) copy-start(s32[1024,1]{0,1:T(1,128)} %compare_select_fusion.2) | copy-start | bytes 12292
  349.5 102.2 %copy-start.29 = (f32[128]{0:T(128)S(1)}, f32[128]{0:T(128)}, u32[]{:S(2)}) copy-start(f32[128]{0:T(128)} %get-tuple-element.21) | copy-start | bytes 1540
  474.1 19.0 %collective-permute-start.13 = (f32[1024]{0:T(1024)S(1)}, f32[1024]{0:T(1024)S(1)}, u32[]{:S(2)}, u32[]{:S(2)}) collective-permute-start(f32[1024]{0:T(1024)S(1)} %get-tuple-element.11), channel_id=1, source_target_pairs={{0,3},{1,4},{2,5},{3,6},{4,7},{5,0},{6,1},{7,2},{8,11},{9,12},{10,... | collective-permute-start | bytes 12296 | tf_op jit(solution)/shard_map/ppermute | solution.py:12
  491.6 120.9 %collective-permute-start.12 = (f32[1024,256]{1,0:T(8,128)}, f32[1024,256]{1,0:T(8,128)S(1)}, u32[]{:S(2)}, u32[]{:S(2)}) collective-permute-start(f32[1024,256]{1,0:T(8,128)} %divide_subtract_fusion), channel_id=1, source_target_pairs={{0,3},{1,4},{2,5},{3,6},{4,7},{5,0},{6,1},{7,2},{8,11},{9,12},{10,... | collective-permute-start | bytes 3145736 | tf_op jit(solution)/shard_map/ppermute | solution.py:12
  (27 other events, 63.0 us)
Sparse Core Ops, SparseCore 0:
  34.7 120.4 all-reduce.4
  178.7 122.2 all-reduce.6
  329.7 120.9 all-reduce.8
  467.2 142.9 all-reduce.10
where the time goes:
time: 629 us; the launch traced here: 621 us
  waiting for transfers between devices  387 us (62%)
  other arithmetic  109 us (17%)
  local copies, waits for them, and re-layouts  58.8 us (9%)
  matrix products  35.4 us (6%)
  starting transfers between devices  15.5 us (2%)
  between operations  14.9 us (2%)
    psum x4, waiting for transfers between devices, train_bucket(): rel_grad = lax.psum(rel_part, ('src', 'dst'))  382 us
    scatter-add x4, other arithmetic, bucket_grads(): dst_grad = dst_grad.at[neg_ids.reshape(-1)].add(grad_neg.reshape(-1, width))  27.5 us
    scatter-add x4, other arithmetic, bucket_grads(): src_grad = jnp.zeros_like(src_block).at[src_ids.reshape(-1)].add((grad_qu...  27.1 us
    scatter-add x4, other arithmetic, bucket_grads(): jnp.zeros_like(dst_block).at[dst_ids.reshape(-1)]  26.6 us
    gather x4, local copies, waits for them, and re-layouts, bucket_grads(): src_rows = src_block[src_ids]  18.7 us
    gather x4, local copies, waits for them, and re-layouts, bucket_grads(): neg_rows = dst_block[neg_ids]  17.4 us
    gather x4, local copies, waits for them, and re-layouts, bucket_grads(): dst_rows = dst_block[dst_ids]  16.3 us
    ppermute x14, starting transfers between devices, shifted(): return lax.ppermute(value, axis, pairs)  15.3 us
  transfers between devices with their start and end apart: 18, of which 6 were waited for; matrix products, arithmetic and copies ran while one was open for 32% of the time, Pallas kernels for 0%

commit v1 on v0

v1 whole, which is shorter than its diff:
```python
import functools

import jax
import jax.numpy as jnp
from jax import lax
from jax.experimental import pallas as pl
from jax.experimental.pallas import tpu as pltpu
from jax.sharding import PartitionSpec as P

STEPS = 4
RATE = 0.3
EPS = 1e-10
F32 = jnp.float32
BF16 = jnp.bfloat16
LANES = 128
CHUNK = 256


def halves(value):
    high = value.astype(BF16)
    return high, (value - high.astype(F32)).astype(BF16)


def dot(lhs, rhs, lhs_dim=1, rhs_dim=0):
    return lax.dot_general(
        lhs, rhs, (((lhs_dim,), (rhs_dim,)), ((), ())), preferred_element_type=F32
    )


def columns(rows):
    return jnp.transpose(rows)


def hot_columns(cols, first, blocks, width):
    lane = lax.broadcasted_iota(jnp.int32, (LANES, width), 1)
    parts = [
        jnp.where(cols[:, b : b + 1] == lane, 1.0, 0.0).astype(BF16)
        for b in range(first, first + blocks)
    ]
    return jnp.concatenate(parts, axis=0)


def hot_rows(ids, first, blocks, start, height):
    row = lax.broadcasted_iota(jnp.int32, (height, LANES), 0) + start
    parts = [
        jnp.where(row == ids[b : b + 1, :], 1.0, 0.0).astype(BF16)
        for b in range(first, first + blocks)
    ]
    return jnp.concatenate(parts, axis=1)


def row_scale(summed, grad):
    total = summed + jnp.sum(grad * grad, axis=1, keepdims=True) * (1.0 / grad.shape[1])
    return total, RATE / (jnp.sqrt(total) + EPS)


def gather_rows(cols, stack, out_ref, edges, rows):
    blocks = CHUNK // LANES
    for c in range(edges // CHUNK):
        hot = hot_columns(cols, c * blocks, blocks, rows)
        out_ref[c * CHUNK : (c + 1) * CHUNK, :] = dot(jnp.concatenate([hot, hot], axis=1), stack)


def first_kernel(ids_ref, src_ref, out_ref, stack_ref):
    rows = src_ref.shape[0]
    high, low = halves(src_ref[...])
    stack_ref[0:rows, :] = high
    stack_ref[rows : 2 * rows, :] = low
    gather_rows(columns(ids_ref[0]), stack_ref[...], out_ref, out_ref.shape[0], rows)


def count_kernel(neg_ref, out_ref):
    steps, blocks, negs = neg_ref.shape
    rows = out_ref.shape[2]
    for t in range(steps):
        cols = columns(neg_ref[t])
        lane = lax.broadcasted_iota(jnp.int32, (negs, rows), 1)
        parts = [
            jnp.sum(jnp.where(cols[:, b : b + 1] == lane, 1.0 / negs, 0.0), axis=0, keepdims=True)
            for b in range(blocks)
        ]
        out_ref[t] = jnp.concatenate(parts, axis=0)


def relation_update(core_ref, mine_ref, peer_ref, rel_ref, acc_ref):
    first = core_ref[0] == 0
    mine, peer = mine_ref[...], peer_ref[...]
    grad = jnp.concatenate(
        [jnp.where(first, mine, peer), jnp.where(first, peer, mine)], axis=0
    )
    total, scale = row_scale(acc_ref[...], grad)
    return rel_ref[...] - grad * scale, total


def query_kernel(step, updated, *refs):
    if updated:
        core_ref, mine_ref, peer_ref, acc_ref = refs[:4]
        refs = refs[4:]
    else:
        core_ref = refs[0]
        refs = refs[1:]
    rel_ref, src_ref, dst_ref, eds_ref, erl_ref, cnt_ref = refs[:6]
    refs = refs[6:]
    keep_ref, send_ref, wgt_ref, qry_ref, gsr_ref = refs[:5]
    refs = refs[5:]
    if updated:
        rel_out_ref, acc_out_ref = refs
        rel, total = relation_update(core_ref, mine_ref, peer_ref, rel_ref, acc_ref)
        rel_out_ref[...] = rel
        acc_out_ref[...] = total
    else:
        rel = rel_ref[...]
    edges = src_ref.shape[0]
    rows = cnt_ref.shape[2]
    nrel = rel.shape[0]
    blocks = CHUNK // LANES
    rel_stack = jnp.concatenate(halves(rel), axis=0)
    dst_high, dst_low = halves(dst_ref[0:rows, :])
    dst_wide = jnp.concatenate([dst_high, dst_low, dst_high], axis=1)
    dst_tall = jnp.concatenate([dst_high, dst_low, dst_high], axis=0)
    rel_cols = columns(erl_ref[step])
    dst_cols = columns(eds_ref[step])
    lane = lax.broadcasted_iota(jnp.int32, (LANES, rows), 1)
    counts = cnt_ref[step]
    grad = None
    for c in range(edges // CHUNK):
        at = slice(c * CHUNK, (c + 1) * CHUNK)
        hot = hot_columns(rel_cols, c * blocks, blocks, nrel)
        rel_rows = dot(jnp.concatenate([hot, hot], axis=1), rel_stack)
        src_rows = src_ref[at, :]
        query = src_rows * rel_rows
        q_high, q_low = halves(query)
        qry_ref[0, at, :] = q_high
        qry_ref[1, at, :] = q_low
        scores = dot(jnp.concatenate([q_high, q_high, q_low], axis=1), dst_wide, 1, 1)
        chance = 0.5 * jnp.tanh(0.5 * scores) + 0.5
        parts = []
        for b in range(blocks):
            block = c * blocks + b
            part = chance[b * LANES : (b + 1) * LANES, :]
            hit = dst_cols[:, block : block + 1] == lane
            parts.append(part * counts[block : block + 1, :] + jnp.where(hit, part - 1.0, 0.0))
        weight = jnp.concatenate(parts, axis=0)
        w_high, w_low = halves(weight)
        wgt_ref[0, at, :] = w_high
        wgt_ref[1, at, :] = w_low
        grad_query = dot(jnp.concatenate([w_high, w_high, w_low], axis=1), dst_tall)
        g_high, g_low = halves(grad_query * rel_rows)
        gsr_ref[0, at, :] = g_high
        gsr_ref[1, at, :] = g_low
        hot_t = hot_rows(erl_ref[step], c * blocks, blocks, 0, nrel)
        part = dot(
            jnp.concatenate([hot_t, hot_t], axis=1),
            jnp.concatenate(halves(grad_query * src_rows), axis=0),
        )
        grad = part if grad is None else grad + part
    first = core_ref[0] == 0
    half = nrel // 2
    top, bottom = grad[:half], grad[half:]
    keep_ref[...] = jnp.where(first, top, bottom)
    send_ref[...] = jnp.where(first, bottom, top)


def dst_kernel(wgt_ref, qry_ref, dst_ref, out_ref):
    rows = wgt_ref.shape[2]
    width = dst_ref.shape[1]
    grad = (
        dot(wgt_ref[0], qry_ref[0], 0, 0)
        + dot(wgt_ref[0], qry_ref[1], 0, 0)
        + dot(wgt_ref[1], qry_ref[0], 0, 0)
    )
    blocks = rows // LANES
    sums = jnp.concatenate(
        [dst_ref[rows : rows + blocks, 0:LANES], jnp.zeros((8 - blocks, LANES), F32)], axis=0
    ) if blocks < 8 else dst_ref[rows : rows + blocks, 0:LANES]
    cols = columns(sums)
    totals = []
    for b in range(blocks):
        at = slice(b * LANES, (b + 1) * LANES)
        total, scale = row_scale(cols[:, b : b + 1], grad[at])
        out_ref[at, :] = dst_ref[at, :] - grad[at] * scale
        totals.append(total)
    fresh = jnp.transpose(jnp.concatenate(totals + [totals[0]] * (8 - blocks), axis=1))
    out_ref[rows : rows + 8, :] = jnp.concatenate(
        [fresh, jnp.zeros((8, width - LANES), F32)], axis=1
    )


def src_kernel(step, last, esr_ref, gsr_ref, src_ref, acc_ref, *refs):
    if last:
        src_out_ref, acc_out_ref = refs
    else:
        src_out_ref, acc_out_ref, next_ref, stack_ref = refs
    rows = src_ref.shape[0]
    edges = gsr_ref.shape[1]
    gsr = jnp.concatenate([gsr_ref[0], gsr_ref[1]], axis=0)
    cols = columns(acc_ref[...])
    totals = []
    for m in range(rows // CHUNK):
        at = slice(m * CHUNK, (m + 1) * CHUNK)
        hot_t = hot_rows(esr_ref[step], 0, edges // LANES, m * CHUNK, CHUNK)
        grad = dot(jnp.concatenate([hot_t, hot_t], axis=1), gsr)
        summed = jnp.concatenate(
            [
                cols[:, b : b + 1]
                for b in range(m * CHUNK // LANES, (m + 1) * CHUNK // LANES)
            ],
            axis=0,
        )
        total, scale = row_scale(summed, grad)
        fresh = src_ref[at, :] - grad * scale
        src_out_ref[at, :] = fresh
        for b in range(CHUNK // LANES):
            totals.append(total[b * LANES : (b + 1) * LANES])
        if not last:
            high, low = halves(fresh)
            stack_ref[at, :] = high
            stack_ref[rows + m * CHUNK : rows + (m + 1) * CHUNK, :] = low
    acc_out_ref[...] = jnp.transpose(jnp.concatenate(totals, axis=1))
    if not last:
        gather_rows(columns(esr_ref[step + 1]), stack_ref[...], next_ref, edges, rows)


def final_kernel(core_ref, mine_ref, peer_ref, rel_ref, acc_ref, rel_out_ref, acc_out_ref):
    rel, total = relation_update(core_ref, mine_ref, peer_ref, rel_ref, acc_ref)
    rel_out_ref[...] = rel
    acc_out_ref[...] = jnp.transpose(jnp.broadcast_to(total, (total.shape[0], LANES)))[0:1, :]


def call(body, outs, args, scratch=(), smem=0):
    in_specs = [
        pl.BlockSpec(memory_space=pltpu.SMEM if k < smem else pltpu.VMEM)
        for k in range(len(args))
    ]
    return pl.pallas_call(
        body,
        out_shape=tuple(jax.ShapeDtypeStruct(s, d) for s, d in outs),
        in_specs=in_specs,
        out_specs=tuple(pl.BlockSpec(memory_space=pltpu.VMEM) for _ in outs),
        scratch_shapes=list(scratch),
        compiler_params=pltpu.CompilerParams(vmem_limit_bytes=40 << 20),
    )(*args)


def shifted(value, axis, steps):
    count = lax.axis_size(axis)
    return lax.ppermute(value, axis, [(k, (k + steps) % count) for k in range(count)])


def crossed(value, axis, bits):
    count = lax.axis_size(axis)
    return lax.ppermute(value, axis, [(k, k ^ bits) for k in range(count)])


def exchanged(value, axis, low):
    count = lax.axis_size(axis)
    while low < count:
        reach = min(4, count // low)
        value = sum([crossed(value, axis, low * k) for k in range(1, reach)], value)
        low *= reach
    return value


def reduced(keep, send):
    half = keep + crossed(send, "dst", 1)
    half = exchanged(half, "src", 1)
    half = exchanged(half, "dst", 2)
    return half, crossed(half, "dst", 1)


def local(
    src_emb, src_acc, dst_emb, dst_acc, rel_emb, rel_acc, edge_src, edge_dst, edge_rel, negatives
):
    esr, eds, erl, neg = (v[0, 0] for v in (edge_src, edge_dst, edge_rel, negatives))
    steps, eblocks, _ = esr.shape
    edges = eblocks * LANES
    srows, width = src_emb.shape
    drows = dst_emb.shape[0]
    nrel = rel_emb.shape[0]
    core = (lax.axis_index("dst") & 1).astype(jnp.int32).reshape(1)
    src, sacc = src_emb, src_acc.reshape(srows // LANES, LANES)
    dblocks = drows // LANES
    tail = jnp.pad(dst_acc.reshape(dblocks, LANES), ((0, 8 - dblocks), (0, width - LANES)))
    dst = jnp.concatenate([dst_emb, tail], axis=0)
    rel, racc = rel_emb, rel_acc.reshape(nrel, 1)
    stack = pltpu.VMEM((2 * srows, width), BF16)
    (rows,) = call(first_kernel, [((edges, width), F32)], [esr, src], [stack])
    (counts,) = call(count_kernel, [((steps, eblocks, drows), F32)], [neg])
    half = peer = None
    for step in range(steps):
        outs = [
            ((nrel // 2, width), F32),
            ((nrel // 2, width), F32),
            ((2, edges, drows), BF16),
            ((2, edges, width), BF16),
            ((2, edges, width), BF16),
        ]
        if step == 0:
            args = [core, rel, rows, dst, eds, erl, counts]
        else:
            args = [core, half, peer, racc, rel, rows, dst, eds, erl, counts]
            outs += [((nrel, width), F32), ((nrel, 1), F32)]
        res = call(functools.partial(query_kernel, step, step > 0), outs, args, smem=1)
        keep, send, wgt, qry, gsr = res[:5]
        if step > 0:
            rel, racc = res[5:]
        (dst,) = call(dst_kernel, [((drows + 8, width), F32)], [wgt, qry, dst])
        last = step == steps - 1
        dst = shifted(dst, "dst", 1 if not last else -(steps - 1))
        outs = [((srows, width), F32), ((srows // LANES, LANES), F32)]
        if not last:
            outs.append(((edges, width), F32))
        res = call(
            functools.partial(src_kernel, step, last),
            outs,
            [esr, gsr, src, sacc],
            [] if last else [stack],
        )
        src, sacc = res[:2]
        if not last:
            rows = res[2]
        half, peer = reduced(keep, send)
    rel, racc = call(
        final_kernel,
        [((nrel, width), F32), ((1, LANES), F32)],
        [core, half, peer, rel, racc],
        smem=1,
    )
    return (
        src,
        sacc.reshape(-1),
        dst[:drows],
        dst[drows : drows + dblocks, :LANES].reshape(-1),
        rel,
        racc.reshape(-1),
    )


def solution(mesh):
    both = P(("src", "dst"))
    wide = P(("src", "dst"), None)
    edge = P("src", "dst", None, None, None)
    return jax.shard_map(
        local,
        mesh=mesh,
        in_specs=(wide, both, wide, both, P(), P(), edge, edge, edge, edge),
        out_specs=(wide, both, wide, both, P(), P()),
        check_vma=False,
    )
```

time: 629 us -> 137 us (0.22); the launches traced: 621 us -> 137 us
  waiting for transfers between devices: 387 us -> 58.4 us
  other arithmetic: 109 us -> 1.29 us
  local copies, waits for them, and re-layouts: 58.8 us -> 4.25 us
  Pallas kernels: 0 us -> 37.6 us
  matrix products: 35.4 us -> 0 us
  starting transfers between devices: 15.5 us -> 34.5 us
  between operations: 14.9 us -> 0.94 us
    psum x4 -> x0, waiting for transfers between devices: 382 us -> none  [train_bucket(): rel_grad = lax.psum(rel_part, ('src', 'dst'))]
    scatter-add x12 -> x0, other arithmetic: 81.2 us -> none  [the longest x4 27.5 us: bucket_grads(): dst_grad = dst_grad.at[neg_ids.reshape(-1)].add(grad_neg.reshape(-1, width))]
    ppermute x14 -> x36, waiting for transfers between devices: 5.37 us -> 58.4 us  [the longest x32 58.4 us: crossed(): return lax.ppermute(value, axis, [(k, k ^ bits) for k in range(count)])]
    gather x12 -> x0, local copies, waits for them, and re-layouts: 52.3 us -> none  [the longest x4 18.7 us: bucket_grads(): src_rows = src_block[src_ids]]
    pallas_call x0 -> x15, Pallas kernels: none -> 37.6 us  [call(): pl.pallas_call(body, out_shape=tuple((jax.ShapeDtypeStruct(s, d) for s, d...]
    dot_general x20 -> x0, matrix products: 35.4 us -> none  [the longest x4 8.94 us: bucket_grads(): jnp.einsum('cbk,ckd->cbd', neg_weight, neg_rows, precision=highest)]
    ppermute x14 -> x36, starting transfers between devices: 15.3 us -> 34.5 us  [the longest x32 30.8 us: crossed(): return lax.ppermute(value, axis, [(k, k ^ bits) for k in range(count)])]
    sub x10 -> x0, other arithmetic: 8.27 us -> none  [adagrad_rows(): embedding - 0.3 * grad / (jnp.sqrt(new_sum)[..., None] + 1e-10)]
  transfers between devices with their start and end apart: 18 -> 36, of which waited for: 6 -> 17; matrix products, arithmetic and copies ran while one was open for 32% -> 0% of each run, Pallas kernels for 0% -> 13%
where the time goes in v1:
time: 137 us
  waiting for transfers between devices  58.4 us (43%)
  Pallas kernels  37.6 us (27%)
  starting transfers between devices  34.5 us (25%)
  local copies, waits for them, and re-layouts  4.25 us (3%)
    ppermute x32, waiting for transfers between devices, crossed(): return lax.ppermute(value, axis, [(k, k ^ bits) for k in range(count)])  58.4 us
    pallas_call x15, Pallas kernels, call(): pl.pallas_call(body, out_shape=tuple((jax.ShapeDtypeStruct(s, d) for s, d...  37.6 us
    ppermute x32, starting transfers between devices, crossed(): return lax.ppermute(value, axis, [(k, k ^ bits) for k in range(count)])  30.8 us
    ppermute x4, starting transfers between devices, shifted(): lax.ppermute(value, axis, [(k, (k + steps) % count) for k in range(count)])  3.65 us
  transfers between devices with their start and end apart: 36, of which 17 were waited for; matrix products, arithmetic and copies ran while one was open for 0% of the time, Pallas kernels for 13%

profile of v1, /device:TPU:1, one launch (start us, length us, event | category | flops | bytes accessed | tf_op | source)
XLA Modules:
  0.0 137.0 jit_solution(7387921794177024486)
XLA Ops:
  7.3 3.8 %shard_map.147 = (f32[64,256]{1,0:T(8,128)S(1)}, f32[64,256]{1,0:T(8,128)S(1)}, bf16[2,1024,512]{2,1,0:T(8,128)(2,1)S(1)}, bf16[2,1024,256]{2,1,0:T(8,128)(2,1)S(1)}, bf16[2,1024,256]{2,1,0:T(8,128)(2,1)S(1)}) custom-call(s32[1]{0:T(128)} %bitcast.1.refs_0_.core_ref, f32[128,256]{1,0:T(8,128)S(1)} %copy-done.2, f32[1024,256]{1,0:T(8,128)S(1)} %shard_map.145.refs_2_, ...), custom_call_target="tpu_custom_call" | custom-call | tf_op jit(solution)/shard_map/pallas_call | solution.py:235
  12.4 3.4 %collective-permute-start.3 = (f32[64,256]{1,0:T(8,128)S(1)}, f32[64,256]{1,0:T(8,128)S(1)}, u32[]{:S(2)}, u32[]{:S(2)}) collective-permute-start(f32[64,256]{1,0:T(8,128)S(1)} %add.86), channel_id=1, source_target_pairs={{0,24},{8,16},{16,8},{24,0},{1,25},{9,17},{17,9},{25,1},{2,26},{10... | collective-permute-start | bytes 196616 | tf_op jit(solution)/shard_map/ppermute | solution.py:252
  17.8 2.7 %collective-permute-start.8 = (f32[520,256]{1,0:T(8,128)S(1)}, f32[520,256]{1,0:T(8,128)S(1)}, u32[]{:S(2)}, u32[]{:S(2)}) collective-permute-start(f32[520,256]{1,0:T(8,128)S(1)} %shard_map.149), channel_id=1, source_target_pairs={{0,1},{1,2},{2,3},{3,4},{4,5},{5,6},{6,7},{7,0},{8,9},{9,10},{10,1... | collective-permute-start | bytes 1597448 | tf_op jit(solution)/shard_map/ppermute | solution.py:247
  20.5 2.1 %collective-permute-start.6 = (f32[64,256]{1,0:T(8,128)S(1)}, f32[64,256]{1,0:T(8,128)S(1)}, u32[]{:S(2)}, u32[]{:S(2)}) collective-permute-start(f32[64,256]{1,0:T(8,128)S(1)} %add_add_fusion.7), channel_id=1, source_target_pairs={{0,6},{1,7},{2,4},{3,5},{4,2},{5,3},{6,0},{7,1},{8,14},{9,15},{10,... | collective-permute-start | bytes 196616 | tf_op jit(solution)/shard_map/ppermute | solution.py:252
  24.1 7.4 %collective-permute-done.6 = f32[64,256]{1,0:T(8,128)S(1)} collective-permute-done((f32[64,256]{1,0:T(8,128)S(1)}, f32[64,256]{1,0:T(8,128)S(1)}, u32[]{:S(2)}, u32[]{:S(2)}) %collective-permute-start.6) | collective-permute-done | bytes 65568 | tf_op jit(solution)/shard_map/ppermute | solution.py:252
  31.6 2.9 %collective-permute-done.5 = f32[64,256]{1,0:T(8,128)S(1)} collective-permute-done((f32[64,256]{1,0:T(8,128)S(1)}, f32[64,256]{1,0:T(8,128)S(1)}, u32[]{:S(2)}, u32[]{:S(2)}) %collective-permute-start.5) | collective-permute-done | bytes 65568 | tf_op jit(solution)/shard_map/ppermute | solution.py:252
  35.2 2.8 %shard_map.148 = (f32[1024,256]{1,0:T(8,128)S(1)}, f32[8,128]{1,0:T(8,128)S(1)}, f32[1024,256]{1,0:T(8,128)S(1)}) custom-call(s32[4,8,128]{2,1,0:T(8,128)S(1)} %bitcast.13, bf16[2,1024,256]{2,1,0:T(8,128)(2,1)S(1)} %get-tuple-element.47.gsr_ref, f32[1024,256]{1,0:T(8,128)S(1)} %copy-done.1, f32[8,128]{1,0:T(8,128)S(1)} %bitcast.26), custom_call_target="tpu_custom_call" | custom-call | tf_op jit(solution)/shard_map/pallas_call | solution.py:235
  38.1 4.8 %shard_map.150 = (f32[64,256]{1,0:T(8,128)S(1)}, f32[64,256]{1,0:T(8,128)S(1)}, bf16[2,1024,512]{2,1,0:T(8,128)(2,1)S(1)}, bf16[2,1024,256]{2,1,0:T(8,128)(2,1)S...) custom-call(s32[1]{0:T(128)} %bitcast.1.refs_0_.core_ref, ...), custom_call_target="tpu_custom_call" | custom-call | tf_op jit(solution)/shard_map/pallas_call | solution.py:235
  44.2 2.6 %collective-permute-start.12 = (f32[64,256]{1,0:T(8,128)S(1)}, f32[64,256]{1,0:T(8,128)S(1)}, u32[]{:S(2)}, u32[]{:S(2)}) collective-permute-start(f32[64,256]{1,0:T(8,128)S(1)} %add.93), channel_id=1, source_target_pairs={{0,24},{8,16},{16,8},{24,0},{1,25},{9,17},{17,9},{25,1},{2,26},{10... | collective-permute-start | bytes 196616 | tf_op jit(solution)/shard_map/ppermute | solution.py:252
  50.5 2.5 %collective-permute-start.15 = (f32[64,256]{1,0:T(8,128)S(1)}, f32[64,256]{1,0:T(8,128)S(1)}, u32[]{:S(2)}, u32[]{:S(2)}) collective-permute-start(f32[64,256]{1,0:T(8,128)S(1)} %add_add_fusion.5), channel_id=1, source_target_pairs={{0,6},{1,7},{2,4},{3,5},{4,2},{5,3},{6,0},{7,1},{8,14},{9,15},{10,... | collective-permute-start | bytes 196616 | tf_op jit(solution)/shard_map/ppermute | solution.py:252
  54.1 8.4 %collective-permute-done.15 = f32[64,256]{1,0:T(8,128)S(1)} collective-permute-done((f32[64,256]{1,0:T(8,128)S(1)}, f32[64,256]{1,0:T(8,128)S(1)}, u32[]{:S(2)}, u32[]{:S(2)}) %collective-permute-start.15) | collective-permute-done | bytes 65568 | tf_op jit(solution)/shard_map/ppermute | solution.py:252
  65.1 2.8 %shard_map.151 = (f32[1024,256]{1,0:T(8,128)S(1)}, f32[8,128]{1,0:T(8,128)S(1)}, f32[1024,256]{1,0:T(8,128)S(1)}) custom-call(s32[4,8,128]{2,1,0:T(8,128)S(1)} %bitcast.14, bf16[2,1024,256]{2,1,0:T(8,128)(2,1)S(1)} %get-tuple-element.55.gsr_ref, f32[1024,256]{1,0:T(8,128)S(1)} %get-tuple-element.56.src_ref, f32[8,128]{1,0:T(8,128)S(1)} %get-tuple-element.57.acc_ref), custom_call_target="tpu_custom_call" | custom-call | tf_op jit(solution)/shard_map/pallas_call | solution.py:235
  68.0 3.9 %shard_map.153 = (f32[64,256]{1,0:T(8,128)S(1)}, f32[64,256]{1,0:T(8,128)S(1)}, bf16[2,1024,512]{2,1,0:T(8,128)(2,1)S(1)}, bf16[2,1024,256]{2,1,0:T(8,128)(2,1)S...) custom-call(s32[1]{0:T(128)} %bitcast.1.refs_0_.core_ref, ...), custom_call_target="tpu_custom_call" | custom-call | tf_op jit(solution)/shard_map/pallas_call | solution.py:235
  73.2 2.1 %collective-permute-start.21 = (f32[64,256]{1,0:T(8,128)S(1)}, f32[64,256]{1,0:T(8,128)S(1)}, u32[]{:S(2)}, u32[]{:S(2)}) collective-permute-start(f32[64,256]{1,0:T(8,128)S(1)} %add.100), channel_id=1, source_target_pairs={{0,24},{8,16},{16,8},{24,0},{1,25},{9,17},{17,9},{25,1},{2,26},{10... | collective-permute-start | bytes 196616 | tf_op jit(solution)/shard_map/ppermute | solution.py:252
  79.2 2.9 %collective-permute-start.24 = (f32[64,256]{1,0:T(8,128)S(1)}, f32[64,256]{1,0:T(8,128)S(1)}, u32[]{:S(2)}, u32[]{:S(2)}) collective-permute-start(f32[64,256]{1,0:T(8,128)S(1)} %add_add_fusion.3), channel_id=1, source_target_pairs={{0,6},{1,7},{2,4},{3,5},{4,2},{5,3},{6,0},{7,1},{8,14},{9,15},{10,... | collective-permute-start | bytes 196616 | tf_op jit(solution)/shard_map/ppermute | solution.py:252
  82.8 8.8 %collective-permute-done.24 = f32[64,256]{1,0:T(8,128)S(1)} collective-permute-done((f32[64,256]{1,0:T(8,128)S(1)}, f32[64,256]{1,0:T(8,128)S(1)}, u32[]{:S(2)}, u32[]{:S(2)}) %collective-permute-start.24) | collective-permute-done | bytes 65568 | tf_op jit(solution)/shard_map/ppermute | solution.py:252
  93.9 2.8 %shard_map.154 = (f32[1024,256]{1,0:T(8,128)S(1)}, f32[8,128]{1,0:T(8,128)S(1)}, f32[1024,256]{1,0:T(8,128)S(1)}) custom-call(s32[4,8,128]{2,1,0:T(8,128)S(1)} %bitcast.15, bf16[2,1024,256]{2,1,0:T(8,128)(2,1)S(1)} %get-tuple-element.65.gsr_ref, f32[1024,256]{1,0:T(8,128)S(1)} %get-tuple-element.66.src_ref, f32[8,128]{1,0:T(8,128)S(1)} %get-tuple-element.67.acc_ref), custom_call_target="tpu_custom_call" | custom-call | tf_op jit(solution)/shard_map/pallas_call | solution.py:235
  96.8 3.9 %shard_map.156 = (f32[64,256]{1,0:T(8,128)S(1)}, f32[64,256]{1,0:T(8,128)S(1)}, bf16[2,1024,512]{2,1,0:T(8,128)(2,1)S(1)}, bf16[2,1024,256]{2,1,0:T(8,128)(2,1)S...) custom-call(s32[1]{0:T(128)} %bitcast.1.refs_0_.core_ref, ...), custom_call_target="tpu_custom_call" | custom-call | tf_op jit(solution)/shard_map/pallas_call | solution.py:235
  106.6 1.7 %collective-permute-done.30 = f32[64,256]{1,0:T(8,128)S(1)} collective-permute-done((f32[64,256]{1,0:T(8,128)S(1)}, f32[64,256]{1,0:T(8,128)S(1)}, u32[]{:S(2)}, u32[]{:S(2)}) %collective-permute-start.30) | collective-permute-done | bytes 65568 | tf_op jit(solution)/shard_map/ppermute | solution.py:252
  110.0 2.0 %collective-permute-start.32 = (f32[64,256]{1,0:T(8,128)S(1)}, f32[64,256]{1,0:T(8,128)S(1)}, u32[]{:S(2)}, u32[]{:S(2)}) collective-permute-start(f32[64,256]{1,0:T(8,128)S(1)} %add_add_fusion.1), channel_id=1, source_target_pairs={{0,2},{1,3},{2,0},{3,1},{4,6},{5,7},{6,4},{7,5},{8,10},{9,11},{10,... | collective-permute-start | bytes 196616 | tf_op jit(solution)/shard_map/ppermute | solution.py:252
  112.0 9.9 %collective-permute-done.34 = f32[64,256]{1,0:T(8,128)S(1)} collective-permute-done((f32[64,256]{1,0:T(8,128)S(1)}, f32[64,256]{1,0:T(8,128)S(1)}, u32[]{:S(2)}, u32[]{:S(2)}) %collective-permute-start.34) | collective-permute-done | bytes 65568 | tf_op jit(solution)/shard_map/ppermute | solution.py:252
  122.0 8.2 %collective-permute-done.33 = f32[64,256]{1,0:T(8,128)S(1)} collective-permute-done((f32[64,256]{1,0:T(8,128)S(1)}, f32[64,256]{1,0:T(8,128)S(1)}, u32[]{:S(2)}, u32[]{:S(2)}) %collective-permute-start.33) | collective-permute-done | bytes 65568 | tf_op jit(solution)/shard_map/ppermute | solution.py:252
  130.2 1.8 %collective-permute-start.35 = (f32[64,256]{1,0:T(8,128)S(1)}, f32[64,256]{1,0:T(8,128)S(1)}, u32[]{:S(2)}, u32[]{:S(2)}) collective-permute-start(f32[64,256]{1,0:T(8,128)S(1)} %add_add_fusion.mine_ref), channel_id=1, source_target_pairs={{0,1},{1,0},{2,3},{3,2},{4,5},{5,4},{6,7},{7,6},{8,9},{9,8},{10,11... | collective-permute-start | bytes 196616 | tf_op jit(solution)/shard_map/ppermute | solution.py:252
  132.0 2.7 %shard_map.157 = (f32[1024,256]{1,0:T(8,128)}, f32[8,128]{1,0:T(8,128)}) custom-call(s32[4,8,128]{2,1,0:T(8,128)S(1)} %bitcast.16, bf16[2,1024,256]{2,1,0:T(8,128)(2,1)S(1)} %get-tuple-element.71.gsr_ref, f32[1024,256]{1,0:T(8,128)S(1)} %get-tuple-element.72.src_ref, f32[8,128]{1,0:T(8,128)S(1)} %get-tuple-element.73.acc_ref), custom_call_target="tpu_custom_call" | custom-call | tf_op jit(solution)/shard_map/pallas_call | solution.py:235
  (99 shorter events, 38.9 us)
Async XLA Ops:
  12.4 8.0 %collective-permute-start.3 = (f32[64,256]{1,0:T(8,128)S(1)}, f32[64,256]{1,0:T(8,128)S(1)}, u32[]{:S(2)}, u32[]{:S(2)}) collective-permute-start(f32[64,256]{1,0:T(8,128)S(1)} %add.86), channel_id=1, source_target_pairs={{0,24},{8,16},{16,8},{24,0},{1,25},{9,17},{17,9},{25,1},{2,26},{10... | collective-permute-start | bytes 196616 | tf_op jit(solution)/shard_map/ppermute | solution.py:252
  15.8 4.7 %collective-permute-start.2 = (f32[64,256]{1,0:T(8,128)S(1)}, f32[64,256]{1,0:T(8,128)S(1)}, u32[]{:S(2)}, u32[]{:S(2)}) collective-permute-start(f32[64,256]{1,0:T(8,128)S(1)} %add.86), channel_id=1, source_target_pairs={{0,16},{8,24},{16,0},{24,8},{1,17},{9,25},{17,1},{25,9},{2,18},{10... | collective-permute-start | bytes 196616 | tf_op jit(solution)/shard_map/ppermute | solution.py:252
  16.0 4.4 %collective-permute-start.1 = (f32[64,256]{1,0:T(8,128)S(1)}, f32[64,256]{1,0:T(8,128)S(1)}, u32[]{:S(2)}, u32[]{:S(2)}) collective-permute-start(f32[64,256]{1,0:T(8,128)S(1)} %add.86), channel_id=1, source_target_pairs={{0,8},{8,0},{16,24},{24,16},{1,9},{9,1},{17,25},{25,17},{2,10},{10... | collective-permute-start | bytes 196616 | tf_op jit(solution)/shard_map/ppermute | solution.py:252
  17.8 20.3 %collective-permute-start.8 = (f32[520,256]{1,0:T(8,128)S(1)}, f32[520,256]{1,0:T(8,128)S(1)}, u32[]{:S(2)}, u32[]{:S(2)}) collective-permute-start(f32[520,256]{1,0:T(8,128)S(1)} %shard_map.149), channel_id=1, source_target_pairs={{0,1},{1,2},{2,3},{3,4},{4,5},{5,6},{6,7},{7,0},{8,9},{9,10},{10,1... | collective-permute-start | bytes 1597448 | tf_op jit(solution)/shard_map/ppermute | solution.py:247
  20.5 11.1 %collective-permute-start.6 = (f32[64,256]{1,0:T(8,128)S(1)}, f32[64,256]{1,0:T(8,128)S(1)}, u32[]{:S(2)}, u32[]{:S(2)}) collective-permute-start(f32[64,256]{1,0:T(8,128)S(1)} %add_add_fusion.7), channel_id=1, source_target_pairs={{0,6},{1,7},{2,4},{3,5},{4,2},{5,3},{6,0},{7,1},{8,14},{9,15},{10,... | collective-permute-start | bytes 196616 | tf_op jit(solution)/shard_map/ppermute | solution.py:252
  22.6 11.9 %collective-permute-start.5 = (f32[64,256]{1,0:T(8,128)S(1)}, f32[64,256]{1,0:T(8,128)S(1)}, u32[]{:S(2)}, u32[]{:S(2)}) collective-permute-start(f32[64,256]{1,0:T(8,128)S(1)} %add_add_fusion.7), channel_id=1, source_target_pairs={{0,4},{1,5},{2,6},{3,7},{4,0},{5,1},{6,2},{7,3},{8,12},{9,13},{10,... | collective-permute-start | bytes 196616 | tf_op jit(solution)/shard_map/ppermute | solution.py:252
  23.1 11.5 %collective-permute-start.4 = (f32[64,256]{1,0:T(8,128)S(1)}, f32[64,256]{1,0:T(8,128)S(1)}, u32[]{:S(2)}, u32[]{:S(2)}) collective-permute-start(f32[64,256]{1,0:T(8,128)S(1)} %add_add_fusion.7), channel_id=1, source_target_pairs={{0,2},{1,3},{2,0},{3,1},{4,6},{5,7},{6,4},{7,5},{8,10},{9,11},{10,... | collective-permute-start | bytes 196616 | tf_op jit(solution)/shard_map/ppermute | solution.py:252
  44.2 4.9 %collective-permute-start.12 = (f32[64,256]{1,0:T(8,128)S(1)}, f32[64,256]{1,0:T(8,128)S(1)}, u32[]{:S(2)}, u32[]{:S(2)}) collective-permute-start(f32[64,256]{1,0:T(8,128)S(1)} %add.93), channel_id=1, source_target_pairs={{0,24},{8,16},{16,8},{24,0},{1,25},{9,17},{17,9},{25,1},{2,26},{10... | collective-permute-start | bytes 196616 | tf_op jit(solution)/shard_map/ppermute | solution.py:252
  48.8 19.2 %collective-permute-start.17 = (f32[520,256]{1,0:T(8,128)S(1)}, f32[520,256]{1,0:T(8,128)S(1)}, u32[]{:S(2)}, u32[]{:S(2)}) collective-permute-start(f32[520,256]{1,0:T(8,128)S(1)} %shard_map.152), channel_id=1, source_target_pairs={{0,1},{1,2},{2,3},{3,4},{4,5},{5,6},{6,7},{7,0},{8,9},{9,10},{10,1... | collective-permute-start | bytes 1597448 | tf_op jit(solution)/shard_map/ppermute | solution.py:247
  50.5 12.0 %collective-permute-start.15 = (f32[64,256]{1,0:T(8,128)S(1)}, f32[64,256]{1,0:T(8,128)S(1)}, u32[]{:S(2)}, u32[]{:S(2)}) collective-permute-start(f32[64,256]{1,0:T(8,128)S(1)} %add_add_fusion.5), channel_id=1, source_target_pairs={{0,6},{1,7},{2,4},{3,5},{4,2},{5,3},{6,0},{7,1},{8,14},{9,15},{10,... | collective-permute-start | bytes 196616 | tf_op jit(solution)/shard_map/ppermute | solution.py:252
  53.0 11.2 %collective-permute-start.14 = (f32[64,256]{1,0:T(8,128)S(1)}, f32[64,256]{1,0:T(8,128)S(1)}, u32[]{:S(2)}, u32[]{:S(2)}) collective-permute-start(f32[64,256]{1,0:T(8,128)S(1)} %add_add_fusion.5), channel_id=1, source_target_pairs={{0,4},{1,5},{2,6},{3,7},{4,0},{5,1},{6,2},{7,3},{8,12},{9,13},{10,... | collective-permute-start | bytes 196616 | tf_op jit(solution)/shard_map/ppermute | solution.py:252
  53.0 11.2 %collective-permute-start.13 = (f32[64,256]{1,0:T(8,128)S(1)}, f32[64,256]{1,0:T(8,128)S(1)}, u32[]{:S(2)}, u32[]{:S(2)}) collective-permute-start(f32[64,256]{1,0:T(8,128)S(1)} %add_add_fusion.5), channel_id=1, source_target_pairs={{0,2},{1,3},{2,0},{3,1},{4,6},{5,7},{6,4},{7,5},{8,10},{9,11},{10,... | collective-permute-start | bytes 196616 | tf_op jit(solution)/shard_map/ppermute | solution.py:252
  73.2 4.8 %collective-permute-start.21 = (f32[64,256]{1,0:T(8,128)S(1)}, f32[64,256]{1,0:T(8,128)S(1)}, u32[]{:S(2)}, u32[]{:S(2)}) collective-permute-start(f32[64,256]{1,0:T(8,128)S(1)} %add.100), channel_id=1, source_target_pairs={{0,24},{8,16},{16,8},{24,0},{1,25},{9,17},{17,9},{25,1},{2,26},{10... | collective-permute-start | bytes 196616 | tf_op jit(solution)/shard_map/ppermute | solution.py:252
  77.5 19.3 %collective-permute-start.26 = (f32[520,256]{1,0:T(8,128)S(1)}, f32[520,256]{1,0:T(8,128)S(1)}, u32[]{:S(2)}, u32[]{:S(2)}) collective-permute-start(f32[520,256]{1,0:T(8,128)S(1)} %shard_map.155), channel_id=1, source_target_pairs={{0,1},{1,2},{2,3},{3,4},{4,5},{5,6},{6,7},{7,0},{8,9},{9,10},{10,1... | collective-permute-start | bytes 1597448 | tf_op jit(solution)/shard_map/ppermute | solution.py:247
  79.2 12.4 %collective-permute-start.24 = (f32[64,256]{1,0:T(8,128)S(1)}, f32[64,256]{1,0:T(8,128)S(1)}, u32[]{:S(2)}, u32[]{:S(2)}) collective-permute-start(f32[64,256]{1,0:T(8,128)S(1)} %add_add_fusion.3), channel_id=1, source_target_pairs={{0,6},{1,7},{2,4},{3,5},{4,2},{5,3},{6,0},{7,1},{8,14},{9,15},{10,... | collective-permute-start | bytes 196616 | tf_op jit(solution)/shard_map/ppermute | solution.py:252
  82.1 11.2 %collective-permute-start.23 = (f32[64,256]{1,0:T(8,128)S(1)}, f32[64,256]{1,0:T(8,128)S(1)}, u32[]{:S(2)}, u32[]{:S(2)}) collective-permute-start(f32[64,256]{1,0:T(8,128)S(1)} %add_add_fusion.3), channel_id=1, source_target_pairs={{0,4},{1,5},{2,6},{3,7},{4,0},{5,1},{6,2},{7,3},{8,12},{9,13},{10,... | collective-permute-start | bytes 196616 | tf_op jit(solution)/shard_map/ppermute | solution.py:252
  82.1 11.2 %collective-permute-start.22 = (f32[64,256]{1,0:T(8,128)S(1)}, f32[64,256]{1,0:T(8,128)S(1)}, u32[]{:S(2)}, u32[]{:S(2)}) collective-permute-start(f32[64,256]{1,0:T(8,128)S(1)} %add_add_fusion.3), channel_id=1, source_target_pairs={{0,2},{1,3},{2,0},{3,1},{4,6},{5,7},{6,4},{7,5},{8,10},{9,11},{10,... | collective-permute-start | bytes 196616 | tf_op jit(solution)/shard_map/ppermute | solution.py:252
  102.1 4.5 %collective-permute-start.31 = (f32[64,256]{1,0:T(8,128)S(1)}, f32[64,256]{1,0:T(8,128)S(1)}, u32[]{:S(2)}, u32[]{:S(2)}) collective-permute-start(f32[64,256]{1,0:T(8,128)S(1)} %add.107), channel_id=1, source_target_pairs={{0,24},{8,16},{16,8},{24,0},{1,25},{9,17},{17,9},{25,1},{2,26},{10... | collective-permute-start | bytes 196616 | tf_op jit(solution)/shard_map/ppermute | solution.py:252
  103.8 4.6 %collective-permute-start.30 = (f32[64,256]{1,0:T(8,128)S(1)}, f32[64,256]{1,0:T(8,128)S(1)}, u32[]{:S(2)}, u32[]{:S(2)}) collective-permute-start(f32[64,256]{1,0:T(8,128)S(1)} %add.107), channel_id=1, source_target_pairs={{0,16},{8,24},{16,0},{24,8},{1,17},{9,25},{17,1},{25,9},{2,18},{10... | collective-permute-start | bytes 196616 | tf_op jit(solution)/shard_map/ppermute | solution.py:252
  106.4 29.2 %collective-permute-start.27 = (f32[520,256]{1,0:T(8,128)S(1)}, f32[520,256]{1,0:T(8,128)S(1)}, u32[]{:S(2)}, u32[]{:S(2)}) collective-permute-start(f32[520,256]{1,0:T(8,128)S(1)} %shard_map.158), channel_id=1, source_target_pairs={{0,5},{1,6},{2,7},{3,0},{4,1},{5,2},{6,3},{7,4},{8,13},{9,14},{10,... | collective-permute-start | bytes 1597448 | tf_op jit(solution)/shard_map/ppermute | solution.py:247
  108.4 13.6 %collective-permute-start.34 = (f32[64,256]{1,0:T(8,128)S(1)}, f32[64,256]{1,0:T(8,128)S(1)}, u32[]{:S(2)}, u32[]{:S(2)}) collective-permute-start(f32[64,256]{1,0:T(8,128)S(1)} %add_add_fusion.1), channel_id=1, source_target_pairs={{0,6},{1,7},{2,4},{3,5},{4,2},{5,3},{6,0},{7,1},{8,14},{9,15},{10,... | collective-permute-start | bytes 196616 | tf_op jit(solution)/shard_map/ppermute | solution.py:252
  108.5 21.7 %collective-permute-start.33 = (f32[64,256]{1,0:T(8,128)S(1)}, f32[64,256]{1,0:T(8,128)S(1)}, u32[]{:S(2)}, u32[]{:S(2)}) collective-permute-start(f32[64,256]{1,0:T(8,128)S(1)} %add_add_fusion.1), channel_id=1, source_target_pairs={{0,4},{1,5},{2,6},{3,7},{4,0},{5,1},{6,2},{7,3},{8,12},{9,13},{10,... | collective-permute-start | bytes 196616 | tf_op jit(solution)/shard_map/ppermute | solution.py:252
  110.0 20.1 %collective-permute-start.32 = (f32[64,256]{1,0:T(8,128)S(1)}, f32[64,256]{1,0:T(8,128)S(1)}, u32[]{:S(2)}, u32[]{:S(2)}) collective-permute-start(f32[64,256]{1,0:T(8,128)S(1)} %add_add_fusion.1), channel_id=1, source_target_pairs={{0,2},{1,3},{2,0},{3,1},{4,6},{5,7},{6,4},{7,5},{8,10},{9,11},{10,... | collective-permute-start | bytes 196616 | tf_op jit(solution)/shard_map/ppermute | solution.py:252
  130.2 4.5 %collective-permute-start.35 = (f32[64,256]{1,0:T(8,128)S(1)}, f32[64,256]{1,0:T(8,128)S(1)}, u32[]{:S(2)}, u32[]{:S(2)}) collective-permute-start(f32[64,256]{1,0:T(8,128)S(1)} %add_add_fusion.mine_ref), channel_id=1, source_target_pairs={{0,1},{1,0},{2,3},{3,2},{4,5},{5,4},{6,7},{7,6},{8,9},{9,8},{10,11... | collective-permute-start | bytes 196616 | tf_op jit(solution)/shard_map/ppermute | solution.py:252
  (22 other events, 133.2 us)

commit v2 on v1

--- a/solution.py
+++ b/solution.py
@@ -61,25 +61,64 @@
         out_ref[c * CHUNK : (c + 1) * CHUNK, :] = dot(jnp.concatenate([hot, hot], axis=1), stack)
 
 
-def first_kernel(ids_ref, src_ref, out_ref, stack_ref):
+def write_counts(neg_ref, step, out_ref):
+    blocks, negs = neg_ref.shape[1:]
+    rows = out_ref.shape[1]
+    cols = columns(neg_ref[step])
+    lane = lax.broadcasted_iota(jnp.int32, (negs, rows), 1)
+    for b in range(blocks):
+        hits = jnp.where(cols[:, b : b + 1] == lane, 0.5 / negs, 0.0)
+        out_ref[b : b + 1, :] = jnp.sum(hits, axis=0, keepdims=True)
+
+
+def first_kernel(
+    esr_hbm, eds_hbm, erl_hbm, neg_hbm, sac_hbm, dac_hbm, rac_hbm, rel_hbm, src_hbm, dst_hbm,
+    esr_ref, eds_ref, erl_ref, neg_ref, sac_ref, rac_ref, rel_ref, src_ref, dst_ref,
+    next_ref, cnt_ref, stack_ref, src_sem, sem,
+):
     rows = src_ref.shape[0]
-    high, low = halves(src_ref[...])
-    stack_ref[0:rows, :] = high
-    stack_ref[rows : 2 * rows, :] = low
-    gather_rows(columns(ids_ref[0]), stack_ref[...], out_ref, out_ref.shape[0], rows)
-
-
-def count_kernel(neg_ref, out_ref):
-    steps, blocks, negs = neg_ref.shape
-    rows = out_ref.shape[2]
-    for t in range(steps):
-        cols = columns(neg_ref[t])
-        lane = lax.broadcasted_iota(jnp.int32, (negs, rows), 1)
-        parts = [
-            jnp.sum(jnp.where(cols[:, b : b + 1] == lane, 1.0 / negs, 0.0), axis=0, keepdims=True)
-            for b in range(blocks)
-        ]
-        out_ref[t] = jnp.concatenate(parts, axis=0)
+    drows, width = dst_hbm.shape
+    small = [
+        pltpu.make_async_copy(source, target, sem.at[k])
+        for k, (source, target) in enumerate(
+            [
+                (neg_hbm, neg_ref),
+                (esr_hbm, esr_ref),
+                (dac_hbm, dst_ref.at[pl.ds(drows, dac_hbm.shape[0]), pl.ds(0, LANES)]),
+                (dst_hbm, dst_ref.at[pl.ds(0, drows)]),
+                (eds_hbm, eds_ref),
+                (erl_hbm, erl_ref),
+                (sac_hbm, sac_ref),
+                (rac_hbm, rac_ref),
+                (rel_hbm, rel_ref),
+            ]
+        )
+    ]
+    for load in small[:2]:
+        load.start()
+    chunks = rows // CHUNK
+    loads = [
+        pltpu.make_async_copy(
+            src_hbm.at[pl.ds(m * CHUNK, CHUNK)], src_ref.at[pl.ds(m * CHUNK, CHUNK)], src_sem.at[m]
+        )
+        for m in range(chunks)
+    ]
+    for load in loads:
+        load.start()
+    dst_ref[drows : drows + 8, :] = jnp.zeros((8, width), F32)
+    for load in small[2:]:
+        load.start()
+    small[0].wait()
+    write_counts(neg_ref, 0, cnt_ref)
+    small[1].wait()
+    for m in range(chunks):
+        loads[m].wait()
+        high, low = halves(src_ref[m * CHUNK : (m + 1) * CHUNK, :])
+        stack_ref[m * CHUNK : (m + 1) * CHUNK, :] = high
+        stack_ref[rows + m * CHUNK : rows + (m + 1) * CHUNK, :] = low
+    gather_rows(columns(esr_ref[0]), stack_ref[...], next_ref, next_ref.shape[0], rows)
+    for load in small[2:]:
+        load.wait()
 
 
 def relation_update(core_ref, mine_ref, peer_ref, rel_ref, acc_ref):
@@ -88,8 +127,9 @@
     grad = jnp.concatenate(
         [jnp.where(first, mine, peer), jnp.where(first, peer, mine)], axis=0
     )
-    total, scale = row_scale(acc_ref[...], grad)
-    return rel_ref[...] - grad * scale, total
+    nrel = grad.shape[0]
+    total, scale = row_scale(columns(jnp.broadcast_to(acc_ref[...], (8, nrel)))[:, 0:1], grad)
+    return rel_ref[...] - grad * scale, columns(jnp.broadcast_to(total, (nrel, LANES)))[0:1, :]
 
 
 def query_kernel(step, updated, *refs):
@@ -111,17 +151,17 @@
     else:
         rel = rel_ref[...]
     edges = src_ref.shape[0]
-    rows = cnt_ref.shape[2]
+    rows = cnt_ref.shape[1]
     nrel = rel.shape[0]
     blocks = CHUNK // LANES
     rel_stack = jnp.concatenate(halves(rel), axis=0)
     dst_high, dst_low = halves(dst_ref[0:rows, :])
-    dst_wide = jnp.concatenate([dst_high, dst_low, dst_high], axis=1)
+    dst_wide = 0.5 * jnp.concatenate([dst_high, dst_low, dst_high], axis=1)
     dst_tall = jnp.concatenate([dst_high, dst_low, dst_high], axis=0)
     rel_cols = columns(erl_ref[step])
     dst_cols = columns(eds_ref[step])
     lane = lax.broadcasted_iota(jnp.int32, (LANES, rows), 1)
-    counts = cnt_ref[step]
+    counts = cnt_ref[...]
     grad = None
     for c in range(edges // CHUNK):
         at = slice(c * CHUNK, (c + 1) * CHUNK)
@@ -133,21 +173,20 @@
         qry_ref[0, at, :] = q_high
         qry_ref[1, at, :] = q_low
         scores = dot(jnp.concatenate([q_high, q_high, q_low], axis=1), dst_wide, 1, 1)
-        chance = 0.5 * jnp.tanh(0.5 * scores) + 0.5
+        slope = jnp.tanh(scores)
         parts = []
         for b in range(blocks):
             block = c * blocks + b
-            part = chance[b * LANES : (b + 1) * LANES, :]
-            hit = dst_cols[:, block : block + 1] == lane
-            parts.append(part * counts[block : block + 1, :] + jnp.where(hit, part - 1.0, 0.0))
+            part = slope[b * LANES : (b + 1) * LANES, :]
+            hit = jnp.where(dst_cols[:, block : block + 1] == lane, 0.5, 0.0)
+            count = counts[block : block + 1, :]
+            parts.append(part * (count + hit) + (count - hit))
         weight = jnp.concatenate(parts, axis=0)
         w_high, w_low = halves(weight)
         wgt_ref[0, at, :] = w_high
         wgt_ref[1, at, :] = w_low
         grad_query = dot(jnp.concatenate([w_high, w_high, w_low], axis=1), dst_tall)
-        g_high, g_low = halves(grad_query * rel_rows)
-        gsr_ref[0, at, :] = g_high
-        gsr_ref[1, at, :] = g_low
+        gsr_ref[at, :] = grad_query * rel_rows
         hot_t = hot_rows(erl_ref[step], c * blocks, blocks, 0, nrel)
         part = dot(
             jnp.concatenate([hot_t, hot_t], axis=1),
@@ -161,7 +200,7 @@
     send_ref[...] = jnp.where(first, bottom, top)
 
 
-def dst_kernel(wgt_ref, qry_ref, dst_ref, out_ref):
+def dst_kernel(wgt_ref, qry_ref, dst_ref, out_ref, *last):
     rows = wgt_ref.shape[2]
     width = dst_ref.shape[1]
     grad = (
@@ -181,19 +220,22 @@
         out_ref[at, :] = dst_ref[at, :] - grad[at] * scale
         totals.append(total)
     fresh = jnp.transpose(jnp.concatenate(totals + [totals[0]] * (8 - blocks), axis=1))
-    out_ref[rows : rows + 8, :] = jnp.concatenate(
-        [fresh, jnp.zeros((8, width - LANES), F32)], axis=1
-    )
-
-
-def src_kernel(step, last, esr_ref, gsr_ref, src_ref, acc_ref, *refs):
+    if last:
+        last[0][...] = fresh[0:blocks]
+    else:
+        out_ref[rows : rows + 8, :] = jnp.concatenate(
+            [fresh, jnp.zeros((8, width - LANES), F32)], axis=1
+        )
+
+
+def src_kernel(step, last, esr_ref, neg_ref, gsr_ref, src_ref, acc_ref, *refs):
     if last:
         src_out_ref, acc_out_ref = refs
     else:
-        src_out_ref, acc_out_ref, next_ref, stack_ref = refs
+        src_out_ref, acc_out_ref, next_ref, cnt_ref, stack_ref = refs
     rows = src_ref.shape[0]
-    edges = gsr_ref.shape[1]
-    gsr = jnp.concatenate([gsr_ref[0], gsr_ref[1]], axis=0)
+    edges = gsr_ref.shape[0]
+    gsr = jnp.concatenate(halves(gsr_ref[...]), axis=0)
     cols = columns(acc_ref[...])
     totals = []
     for m in range(rows // CHUNK):
@@ -219,19 +261,18 @@
     acc_out_ref[...] = jnp.transpose(jnp.concatenate(totals, axis=1))
     if not last:
         gather_rows(columns(esr_ref[step + 1]), stack_ref[...], next_ref, edges, rows)
+        write_counts(neg_ref, step + 1, cnt_ref)
 
 
 def final_kernel(core_ref, mine_ref, peer_ref, rel_ref, acc_ref, rel_out_ref, acc_out_ref):
     rel, total = relation_update(core_ref, mine_ref, peer_ref, rel_ref, acc_ref)
     rel_out_ref[...] = rel
-    acc_out_ref[...] = jnp.transpose(jnp.broadcast_to(total, (total.shape[0], LANES)))[0:1, :]
-
-
-def call(body, outs, args, scratch=(), smem=0):
-    in_specs = [
-        pl.BlockSpec(memory_space=pltpu.SMEM if k < smem else pltpu.VMEM)
-        for k in range(len(args))
-    ]
+    acc_out_ref[...] = total
+
+
+def call(body, outs, args, scratch=(), smem=0, hbm=0):
+    spaces = [pltpu.SMEM] * smem + [pltpu.VMEM] * (len(args) - smem - hbm) + [pltpu.HBM] * hbm
+    in_specs = [pl.BlockSpec(memory_space=space) for space in spaces]
     return pl.pallas_call(
         body,
         out_shape=tuple(jax.ShapeDtypeStruct(s, d) for s, d in outs),
@@ -239,7 +280,7 @@
         out_specs=tuple(pl.BlockSpec(memory_space=pltpu.VMEM) for _ in outs),
         scratch_shapes=list(scratch),
         compiler_params=pltpu.CompilerParams(vmem_limit_bytes=40 << 20),
-    )(*args)
+    )(*args[: len(args) - hbm], *[pltpu.with_memory_space_constraint(v, pltpu.HBM) for v in args[len(args) - hbm :]])
 
 
 def shifted(value, axis, steps):
@@ -259,13 +300,6 @@
         value = sum([crossed(value, axis, low * k) for k in range(1, reach)], value)
         low *= reach
     return value
-
-
-def reduced(keep, send):
-    half = keep + crossed(send, "dst", 1)
-    half = exchanged(half, "src", 1)
-    half = exchanged(half, "dst", 2)
-    return half, crossed(half, "dst", 1)
 
 
 def local(
@@ -278,59 +312,86 @@
     drows = dst_emb.shape[0]
     nrel = rel_emb.shape[0]
     core = (lax.axis_index("dst") & 1).astype(jnp.int32).reshape(1)
-    src, sacc = src_emb, src_acc.reshape(srows // LANES, LANES)
+    sacc = src_acc.reshape(srows // LANES, LANES)
     dblocks = drows // LANES
-    tail = jnp.pad(dst_acc.reshape(dblocks, LANES), ((0, 8 - dblocks), (0, width - LANES)))
-    dst = jnp.concatenate([dst_emb, tail], axis=0)
-    rel, racc = rel_emb, rel_acc.reshape(nrel, 1)
     stack = pltpu.VMEM((2 * srows, width), BF16)
-    (rows,) = call(first_kernel, [((edges, width), F32)], [esr, src], [stack])
-    (counts,) = call(count_kernel, [((steps, eblocks, drows), F32)], [neg])
+    ids = (esr.shape, jnp.int32)
+    firsts = [
+        esr, eds, erl, neg, sacc, dst_acc.reshape(dblocks, LANES), rel_acc.reshape(1, nrel),
+        rel_emb, src_emb, dst_emb,
+    ]
+    esr, eds, erl, neg, sacc, racc, rel, src, dst, rows, counts = call(
+        first_kernel,
+        [
+            ids, ids, ids, ids,
+            ((srows // LANES, LANES), F32),
+            ((1, nrel), F32),
+            ((nrel, width), F32),
+            ((srows, width), F32),
+            ((drows + 8, width), F32),
+            ((edges, width), F32),
+            ((eblocks, drows), F32),
+        ],
+        firsts,
+        [stack, pltpu.SemaphoreType.DMA((srows // CHUNK,)), pltpu.SemaphoreType.DMA((len(firsts) - 1,))],
+        hbm=len(firsts),
+    )
     half = peer = None
     for step in range(steps):
+        last = step == steps - 1
         outs = [
             ((nrel // 2, width), F32),
             ((nrel // 2, width), F32),
             ((2, edges, drows), BF16),
             ((2, edges, width), BF16),
-            ((2, edges, width), BF16),
+            ((edges, width), F32),
         ]
         if step == 0:
             args = [core, rel, rows, dst, eds, erl, counts]
         else:
             args = [core, half, peer, racc, rel, rows, dst, eds, erl, counts]
-            outs += [((nrel, width), F32), ((nrel, 1), F32)]
+            outs += [((nrel, width), F32), ((1, nrel), F32)]
         res = call(functools.partial(query_kernel, step, step > 0), outs, args, smem=1)
         keep, send, wgt, qry, gsr = res[:5]
         if step > 0:
             rel, racc = res[5:]
-        (dst,) = call(dst_kernel, [((drows + 8, width), F32)], [wgt, qry, dst])
-        last = step == steps - 1
-        dst = shifted(dst, "dst", 1 if not last else -(steps - 1))
+        half = crossed(send, "dst", 1)
+        outs = [((drows, width), F32), ((dblocks, LANES), F32)] if last else [((drows + 8, width), F32)]
+        res = call(dst_kernel, outs, [wgt, qry, dst])
+        half, *res = lax.optimization_barrier((keep + half, *res))
+        moved = [shifted(v, "dst", 1 if not last else -(steps - 1)) for v in res]
+        half = exchanged(half, "src", 1)
+        if last:
+            half, gsr = lax.optimization_barrier((half, gsr))
+        else:
+            half, gsr, moved = lax.optimization_barrier((half, gsr, moved))
         outs = [((srows, width), F32), ((srows // LANES, LANES), F32)]
         if not last:
-            outs.append(((edges, width), F32))
+            outs += [((edges, width), F32), ((eblocks, drows), F32)]
         res = call(
             functools.partial(src_kernel, step, last),
             outs,
-            [esr, gsr, src, sacc],
+            [esr, neg, gsr, src, sacc],
             [] if last else [stack],
         )
+        half = exchanged(half, "dst", 2)
+        half, *res = lax.optimization_barrier((half, *res))
+        peer = crossed(half, "dst", 1)
         src, sacc = res[:2]
         if not last:
-            rows = res[2]
-        half, peer = reduced(keep, send)
+            rows, counts = res[2:]
+            (dst,) = moved
     rel, racc = call(
         final_kernel,
-        [((nrel, width), F32), ((1, LANES), F32)],
+        [((nrel, width), F32), ((1, nrel), F32)],
         [core, half, peer, rel, racc],
         smem=1,
     )
     return (
         src,
         sacc.reshape(-1),
-        dst[:drows],
-        dst[drows : drows + dblocks, :LANES].reshape(-1),
+        moved[0],
+        moved[1].reshape(-1),
         rel,
         racc.reshape(-1),
     )

time: 137 us -> 123 us (0.90)
  waiting for transfers between devices: 58.4 us -> 35.7 us
  starting transfers between devices: 34.5 us -> 47 us
  local copies, waits for them, and re-layouts: 4.25 us -> 1.37 us
    ppermute x32, waiting for transfers between devices: 58.4 us -> 33 us  [crossed(): return lax.ppermute(value, axis, [(k, k ^ bits) for k in range(count)])]
    ppermute x32, starting transfers between devices: 30.8 us -> 38.3 us  [crossed(): return lax.ppermute(value, axis, [(k, k ^ bits) for k in range(count)])]
    ppermute x4 -> x5, starting transfers between devices: 3.65 us -> 8.76 us  [shifted(): lax.ppermute(value, axis, [(k, (k + steps) % count) for k in range(count)])]
    ppermute x4 -> x5, waiting for transfers between devices: 0.01 us -> 2.66 us  [shifted(): lax.ppermute(value, axis, [(k, (k + steps) % count) for k in range(count)])]
    pallas_call x15 -> x14, Pallas kernels: 37.6 us -> 37.5 us  [call(): pl.pallas_call(body, out_shape=tuple((jax.ShapeDtypeStruct(s, d) for s, d...]
  transfers between devices with their start and end apart: 36 -> 37, of which waited for: 17 -> 17; matrix products, arithmetic and copies ran while one was open for 0% -> 0% of each run, Pallas kernels for 13% -> 16%
where the time goes in v2:
time: 123 us
  starting transfers between devices  47 us (38%)
  Pallas kernels  37.5 us (30%)
  waiting for transfers between devices  35.7 us (29%)
  local copies, waits for them, and re-layouts  1.37 us (1%)
    ppermute x32, starting transfers between devices, crossed(): return lax.ppermute(value, axis, [(k, k ^ bits) for k in range(count)])  38.3 us
    pallas_call x14, Pallas kernels, call(): pl.pallas_call(body, out_shape=tuple((jax.ShapeDtypeStruct(s, d) for s, d...  37.5 us
    ppermute x32, waiting for transfers between devices, crossed(): return lax.ppermute(value, axis, [(k, k ^ bits) for k in range(count)])  33 us
    ppermute x5, starting transfers between devices, shifted(): lax.ppermute(value, axis, [(k, (k + steps) % count) for k in range(count)])  8.76 us
    ppermute x5, waiting for transfers between devices, shifted(): lax.ppermute(value, axis, [(k, (k + steps) % count) for k in range(count)])  2.66 us
  transfers between devices with their start and end apart: 37, of which 17 were waited for; matrix products, arithmetic and copies ran while one was open for 0% of the time, Pallas kernels for 16%

profile of v2, /device:TPU:1, one launch (start us, length us, event | category | flops | bytes accessed | tf_op | source)
XLA Modules:
  0.0 122.6 jit_solution(12227918076436177300)
XLA Ops:
  0.6 3.0 %shard_map.145 = (s32[4,8,128]{2,1,0:T(8,128)S(1)}, s32[4,8,128]{2,1,0:T(8,128)S(1)}, s32[4,8,128]{2,1,0:T(8,128)S(1)}, s32[4,8,128]{2,1,0:T(8,128)S(1)}, f32[8,...) custom-call(s32[4,8,128]{2,1,0:T(8,128)} %bitcast.11, ...), custom_call_target="tpu_custom_call" | custom-call | tf_op jit(solution)/shard_map/pallas_call | solution.py:276
  3.7 3.6 %shard_map.146 = (f32[64,256]{1,0:T(8,128)S(1)}, f32[64,256]{1,0:T(8,128)S(1)}, bf16[2,1024,512]{2,1,0:T(8,128)(2,1)S(1)}, bf16[2,1024,256]{2,1,0:T(8,128)(2,1)S(1)}, f32[1024,256]{1,0:T(8,128)S(1)}) custom-call(s32[1]{0:T(128)} %bitcast.refs_0_.core_ref, f32[128,256]{1,0:T(8,128)S(1)} %get-tuple-element.99.refs_1_.refs_4_, ...), custom_call_target="tpu_custom_call" | custom-call | tf_op jit(solution)/shard_map/pallas_call | solution.py:276
  9.1 2.9 %collective-permute-start.4 = (f32[520,256]{1,0:T(8,128)S(1)}, f32[520,256]{1,0:T(8,128)S(1)}, u32[]{:S(2)}, u32[]{:S(2)}) collective-permute-start(f32[520,256]{1,0:T(8,128)S(1)} %shard_map.147), channel_id=1, source_target_pairs={{0,1},{1,2},{2,3},{3,4},{4,5},{5,6},{6,7},{7,0},{8,9},{9,10},{10,1... | collective-permute-start | bytes 1597448 | tf_op jit(solution)/shard_map/ppermute | solution.py:288
  11.9 2.2 %collective-permute-start.3 = (f32[64,256]{1,0:T(8,128)S(1)}, f32[64,256]{1,0:T(8,128)S(1)}, u32[]{:S(2)}, u32[]{:S(2)}) collective-permute-start(f32[64,256]{1,0:T(8,128)S(1)} %add.84), channel_id=1, source_target_pairs={{0,24},{8,16},{16,8},{24,0},{1,25},{9,17},{17,9},{25,1},{2,26},{10... | collective-permute-start | bytes 196616 | tf_op jit(solution)/shard_map/ppermute | solution.py:293
  21.8 3.0 %shard_map.148 = (f32[1024,256]{1,0:T(8,128)S(1)}, f32[8,128]{1,0:T(8,128)S(1)}, f32[1024,256]{1,0:T(8,128)S(1)}, f32[8,512]{1,0:T(8,128)S(1)}) custom-call(s32[4,8,128]{2,1,0:T(8,128)S(1)} %get-tuple-element.113.esr_ref, s32[4,8,128]{2,1,0:T(8,128)S(1)} %get-tuple-element.114.neg_ref, f32[1024,256]{1,0:T(8,128)S(1)} %get-tuple-element.115.gsr_ref, ...), custom_call_target="tpu_custom_call" | custom-call | tf_op jit(solution)/shard_map/pallas_call | solution.py:276
  25.5 3.5 %collective-permute-start.8 = (f32[64,256]{1,0:T(8,128)S(1)}, f32[64,256]{1,0:T(8,128)S(1)}, u32[]{:S(2)}, u32[]{:S(2)}) collective-permute-start(f32[64,256]{1,0:T(8,128)S(1)} %add_add_fusion.6.refs_1_), channel_id=1, source_target_pairs={{0,1},{1,0},{2,3},{3,2},{4,5},{5,4},{6,7},{7,6},{8,9},{9,8},{10,11... | collective-permute-start | bytes 196616 | tf_op jit(solution)/shard_map/ppermute | solution.py:293
  29.9 3.9 %shard_map.149 = (f32[64,256]{1,0:T(8,128)S(1)}, f32[64,256]{1,0:T(8,128)S(1)}, bf16[2,1024,512]{2,1,0:T(8,128)(2,1)S(1)}, bf16[2,1024,256]{2,1,0:T(8,128)(2,1)S...) custom-call(s32[1]{0:T(128)} %bitcast.refs_0_.core_ref, ...), custom_call_target="tpu_custom_call" | custom-call | tf_op jit(solution)/shard_map/pallas_call | solution.py:276
  37.0 2.2 %collective-permute-start.12 = (f32[64,256]{1,0:T(8,128)S(1)}, f32[64,256]{1,0:T(8,128)S(1)}, u32[]{:S(2)}, u32[]{:S(2)}) collective-permute-start(f32[64,256]{1,0:T(8,128)S(1)} %add.91), channel_id=1, source_target_pairs={{0,24},{8,16},{16,8},{24,0},{1,25},{9,17},{17,9},{25,1},{2,26},{10... | collective-permute-start | bytes 196616 | tf_op jit(solution)/shard_map/ppermute | solution.py:293
  39.7 2.3 %collective-permute-done.12 = f32[64,256]{1,0:T(8,128)S(1)} collective-permute-done((f32[64,256]{1,0:T(8,128)S(1)}, f32[64,256]{1,0:T(8,128)S(1)}, u32[]{:S(2)}, u32[]{:S(2)}) %collective-permute-start.12) | collective-permute-done | bytes 65568 | tf_op jit(solution)/shard_map/ppermute | solution.py:293
  43.3 2.3 %collective-permute-start.16 = (f32[64,256]{1,0:T(8,128)S(1)}, f32[64,256]{1,0:T(8,128)S(1)}, u32[]{:S(2)}, u32[]{:S(2)}) collective-permute-start(f32[64,256]{1,0:T(8,128)S(1)} %add_add_fusion.5), channel_id=1, source_target_pairs={{0,6},{1,7},{2,4},{3,5},{4,2},{5,3},{6,0},{7,1},{8,14},{9,15},{10,... | collective-permute-start | bytes 196616 | tf_op jit(solution)/shard_map/ppermute | solution.py:293
  46.9 3.0 %shard_map.151 = (f32[1024,256]{1,0:T(8,128)S(1)}, f32[8,128]{1,0:T(8,128)S(1)}, f32[1024,256]{1,0:T(8,128)S(1)}, f32[8,512]{1,0:T(8,128)S(1)}) custom-call(s32[4,8,128]{2,1,0:T(8,128)S(1)} %get-tuple-element.113.esr_ref, s32[4,8,128]{2,1,0:T(8,128)S(1)} %get-tuple-element.114.neg_ref, f32[1024,256]{1,0:T(8,128)S(1)} %get-tuple-element.135.gsr_ref, ...), custom_call_target="tpu_custom_call" | custom-call | tf_op jit(solution)/shard_map/pallas_call | solution.py:276
  50.4 3.9 %collective-permute-start.17 = (f32[64,256]{1,0:T(8,128)S(1)}, f32[64,256]{1,0:T(8,128)S(1)}, u32[]{:S(2)}, u32[]{:S(2)}) collective-permute-start(f32[64,256]{1,0:T(8,128)S(1)} %add_add_fusion.4.refs_1_), channel_id=1, source_target_pairs={{0,1},{1,0},{2,3},{3,2},{4,5},{5,4},{6,7},{7,6},{8,9},{9,8},{10,11... | collective-permute-start | bytes 196616 | tf_op jit(solution)/shard_map/ppermute | solution.py:293
  55.2 3.9 %shard_map.152 = (f32[64,256]{1,0:T(8,128)S(1)}, f32[64,256]{1,0:T(8,128)S(1)}, bf16[2,1024,512]{2,1,0:T(8,128)(2,1)S(1)}, bf16[2,1024,256]{2,1,0:T(8,128)(2,1)S...) custom-call(s32[1]{0:T(128)} %bitcast.refs_0_.core_ref, ...), custom_call_target="tpu_custom_call" | custom-call | tf_op jit(solution)/shard_map/pallas_call | solution.py:276
  62.4 2.2 %collective-permute-start.21 = (f32[64,256]{1,0:T(8,128)S(1)}, f32[64,256]{1,0:T(8,128)S(1)}, u32[]{:S(2)}, u32[]{:S(2)}) collective-permute-start(f32[64,256]{1,0:T(8,128)S(1)} %add.98), channel_id=1, source_target_pairs={{0,24},{8,16},{16,8},{24,0},{1,25},{9,17},{17,9},{25,1},{2,26},{10... | collective-permute-start | bytes 196616 | tf_op jit(solution)/shard_map/ppermute | solution.py:293
  65.1 2.3 %collective-permute-done.21 = f32[64,256]{1,0:T(8,128)S(1)} collective-permute-done((f32[64,256]{1,0:T(8,128)S(1)}, f32[64,256]{1,0:T(8,128)S(1)}, u32[]{:S(2)}, u32[]{:S(2)}) %collective-permute-start.21) | collective-permute-done | bytes 65568 | tf_op jit(solution)/shard_map/ppermute | solution.py:293
  68.7 2.3 %collective-permute-start.25 = (f32[64,256]{1,0:T(8,128)S(1)}, f32[64,256]{1,0:T(8,128)S(1)}, u32[]{:S(2)}, u32[]{:S(2)}) collective-permute-start(f32[64,256]{1,0:T(8,128)S(1)} %add_add_fusion.3), channel_id=1, source_target_pairs={{0,6},{1,7},{2,4},{3,5},{4,2},{5,3},{6,0},{7,1},{8,14},{9,15},{10,... | collective-permute-start | bytes 196616 | tf_op jit(solution)/shard_map/ppermute | solution.py:293
  72.3 3.0 %shard_map.154 = (f32[1024,256]{1,0:T(8,128)S(1)}, f32[8,128]{1,0:T(8,128)S(1)}, f32[1024,256]{1,0:T(8,128)S(1)}, f32[8,512]{1,0:T(8,128)S(1)}) custom-call(s32[4,8,128]{2,1,0:T(8,128)S(1)} %get-tuple-element.113.esr_ref, s32[4,8,128]{2,1,0:T(8,128)S(1)} %get-tuple-element.114.neg_ref, f32[1024,256]{1,0:T(8,128)S(1)} %get-tuple-element.156.gsr_ref, ...), custom_call_target="tpu_custom_call" | custom-call | tf_op jit(solution)/shard_map/pallas_call | solution.py:276
  75.8 3.9 %collective-permute-start.26 = (f32[64,256]{1,0:T(8,128)S(1)}, f32[64,256]{1,0:T(8,128)S(1)}, u32[]{:S(2)}, u32[]{:S(2)}) collective-permute-start(f32[64,256]{1,0:T(8,128)S(1)} %add_add_fusion.2.refs_1_), channel_id=1, source_target_pairs={{0,1},{1,0},{2,3},{3,2},{4,5},{5,4},{6,7},{7,6},{8,9},{9,8},{10,11... | collective-permute-start | bytes 196616 | tf_op jit(solution)/shard_map/ppermute | solution.py:293
  80.6 3.9 %shard_map.155 = (f32[64,256]{1,0:T(8,128)S(1)}, f32[64,256]{1,0:T(8,128)S(1)}, bf16[2,1024,512]{2,1,0:T(8,128)(2,1)S(1)}, bf16[2,1024,256]{2,1,0:T(8,128)(2,1)S...) custom-call(s32[1]{0:T(128)} %bitcast.refs_0_.core_ref, ...), custom_call_target="tpu_custom_call" | custom-call | tf_op jit(solution)/shard_map/pallas_call | solution.py:276
  86.6 2.2 %collective-permute-start.30 = (f32[64,256]{1,0:T(8,128)S(1)}, f32[64,256]{1,0:T(8,128)S(1)}, u32[]{:S(2)}, u32[]{:S(2)}) collective-permute-start(f32[64,256]{1,0:T(8,128)S(1)} %add.105), channel_id=1, source_target_pairs={{0,24},{8,16},{16,8},{24,0},{1,25},{9,17},{17,9},{25,1},{2,26},{10... | collective-permute-start | bytes 196616 | tf_op jit(solution)/shard_map/ppermute | solution.py:293
  95.8 2.7 %shard_map.157 = (f32[1024,256]{1,0:T(8,128)}, f32[8,128]{1,0:T(8,128)}) custom-call(s32[4,8,128]{2,1,0:T(8,128)S(1)} %get-tuple-element.113.esr_ref, s32[4,8,128]{2,1,0:T(8,128)S(1)} %get-tuple-element.114.neg_ref, f32[1024,256]{1,0:T(8,128)S(1)} %get-tuple-element.178.gsr_ref, f32[1024,256]{1,0:T(8,128)S(1)} %get-tuple-element.179.src_ref, ...), custom_call_target="tpu_custom_call" | custom-call | tf_op jit(solution)/shard_map/pallas_call | solution.py:276
  98.5 6.1 %collective-permute-done.33 = f32[64,256]{1,0:T(8,128)S(1)} collective-permute-done((f32[64,256]{1,0:T(8,128)S(1)}, f32[64,256]{1,0:T(8,128)S(1)}, u32[]{:S(2)}, u32[]{:S(2)}) %collective-permute-start.33) | collective-permute-done | bytes 65568 | tf_op jit(solution)/shard_map/ppermute | solution.py:293
  104.6 11.3 %collective-permute-done.32 = f32[64,256]{1,0:T(8,128)S(1)} collective-permute-done((f32[64,256]{1,0:T(8,128)S(1)}, f32[64,256]{1,0:T(8,128)S(1)}, u32[]{:S(2)}, u32[]{:S(2)}) %collective-permute-start.32) | collective-permute-done | bytes 65568 | tf_op jit(solution)/shard_map/ppermute | solution.py:293
  117.6 2.7 %collective-permute-done.35 = f32[4,128]{1,0:T(4,128)S(1)} collective-permute-done((f32[4,128]{1,0:T(4,128)S(1)}, f32[4,128]{1,0:T(4,128)S(1)}, u32[]{:S(2)}, u32[]{:S(2)}) %collective-permute-start.35) | collective-permute-done | bytes 2080 | tf_op jit(solution)/shard_map/ppermute | solution.py:288
  (78 shorter events, 39.3 us)
Async XLA Ops:
  9.1 9.1 %collective-permute-start.4 = (f32[520,256]{1,0:T(8,128)S(1)}, f32[520,256]{1,0:T(8,128)S(1)}, u32[]{:S(2)}, u32[]{:S(2)}) collective-permute-start(f32[520,256]{1,0:T(8,128)S(1)} %shard_map.147), channel_id=1, source_target_pairs={{0,1},{1,2},{2,3},{3,4},{4,5},{5,6},{6,7},{7,0},{8,9},{9,10},{10,1... | collective-permute-start | bytes 1597448 | tf_op jit(solution)/shard_map/ppermute | solution.py:288
  11.9 4.3 %collective-permute-start.3 = (f32[64,256]{1,0:T(8,128)S(1)}, f32[64,256]{1,0:T(8,128)S(1)}, u32[]{:S(2)}, u32[]{:S(2)}) collective-permute-start(f32[64,256]{1,0:T(8,128)S(1)} %add.84), channel_id=1, source_target_pairs={{0,24},{8,16},{16,8},{24,0},{1,25},{9,17},{17,9},{25,1},{2,26},{10... | collective-permute-start | bytes 196616 | tf_op jit(solution)/shard_map/ppermute | solution.py:293
  18.2 6.7 %collective-permute-start.7 = (f32[64,256]{1,0:T(8,128)S(1)}, f32[64,256]{1,0:T(8,128)S(1)}, u32[]{:S(2)}, u32[]{:S(2)}) collective-permute-start(f32[64,256]{1,0:T(8,128)S(1)} %add_add_fusion.7), channel_id=1, source_target_pairs={{0,6},{1,7},{2,4},{3,5},{4,2},{5,3},{6,0},{7,1},{8,14},{9,15},{10,... | collective-permute-start | bytes 196616 | tf_op jit(solution)/shard_map/ppermute | solution.py:293
  20.3 5.2 %collective-permute-start.6 = (f32[64,256]{1,0:T(8,128)S(1)}, f32[64,256]{1,0:T(8,128)S(1)}, u32[]{:S(2)}, u32[]{:S(2)}) collective-permute-start(f32[64,256]{1,0:T(8,128)S(1)} %add_add_fusion.7), channel_id=1, source_target_pairs={{0,4},{1,5},{2,6},{3,7},{4,0},{5,1},{6,2},{7,3},{8,12},{9,13},{10,... | collective-permute-start | bytes 196616 | tf_op jit(solution)/shard_map/ppermute | solution.py:293
  20.7 4.7 %collective-permute-start.5 = (f32[64,256]{1,0:T(8,128)S(1)}, f32[64,256]{1,0:T(8,128)S(1)}, u32[]{:S(2)}, u32[]{:S(2)}) collective-permute-start(f32[64,256]{1,0:T(8,128)S(1)} %add_add_fusion.7), channel_id=1, source_target_pairs={{0,2},{1,3},{2,0},{3,1},{4,6},{5,7},{6,4},{7,5},{8,10},{9,11},{10,... | collective-permute-start | bytes 196616 | tf_op jit(solution)/shard_map/ppermute | solution.py:293
  25.5 4.4 %collective-permute-start.8 = (f32[64,256]{1,0:T(8,128)S(1)}, f32[64,256]{1,0:T(8,128)S(1)}, u32[]{:S(2)}, u32[]{:S(2)}) collective-permute-start(f32[64,256]{1,0:T(8,128)S(1)} %add_add_fusion.6.refs_1_), channel_id=1, source_target_pairs={{0,1},{1,0},{2,3},{3,2},{4,5},{5,4},{6,7},{7,6},{8,9},{9,8},{10,11... | collective-permute-start | bytes 196616 | tf_op jit(solution)/shard_map/ppermute | solution.py:293
  35.8 7.5 %collective-permute-start.13 = (f32[520,256]{1,0:T(8,128)S(1)}, f32[520,256]{1,0:T(8,128)S(1)}, u32[]{:S(2)}, u32[]{:S(2)}) collective-permute-start(f32[520,256]{1,0:T(8,128)S(1)} %shard_map.150), channel_id=1, source_target_pairs={{0,1},{1,2},{2,3},{3,4},{4,5},{5,6},{6,7},{7,0},{8,9},{9,10},{10,1... | collective-permute-start | bytes 1597448 | tf_op jit(solution)/shard_map/ppermute | solution.py:288
  37.0 5.0 %collective-permute-start.12 = (f32[64,256]{1,0:T(8,128)S(1)}, f32[64,256]{1,0:T(8,128)S(1)}, u32[]{:S(2)}, u32[]{:S(2)}) collective-permute-start(f32[64,256]{1,0:T(8,128)S(1)} %add.91), channel_id=1, source_target_pairs={{0,24},{8,16},{16,8},{24,0},{1,25},{9,17},{17,9},{25,1},{2,26},{10... | collective-permute-start | bytes 196616 | tf_op jit(solution)/shard_map/ppermute | solution.py:293
  43.3 6.6 %collective-permute-start.16 = (f32[64,256]{1,0:T(8,128)S(1)}, f32[64,256]{1,0:T(8,128)S(1)}, u32[]{:S(2)}, u32[]{:S(2)}) collective-permute-start(f32[64,256]{1,0:T(8,128)S(1)} %add_add_fusion.5), channel_id=1, source_target_pairs={{0,6},{1,7},{2,4},{3,5},{4,2},{5,3},{6,0},{7,1},{8,14},{9,15},{10,... | collective-permute-start | bytes 196616 | tf_op jit(solution)/shard_map/ppermute | solution.py:293
  45.6 4.8 %collective-permute-start.15 = (f32[64,256]{1,0:T(8,128)S(1)}, f32[64,256]{1,0:T(8,128)S(1)}, u32[]{:S(2)}, u32[]{:S(2)}) collective-permute-start(f32[64,256]{1,0:T(8,128)S(1)} %add_add_fusion.5), channel_id=1, source_target_pairs={{0,4},{1,5},{2,6},{3,7},{4,0},{5,1},{6,2},{7,3},{8,12},{9,13},{10,... | collective-permute-start | bytes 196616 | tf_op jit(solution)/shard_map/ppermute | solution.py:293
  45.6 4.8 %collective-permute-start.14 = (f32[64,256]{1,0:T(8,128)S(1)}, f32[64,256]{1,0:T(8,128)S(1)}, u32[]{:S(2)}, u32[]{:S(2)}) collective-permute-start(f32[64,256]{1,0:T(8,128)S(1)} %add_add_fusion.5), channel_id=1, source_target_pairs={{0,2},{1,3},{2,0},{3,1},{4,6},{5,7},{6,4},{7,5},{8,10},{9,11},{10,... | collective-permute-start | bytes 196616 | tf_op jit(solution)/shard_map/ppermute | solution.py:293
  50.4 4.8 %collective-permute-start.17 = (f32[64,256]{1,0:T(8,128)S(1)}, f32[64,256]{1,0:T(8,128)S(1)}, u32[]{:S(2)}, u32[]{:S(2)}) collective-permute-start(f32[64,256]{1,0:T(8,128)S(1)} %add_add_fusion.4.refs_1_), channel_id=1, source_target_pairs={{0,1},{1,0},{2,3},{3,2},{4,5},{5,4},{6,7},{7,6},{8,9},{9,8},{10,11... | collective-permute-start | bytes 196616 | tf_op jit(solution)/shard_map/ppermute | solution.py:293
  61.2 7.6 %collective-permute-start.22 = (f32[520,256]{1,0:T(8,128)S(1)}, f32[520,256]{1,0:T(8,128)S(1)}, u32[]{:S(2)}, u32[]{:S(2)}) collective-permute-start(f32[520,256]{1,0:T(8,128)S(1)} %shard_map.153), channel_id=1, source_target_pairs={{0,1},{1,2},{2,3},{3,4},{4,5},{5,6},{6,7},{7,0},{8,9},{9,10},{10,1... | collective-permute-start | bytes 1597448 | tf_op jit(solution)/shard_map/ppermute | solution.py:288
  62.4 5.0 %collective-permute-start.21 = (f32[64,256]{1,0:T(8,128)S(1)}, f32[64,256]{1,0:T(8,128)S(1)}, u32[]{:S(2)}, u32[]{:S(2)}) collective-permute-start(f32[64,256]{1,0:T(8,128)S(1)} %add.98), channel_id=1, source_target_pairs={{0,24},{8,16},{16,8},{24,0},{1,25},{9,17},{17,9},{25,1},{2,26},{10... | collective-permute-start | bytes 196616 | tf_op jit(solution)/shard_map/ppermute | solution.py:293
  68.7 6.6 %collective-permute-start.25 = (f32[64,256]{1,0:T(8,128)S(1)}, f32[64,256]{1,0:T(8,128)S(1)}, u32[]{:S(2)}, u32[]{:S(2)}) collective-permute-start(f32[64,256]{1,0:T(8,128)S(1)} %add_add_fusion.3), channel_id=1, source_target_pairs={{0,6},{1,7},{2,4},{3,5},{4,2},{5,3},{6,0},{7,1},{8,14},{9,15},{10,... | collective-permute-start | bytes 196616 | tf_op jit(solution)/shard_map/ppermute | solution.py:293
  71.0 4.8 %collective-permute-start.24 = (f32[64,256]{1,0:T(8,128)S(1)}, f32[64,256]{1,0:T(8,128)S(1)}, u32[]{:S(2)}, u32[]{:S(2)}) collective-permute-start(f32[64,256]{1,0:T(8,128)S(1)} %add_add_fusion.3), channel_id=1, source_target_pairs={{0,4},{1,5},{2,6},{3,7},{4,0},{5,1},{6,2},{7,3},{8,12},{9,13},{10,... | collective-permute-start | bytes 196616 | tf_op jit(solution)/shard_map/ppermute | solution.py:293
  71.0 4.8 %collective-permute-start.23 = (f32[64,256]{1,0:T(8,128)S(1)}, f32[64,256]{1,0:T(8,128)S(1)}, u32[]{:S(2)}, u32[]{:S(2)}) collective-permute-start(f32[64,256]{1,0:T(8,128)S(1)} %add_add_fusion.3), channel_id=1, source_target_pairs={{0,2},{1,3},{2,0},{3,1},{4,6},{5,7},{6,4},{7,5},{8,10},{9,11},{10,... | collective-permute-start | bytes 196616 | tf_op jit(solution)/shard_map/ppermute | solution.py:293
  75.8 4.8 %collective-permute-start.26 = (f32[64,256]{1,0:T(8,128)S(1)}, f32[64,256]{1,0:T(8,128)S(1)}, u32[]{:S(2)}, u32[]{:S(2)}) collective-permute-start(f32[64,256]{1,0:T(8,128)S(1)} %add_add_fusion.2.refs_1_), channel_id=1, source_target_pairs={{0,1},{1,0},{2,3},{3,2},{4,5},{5,4},{6,7},{7,6},{8,9},{9,8},{10,11... | collective-permute-start | bytes 196616 | tf_op jit(solution)/shard_map/ppermute | solution.py:293
  86.6 4.9 %collective-permute-start.30 = (f32[64,256]{1,0:T(8,128)S(1)}, f32[64,256]{1,0:T(8,128)S(1)}, u32[]{:S(2)}, u32[]{:S(2)}) collective-permute-start(f32[64,256]{1,0:T(8,128)S(1)} %add.105), channel_id=1, source_target_pairs={{0,24},{8,16},{16,8},{24,0},{1,25},{9,17},{17,9},{25,1},{2,26},{10... | collective-permute-start | bytes 196616 | tf_op jit(solution)/shard_map/ppermute | solution.py:293
  89.3 31.9 %collective-permute-start.34 = (f32[512,256]{1,0:T(8,128)S(1)}, f32[512,256]{1,0:T(8,128)S(1)}, u32[]{:S(2)}, u32[]{:S(2)}) collective-permute-start(f32[512,256]{1,0:T(8,128)S(1)} %get-tuple-element.185), channel_id=1, source_target_pairs={{0,5},{1,6},{2,7},{3,0},{4,1},{5,2},{6,3},{7,4},{8,13},{9,14},{10,... | collective-permute-start | bytes 1572872 | tf_op jit(solution)/shard_map/ppermute | solution.py:288
  92.2 12.5 %collective-permute-start.33 = (f32[64,256]{1,0:T(8,128)S(1)}, f32[64,256]{1,0:T(8,128)S(1)}, u32[]{:S(2)}, u32[]{:S(2)}) collective-permute-start(f32[64,256]{1,0:T(8,128)S(1)} %add_add_fusion.1), channel_id=1, source_target_pairs={{0,6},{1,7},{2,4},{3,5},{4,2},{5,3},{6,0},{7,1},{8,14},{9,15},{10,... | collective-permute-start | bytes 196616 | tf_op jit(solution)/shard_map/ppermute | solution.py:293
  93.8 22.1 %collective-permute-start.32 = (f32[64,256]{1,0:T(8,128)S(1)}, f32[64,256]{1,0:T(8,128)S(1)}, u32[]{:S(2)}, u32[]{:S(2)}) collective-permute-start(f32[64,256]{1,0:T(8,128)S(1)} %add_add_fusion.1), channel_id=1, source_target_pairs={{0,4},{1,5},{2,6},{3,7},{4,0},{5,1},{6,2},{7,3},{8,12},{9,13},{10,... | collective-permute-start | bytes 196616 | tf_op jit(solution)/shard_map/ppermute | solution.py:293
  94.3 21.6 %collective-permute-start.31 = (f32[64,256]{1,0:T(8,128)S(1)}, f32[64,256]{1,0:T(8,128)S(1)}, u32[]{:S(2)}, u32[]{:S(2)}) collective-permute-start(f32[64,256]{1,0:T(8,128)S(1)} %add_add_fusion.1), channel_id=1, source_target_pairs={{0,2},{1,3},{2,0},{3,1},{4,6},{5,7},{6,4},{7,5},{8,10},{9,11},{10,... | collective-permute-start | bytes 196616 | tf_op jit(solution)/shard_map/ppermute | solution.py:293
  115.9 4.4 %collective-permute-start.36 = (f32[64,256]{1,0:T(8,128)S(1)}, f32[64,256]{1,0:T(8,128)S(1)}, u32[]{:S(2)}, u32[]{:S(2)}) collective-permute-start(f32[64,256]{1,0:T(8,128)S(1)} %add_add_fusion.mine_ref), channel_id=1, source_target_pairs={{0,1},{1,0},{2,3},{3,2},{4,5},{5,4},{6,7},{7,6},{8,9},{9,8},{10,11... | collective-permute-start | bytes 196616 | tf_op jit(solution)/shard_map/ppermute | solution.py:293
  (13 other events, 41.8 us)

commit v3 on v2

--- a/solution.py
+++ b/solution.py
@@ -121,18 +121,20 @@
         load.wait()
 
 
-def relation_update(core_ref, mine_ref, peer_ref, rel_ref, acc_ref):
+def both_halves(core_ref, mine_ref, peer_ref):
     first = core_ref[0] == 0
     mine, peer = mine_ref[...], peer_ref[...]
-    grad = jnp.concatenate(
-        [jnp.where(first, mine, peer), jnp.where(first, peer, mine)], axis=0
-    )
+    return jnp.concatenate([jnp.where(first, mine, peer), jnp.where(first, peer, mine)], axis=0)
+
+
+def relation_update(grad, rel_ref, acc_ref):
     nrel = grad.shape[0]
     total, scale = row_scale(columns(jnp.broadcast_to(acc_ref[...], (8, nrel)))[:, 0:1], grad)
     return rel_ref[...] - grad * scale, columns(jnp.broadcast_to(total, (nrel, LANES)))[0:1, :]
 
 
-def query_kernel(step, updated, *refs):
+def query_kernel(step, updated, pieces, *refs):
+    spot_ref, *refs = refs
     if updated:
         core_ref, mine_ref, peer_ref, acc_ref = refs[:4]
         refs = refs[4:]
@@ -145,7 +147,7 @@
     refs = refs[5:]
     if updated:
         rel_out_ref, acc_out_ref = refs
-        rel, total = relation_update(core_ref, mine_ref, peer_ref, rel_ref, acc_ref)
+        rel, total = relation_update(both_halves(core_ref, mine_ref, peer_ref), rel_ref, acc_ref)
         rel_out_ref[...] = rel
         acc_out_ref[...] = total
     else:
@@ -196,36 +198,41 @@
     first = core_ref[0] == 0
     half = nrel // 2
     top, bottom = grad[:half], grad[half:]
-    keep_ref[...] = jnp.where(first, top, bottom)
-    send_ref[...] = jnp.where(first, bottom, top)
-
-
-def dst_kernel(wgt_ref, qry_ref, dst_ref, out_ref, *last):
+    keep = jnp.where(first, top, bottom)
+    send = jnp.where(first, bottom, top)
+    size = half // pieces
+    for m in range(pieces):
+        at = pl.ds(pl.multiple_of((spot_ref[0] ^ m) * size, size), size) if pieces > 1 else slice(0, half)
+        keep_ref[at, :] = keep[m * size : (m + 1) * size]
+        send_ref[at, :] = send[m * size : (m + 1) * size]
+
+
+def dst_kernel(wgt_ref, qry_ref, dst_ref, *outs):
     rows = wgt_ref.shape[2]
     width = dst_ref.shape[1]
+    head = 0 if len(outs) == 1 else outs[0].shape[0]
+    tail_ref = outs[-1]
     grad = (
         dot(wgt_ref[0], qry_ref[0], 0, 0)
         + dot(wgt_ref[0], qry_ref[1], 0, 0)
         + dot(wgt_ref[1], qry_ref[0], 0, 0)
     )
     blocks = rows // LANES
-    sums = jnp.concatenate(
-        [dst_ref[rows : rows + blocks, 0:LANES], jnp.zeros((8 - blocks, LANES), F32)], axis=0
-    ) if blocks < 8 else dst_ref[rows : rows + blocks, 0:LANES]
-    cols = columns(sums)
+    cols = columns(dst_ref[rows : rows + 8, 0:LANES])
     totals = []
     for b in range(blocks):
         at = slice(b * LANES, (b + 1) * LANES)
         total, scale = row_scale(cols[:, b : b + 1], grad[at])
-        out_ref[at, :] = dst_ref[at, :] - grad[at] * scale
         totals.append(total)
-    fresh = jnp.transpose(jnp.concatenate(totals + [totals[0]] * (8 - blocks), axis=1))
-    if last:
-        last[0][...] = fresh[0:blocks]
-    else:
-        out_ref[rows : rows + 8, :] = jnp.concatenate(
-            [fresh, jnp.zeros((8, width - LANES), F32)], axis=1
-        )
+        fresh = dst_ref[at, :] - grad[at] * scale
+        if b * LANES < head:
+            outs[0][at, :] = fresh
+        else:
+            tail_ref[b * LANES - head : (b + 1) * LANES - head, :] = fresh
+    sums = jnp.transpose(jnp.concatenate(totals + [totals[0]] * (8 - blocks), axis=1))
+    tail_ref[rows - head : rows - head + 8, :] = jnp.concatenate(
+        [sums, jnp.zeros((8, width - LANES), F32)], axis=1
+    )
 
 
 def src_kernel(step, last, esr_ref, neg_ref, gsr_ref, src_ref, acc_ref, *refs):
@@ -264,20 +271,52 @@
         write_counts(neg_ref, step + 1, cnt_ref)
 
 
-def final_kernel(core_ref, mine_ref, peer_ref, rel_ref, acc_ref, rel_out_ref, acc_out_ref):
-    rel, total = relation_update(core_ref, mine_ref, peer_ref, rel_ref, acc_ref)
-    rel_out_ref[...] = rel
-    acc_out_ref[...] = total
-
-
-def call(body, outs, args, scratch=(), smem=0, hbm=0):
+def final_kernel(core_ref, spot_ref, *refs):
+    pairs = refs[:-12]
+    rel_ref, acc_ref, head_ref, tail_ref = refs[-12:-8]
+    rel_out, acc_out, dst_out, dac_out, grad_ref, rel_buf, acc_buf, sem = refs[-8:]
+    head = head_ref.shape[0]
+    rest = dst_out.shape[0] - head
+    moves = [
+        pltpu.make_async_copy(source, target, sem.at[k])
+        for k, (source, target) in enumerate(
+            [
+                (head_ref, dst_out.at[pl.ds(0, head)]),
+                (tail_ref.at[pl.ds(0, rest)], dst_out.at[pl.ds(head, rest)]),
+                (tail_ref.at[pl.ds(rest, dac_out.shape[0]), pl.ds(0, LANES)], dac_out),
+                (rel_buf, rel_out),
+                (acc_buf, acc_out),
+            ]
+        )
+    ]
+    for move in moves[:3]:
+        move.start()
+    rows = pairs[0].shape[0] // 2
+    half = grad_ref.shape[0] // 2
+    core = core_ref[0]
+    for k, pair_ref in enumerate(pairs):
+        at = (spot_ref[0] ^ k) * rows
+        mine = pl.multiple_of(core * half + at, rows)
+        peer = pl.multiple_of((1 - core) * half + at, rows)
+        grad_ref[pl.ds(mine, rows), :] = pair_ref[0:rows, :]
+        grad_ref[pl.ds(peer, rows), :] = pair_ref[rows : 2 * rows, :]
+    rel, total = relation_update(grad_ref[...], rel_ref, acc_ref)
+    rel_buf[...] = rel
+    acc_buf[...] = total
+    for move in moves[3:]:
+        move.start()
+    for move in moves:
+        move.wait()
+
+
+def call(body, outs, args, scratch=(), smem=0, hbm=0, out_space=pltpu.VMEM):
     spaces = [pltpu.SMEM] * smem + [pltpu.VMEM] * (len(args) - smem - hbm) + [pltpu.HBM] * hbm
     in_specs = [pl.BlockSpec(memory_space=space) for space in spaces]
     return pl.pallas_call(
         body,
         out_shape=tuple(jax.ShapeDtypeStruct(s, d) for s, d in outs),
         in_specs=in_specs,
-        out_specs=tuple(pl.BlockSpec(memory_space=pltpu.VMEM) for _ in outs),
+        out_specs=tuple(pl.BlockSpec(memory_space=out_space) for _ in outs),
         scratch_shapes=list(scratch),
         compiler_params=pltpu.CompilerParams(vmem_limit_bytes=40 << 20),
     )(*args[: len(args) - hbm], *[pltpu.with_memory_space_constraint(v, pltpu.HBM) for v in args[len(args) - hbm :]])
@@ -293,12 +332,18 @@
     return lax.ppermute(value, axis, [(k, k ^ bits) for k in range(count)])
 
 
-def exchanged(value, axis, low):
+def exchanged(value, axis, low, late=None):
     count = lax.axis_size(axis)
     while low < count:
         reach = min(4, count // low)
-        value = sum([crossed(value, axis, low * k) for k in range(1, reach)], value)
+        last = value
+        if late is not None:
+            last, late = lax.optimization_barrier((value, late))
+        come = [crossed(last if k == 1 else value, axis, low * k) for k in range(1, reach)]
+        value = sum(come, value)
         low *= reach
+        if late is not None:
+            return exchanged(value, axis, low), late
     return value
 
 
@@ -312,6 +357,9 @@
     drows = dst_emb.shape[0]
     nrel = rel_emb.shape[0]
     core = (lax.axis_index("dst") & 1).astype(jnp.int32).reshape(1)
+    spot = lax.axis_index("src").astype(jnp.int32).reshape(1)
+    nsrc = lax.axis_size("src")
+    head = (drows // LANES // 2) * LANES
     sacc = src_acc.reshape(srows // LANES, LANES)
     dblocks = drows // LANES
     stack = pltpu.VMEM((2 * srows, width), BF16)
@@ -333,7 +381,7 @@
             ((eblocks, drows), F32),
         ],
         firsts,
-        [stack, pltpu.SemaphoreType.DMA((srows // CHUNK,)), pltpu.SemaphoreType.DMA((len(firsts) - 1,))],
+        [stack, pltpu.SemaphoreType.DMA((srows // CHUNK,)), pltpu.SemaphoreType.DMA((len(firsts),))],
         hbm=len(firsts),
     )
     half = peer = None
@@ -347,54 +395,57 @@
             ((edges, width), F32),
         ]
         if step == 0:
-            args = [core, rel, rows, dst, eds, erl, counts]
+            args = [spot, core, rel, rows, dst, eds, erl, counts]
         else:
-            args = [core, half, peer, racc, rel, rows, dst, eds, erl, counts]
+            args = [spot, core, half, peer, racc, rel, rows, dst, eds, erl, counts]
             outs += [((nrel, width), F32), ((1, nrel), F32)]
-        res = call(functools.partial(query_kernel, step, step > 0), outs, args, smem=1)
+        res = call(functools.partial(query_kernel, step, step > 0, nsrc if last else 1), outs, args, smem=2)
         keep, send, wgt, qry, gsr = res[:5]
         if step > 0:
             rel, racc = res[5:]
-        half = crossed(send, "dst", 1)
-        outs = [((drows, width), F32), ((dblocks, LANES), F32)] if last else [((drows + 8, width), F32)]
-        res = call(dst_kernel, outs, [wgt, qry, dst])
-        half, *res = lax.optimization_barrier((keep + half, *res))
-        moved = [shifted(v, "dst", 1 if not last else -(steps - 1)) for v in res]
-        half = exchanged(half, "src", 1)
+        come = crossed(send, "dst", 1)
+        parts = [head, drows - head + 8] if last else [drows + 8]
+        dst = call(dst_kernel, [((n, width), F32) for n in parts], [wgt, qry, dst])
+        come, *dst = lax.optimization_barrier((come, *dst))
+        dst = [shifted(v, "dst", -(steps - 1) if last else 1) for v in dst]
+        half = keep + come
+        outs = [((srows, width), F32), ((srows // LANES, LANES), F32)]
         if last:
+            size = nrel // 2 // nsrc
+            half = half[:size] + sum(
+                crossed(half[k * size : (k + 1) * size], "src", k) for k in range(1, nsrc)
+            )
+            src, sacc = call(
+                functools.partial(src_kernel, step, last), outs, [esr, neg, gsr, src, sacc]
+            )
+            half, src, sacc, dst[0] = lax.optimization_barrier((half, src, sacc, dst[0]))
+            half = exchanged(half, "dst", 2)
+            pair = jnp.concatenate([half, crossed(half, "dst", 1)], axis=0)
+            pairs = [pair] + [crossed(pair, "src", k) for k in range(1, nsrc)]
+        else:
+            half = exchanged(half, "src", 1)
             half, gsr = lax.optimization_barrier((half, gsr))
-        else:
-            half, gsr, moved = lax.optimization_barrier((half, gsr, moved))
-        outs = [((srows, width), F32), ((srows // LANES, LANES), F32)]
-        if not last:
             outs += [((edges, width), F32), ((eblocks, drows), F32)]
-        res = call(
-            functools.partial(src_kernel, step, last),
-            outs,
-            [esr, neg, gsr, src, sacc],
-            [] if last else [stack],
-        )
-        half = exchanged(half, "dst", 2)
-        half, *res = lax.optimization_barrier((half, *res))
-        peer = crossed(half, "dst", 1)
-        src, sacc = res[:2]
-        if not last:
-            rows, counts = res[2:]
-            (dst,) = moved
-    rel, racc = call(
+            res = call(
+                functools.partial(src_kernel, step, last), outs, [esr, neg, gsr, src, sacc], [stack]
+            )
+            half, (dst,) = exchanged(half, "dst", 2, dst)
+            half, src, sacc, rows, counts = lax.optimization_barrier((half, *res))
+            peer = crossed(half, "dst", 1)
+    rel, racc, dst, dacc = call(
         final_kernel,
-        [((nrel, width), F32), ((1, nrel), F32)],
-        [core, half, peer, rel, racc],
-        smem=1,
-    )
-    return (
-        src,
-        sacc.reshape(-1),
-        moved[0],
-        moved[1].reshape(-1),
-        rel,
-        racc.reshape(-1),
-    )
+        [((nrel, width), F32), ((1, nrel), F32), ((drows, width), F32), ((dblocks, LANES), F32)],
+        [core, spot, *pairs, rel, racc, *dst],
+        [
+            pltpu.VMEM((nrel, width), F32),
+            pltpu.VMEM((nrel, width), F32),
+            pltpu.VMEM((1, nrel), F32),
+            pltpu.SemaphoreType.DMA((5,)),
+        ],
+        smem=2,
+        out_space=pltpu.HBM,
+    )
+    return src, sacc.reshape(-1), dst, dacc.reshape(-1), rel, racc.reshape(-1)
 
 
 def solution(mesh):

time: 123 us -> 110 us (0.89)
  starting transfers between devices: 47 us -> 39.8 us
  waiting for transfers between devices: 35.7 us -> 31.8 us
  local copies, waits for them, and re-layouts: 1.37 us -> 0.01 us
    ppermute x32 -> x35, waiting for transfers between devices: 33 us -> 23.4 us  [crossed(): return lax.ppermute(value, axis, [(k, k ^ bits) for k in range(count)])]
    ppermute x32 -> x35, starting transfers between devices: 38.3 us -> 32 us  [crossed(): return lax.ppermute(value, axis, [(k, k ^ bits) for k in range(count)])]
    ppermute x5, waiting for transfers between devices: 2.66 us -> 8.34 us  [shifted(): lax.ppermute(value, axis, [(k, (k + steps) % count) for k in range(count)])]
    unnamed x2 -> x0, local copies, waits for them, and re-layouts: 1.37 us -> none
  transfers between devices with their start and end apart: 37 -> 40, of which waited for: 17 -> 16; matrix products, arithmetic and copies ran while one was open for 0% -> 0% of each run, Pallas kernels for 16% -> 16%
where the time goes in v3:
time: 110 us
  starting transfers between devices  39.8 us (36%)
  Pallas kernels  37.3 us (34%)
  waiting for transfers between devices  31.8 us (29%)
    pallas_call x14, Pallas kernels, call(): pl.pallas_call(body, out_shape=tuple((jax.ShapeDtypeStruct(s, d) for s, d...  37.3 us
    ppermute x35, starting transfers between devices, crossed(): return lax.ppermute(value, axis, [(k, k ^ bits) for k in range(count)])  32 us
    ppermute x35, waiting for transfers between devices, crossed(): return lax.ppermute(value, axis, [(k, k ^ bits) for k in range(count)])  23.4 us
    ppermute x5, waiting for transfers between devices, shifted(): lax.ppermute(value, axis, [(k, (k + steps) % count) for k in range(count)])  8.34 us
    ppermute x5, starting transfers between devices, shifted(): lax.ppermute(value, axis, [(k, (k + steps) % count) for k in range(count)])  7.79 us
  transfers between devices with their start and end apart: 40, of which 16 were waited for; matrix products, arithmetic and copies ran while one was open for 0% of the time, Pallas kernels for 16%

profile of v3, /device:TPU:1, one launch (start us, length us, event | category | flops | bytes accessed | tf_op | source)
XLA Modules:
  0.0 110.1 jit_solution(17451778145456407710)
XLA Ops:
  0.6 3.0 %shard_map.145 = (s32[4,8,128]{2,1,0:T(8,128)S(1)}, s32[4,8,128]{2,1,0:T(8,128)S(1)}, s32[4,8,128]{2,1,0:T(8,128)S(1)}, s32[4,8,128]{2,1,0:T(8,128)S(1)}, f32[8,...) custom-call(s32[4,8,128]{2,1,0:T(8,128)} %bitcast.12, ...), custom_call_target="tpu_custom_call" | custom-call | tf_op jit(solution)/shard_map/pallas_call | solution.py:315
  3.7 3.6 %shard_map.146 = (f32[64,256]{1,0:T(8,128)S(1)}, f32[64,256]{1,0:T(8,128)S(1)}, bf16[2,1024,512]{2,1,0:T(8,128)(2,1)S(1)}, bf16[2,1024,256]{2,1,0:T(8,128)(2,1)S(1)}, f32[1024,256]{1,0:T(8,128)S(1)}) custom-call(s32[1]{0:T(128)} %bitcast.refs_0_.spot_ref, s32[1]{0:T(128)} %bitcast.1.refs_1_.core_ref, f32[128,256]{1,0:T(8,128)S(1)} %get-tuple-element.103.refs_2_.refs_5_, ...), custom_call_target="tpu_custom_call" | custom-call | tf_op jit(solution)/shard_map/pallas_call | solution.py:315
  9.0 2.9 %collective-permute-start.4 = (f32[520,256]{1,0:T(8,128)S(1)}, f32[520,256]{1,0:T(8,128)S(1)}, u32[]{:S(2)}, u32[]{:S(2)}) collective-permute-start(f32[520,256]{1,0:T(8,128)S(1)} %shard_map.147), channel_id=1, source_target_pairs={{0,1},{1,2},{2,3},{3,4},{4,5},{5,6},{6,7},{7,0},{8,9},{9,10},{10,1... | collective-permute-start | bytes 1597448 | tf_op jit(solution)/shard_map/ppermute | solution.py:327
  11.9 2.2 %collective-permute-start.3 = (f32[64,256]{1,0:T(8,128)S(1)}, f32[64,256]{1,0:T(8,128)S(1)}, u32[]{:S(2)}, u32[]{:S(2)}) collective-permute-start(f32[64,256]{1,0:T(8,128)S(1)} %add.84), channel_id=1, source_target_pairs={{0,24},{8,16},{16,8},{24,0},{1,25},{9,17},{17,9},{25,1},{2,26},{10... | collective-permute-start | bytes 196616 | tf_op jit(solution)/shard_map/ppermute | solution.py:332
  16.3 1.9 %collective-permute-done.2 = f32[64,256]{1,0:T(8,128)S(1)} collective-permute-done((f32[64,256]{1,0:T(8,128)S(1)}, f32[64,256]{1,0:T(8,128)S(1)}, u32[]{:S(2)}, u32[]{:S(2)}) %collective-permute-start.2) | collective-permute-done | bytes 65568 | tf_op jit(solution)/shard_map/ppermute | solution.py:332
  18.2 2.0 %collective-permute-start.7 = (f32[64,256]{1,0:T(8,128)S(1)}, f32[64,256]{1,0:T(8,128)S(1)}, u32[]{:S(2)}, u32[]{:S(2)}) collective-permute-start(f32[64,256]{1,0:T(8,128)S(1)} %add_add_fusion.5), channel_id=1, source_target_pairs={{0,6},{1,7},{2,4},{3,5},{4,2},{5,3},{6,0},{7,1},{8,14},{9,15},{10,... | collective-permute-start | bytes 196616 | tf_op jit(solution)/shard_map/ppermute | solution.py:332
  21.8 3.0 %shard_map.148 = (f32[1024,256]{1,0:T(8,128)S(1)}, f32[8,128]{1,0:T(8,128)S(1)}, f32[1024,256]{1,0:T(8,128)S(1)}, f32[8,512]{1,0:T(8,128)S(1)}) custom-call(s32[4,8,128]{2,1,0:T(8,128)S(1)} %get-tuple-element.118.esr_ref, s32[4,8,128]{2,1,0:T(8,128)S(1)} %get-tuple-element.119.neg_ref, f32[1024,256]{1,0:T(8,128)S(1)} %get-tuple-element.120.gsr_ref, ...), custom_call_target="tpu_custom_call" | custom-call | tf_op jit(solution)/shard_map/pallas_call | solution.py:315
  24.8 2.5 %collective-permute-done.6 = f32[64,256]{1,0:T(8,128)S(1)} collective-permute-done((f32[64,256]{1,0:T(8,128)S(1)}, f32[64,256]{1,0:T(8,128)S(1)}, u32[]{:S(2)}, u32[]{:S(2)}) %collective-permute-start.6) | collective-permute-done | bytes 65568 | tf_op jit(solution)/shard_map/ppermute | solution.py:332
  29.1 3.9 %shard_map.149 = (f32[64,256]{1,0:T(8,128)S(1)}, f32[64,256]{1,0:T(8,128)S(1)}, bf16[2,1024,512]{2,1,0:T(8,128)(2,1)S(1)}, bf16[2,1024,256]{2,1,0:T(8,128)(2,1)S...) custom-call(s32[1]{0:T(128)} %bitcast.refs_0_.spot_ref, s32[1]{0:T(128)} %bitcast.1.refs_1_.core_ref, ...), custom_call_target="tpu_custom_call" | custom-call | tf_op jit(solution)/shard_map/pallas_call | solution.py:315
  39.4 1.9 %collective-permute-done.11 = f32[64,256]{1,0:T(8,128)S(1)} collective-permute-done((f32[64,256]{1,0:T(8,128)S(1)}, f32[64,256]{1,0:T(8,128)S(1)}, u32[]{:S(2)}, u32[]{:S(2)}) %collective-permute-start.11) | collective-permute-done | bytes 65568 | tf_op jit(solution)/shard_map/ppermute | solution.py:332
  41.4 3.6 %collective-permute-start.16 = (f32[64,256]{1,0:T(8,128)S(1)}, f32[64,256]{1,0:T(8,128)S(1)}, u32[]{:S(2)}, u32[]{:S(2)}) collective-permute-start(f32[64,256]{1,0:T(8,128)S(1)} %add_add_fusion.3), channel_id=1, source_target_pairs={{0,6},{1,7},{2,4},{3,5},{4,2},{5,3},{6,0},{7,1},{8,14},{9,15},{10,... | collective-permute-start | bytes 196616 | tf_op jit(solution)/shard_map/ppermute | solution.py:332
  45.4 3.0 %shard_map.151 = (f32[1024,256]{1,0:T(8,128)S(1)}, f32[8,128]{1,0:T(8,128)S(1)}, f32[1024,256]{1,0:T(8,128)S(1)}, f32[8,512]{1,0:T(8,128)S(1)}) custom-call(s32[4,8,128]{2,1,0:T(8,128)S(1)} %get-tuple-element.118.esr_ref, s32[4,8,128]{2,1,0:T(8,128)S(1)} %get-tuple-element.119.neg_ref, f32[1024,256]{1,0:T(8,128)S(1)} %get-tuple-element.141.gsr_ref, ...), custom_call_target="tpu_custom_call" | custom-call | tf_op jit(solution)/shard_map/pallas_call | solution.py:315
  48.4 2.5 %collective-permute-done.15 = f32[64,256]{1,0:T(8,128)S(1)} collective-permute-done((f32[64,256]{1,0:T(8,128)S(1)}, f32[64,256]{1,0:T(8,128)S(1)}, u32[]{:S(2)}, u32[]{:S(2)}) %collective-permute-start.15) | collective-permute-done | bytes 65568 | tf_op jit(solution)/shard_map/ppermute | solution.py:332
  52.6 3.9 %shard_map.152 = (f32[64,256]{1,0:T(8,128)S(1)}, f32[64,256]{1,0:T(8,128)S(1)}, bf16[2,1024,512]{2,1,0:T(8,128)(2,1)S(1)}, bf16[2,1024,256]{2,1,0:T(8,128)(2,1)S...) custom-call(s32[1]{0:T(128)} %bitcast.refs_0_.spot_ref, s32[1]{0:T(128)} %bitcast.1.refs_1_.core_ref, ...), custom_call_target="tpu_custom_call" | custom-call | tf_op jit(solution)/shard_map/pallas_call | solution.py:315
  62.3 2.2 %collective-permute-done.21 = f32[64,256]{1,0:T(8,128)S(1)} collective-permute-done((f32[64,256]{1,0:T(8,128)S(1)}, f32[64,256]{1,0:T(8,128)S(1)}, u32[]{:S(2)}, u32[]{:S(2)}) %collective-permute-start.21) | collective-permute-done | bytes 65568 | tf_op jit(solution)/shard_map/ppermute | solution.py:332
  66.1 2.7 %collective-permute-start.25 = (f32[64,256]{1,0:T(8,128)S(1)}, f32[64,256]{1,0:T(8,128)S(1)}, u32[]{:S(2)}, u32[]{:S(2)}) collective-permute-start(f32[64,256]{1,0:T(8,128)S(1)} %add_add_fusion.1), channel_id=1, source_target_pairs={{0,6},{1,7},{2,4},{3,5},{4,2},{5,3},{6,0},{7,1},{8,14},{9,15},{10,... | collective-permute-start | bytes 196616 | tf_op jit(solution)/shard_map/ppermute | solution.py:332
  69.7 3.0 %shard_map.154 = (f32[1024,256]{1,0:T(8,128)S(1)}, f32[8,128]{1,0:T(8,128)S(1)}, f32[1024,256]{1,0:T(8,128)S(1)}, f32[8,512]{1,0:T(8,128)S(1)}) custom-call(s32[4,8,128]{2,1,0:T(8,128)S(1)} %get-tuple-element.118.esr_ref, s32[4,8,128]{2,1,0:T(8,128)S(1)} %get-tuple-element.119.neg_ref, f32[1024,256]{1,0:T(8,128)S(1)} %get-tuple-element.163.gsr_ref, ...), custom_call_target="tpu_custom_call" | custom-call | tf_op jit(solution)/shard_map/pallas_call | solution.py:315
  72.7 2.3 %collective-permute-done.24 = f32[64,256]{1,0:T(8,128)S(1)} collective-permute-done((f32[64,256]{1,0:T(8,128)S(1)}, f32[64,256]{1,0:T(8,128)S(1)}, u32[]{:S(2)}, u32[]{:S(2)}) %collective-permute-start.24) | collective-permute-done | bytes 65568 | tf_op jit(solution)/shard_map/ppermute | solution.py:332
  76.6 3.9 %shard_map.155 = (f32[64,256]{1,0:T(8,128)S(1)}, f32[64,256]{1,0:T(8,128)S(1)}, bf16[2,1024,512]{2,1,0:T(8,128)(2,1)S(1)}, bf16[2,1024,256]{2,1,0:T(8,128)(2,1)S...) custom-call(s32[1]{0:T(128)} %bitcast.refs_0_.spot_ref, s32[1]{0:T(128)} %bitcast.1.refs_1_.core_ref, ...), custom_call_target="tpu_custom_call" | custom-call | tf_op jit(solution)/shard_map/pallas_call | solution.py:315
  82.5 2.1 %collective-permute-start.31 = (f32[256,256]{1,0:T(8,128)S(1)}, f32[256,256]{1,0:T(8,128)S(1)}, u32[]{:S(2)}, u32[]{:S(2)}) collective-permute-start(f32[256,256]{1,0:T(8,128)S(1)} %get-tuple-element.188), channel_id=1, source_target_pairs={{0,5},{1,6},{2,7},{3,0},{4,1},{5,2},{6,3},{7,4},{8,13},{9,14},{10,... | collective-permute-start | bytes 786440 | tf_op jit(solution)/shard_map/ppermute | solution.py:327
  87.3 2.7 %shard_map.157 = (f32[1024,256]{1,0:T(8,128)}, f32[8,128]{1,0:T(8,128)}) custom-call(s32[4,8,128]{2,1,0:T(8,128)S(1)} %get-tuple-element.118.esr_ref, s32[4,8,128]{2,1,0:T(8,128)S(1)} %get-tuple-element.119.neg_ref, f32[1024,256]{1,0:T(8,128)S(1)} %get-tuple-element.183.gsr_ref, f32[1024,256]{1,0:T(8,128)S(1)} %get-tuple-element.184.src_ref, ...), custom_call_target="tpu_custom_call" | custom-call | tf_op jit(solution)/shard_map/pallas_call | solution.py:315
  90.0 3.7 %collective-permute-done.31.refs_6_ = f32[256,256]{1,0:T(8,128)S(1)} collective-permute-done((f32[256,256]{1,0:T(8,128)S(1)}, f32[256,256]{1,0:T(8,128)S(1)}, u32[]{:S(2)}, u32[]{:S(2)}) %collective-permute-start.31) | collective-permute-done | bytes 262176 | tf_op jit(solution)/shard_map/ppermute | solution.py:327
  93.7 3.0 %collective-permute-start.34 = (f32[16,256]{1,0:T(8,128)S(1)}, f32[16,256]{1,0:T(8,128)S(1)}, u32[]{:S(2)}, u32[]{:S(2)}) collective-permute-start(f32[16,256]{1,0:T(8,128)S(1)} %slice_add_fusion), channel_id=1, source_target_pairs={{0,6},{1,7},{2,4},{3,5},{4,2},{5,3},{6,0},{7,1},{8,14},{9,15},{10,... | collective-permute-start | bytes 49160 | tf_op jit(solution)/shard_map/ppermute | solution.py:332
  104.2 4.7 %collective-permute-done.39.refs_7_ = f32[264,256]{1,0:T(8,128)S(1)} collective-permute-done((f32[264,256]{1,0:T(8,128)S(1)}, f32[264,256]{1,0:T(8,128)S(1)}, u32[]{:S(2)}, u32[]{:S(2)}) %collective-permute-start.39) | collective-permute-done | bytes 270368 | tf_op jit(solution)/shard_map/ppermute | solution.py:327
  (84 shorter events, 38.8 us)
Async XLA Ops:
  9.0 11.7 %collective-permute-start.4 = (f32[520,256]{1,0:T(8,128)S(1)}, f32[520,256]{1,0:T(8,128)S(1)}, u32[]{:S(2)}, u32[]{:S(2)}) collective-permute-start(f32[520,256]{1,0:T(8,128)S(1)} %shard_map.147), channel_id=1, source_target_pairs={{0,1},{1,2},{2,3},{3,4},{4,5},{5,6},{6,7},{7,0},{8,9},{9,10},{10,1... | collective-permute-start | bytes 1597448 | tf_op jit(solution)/shard_map/ppermute | solution.py:327
  11.9 4.4 %collective-permute-start.3 = (f32[64,256]{1,0:T(8,128)S(1)}, f32[64,256]{1,0:T(8,128)S(1)}, u32[]{:S(2)}, u32[]{:S(2)}) collective-permute-start(f32[64,256]{1,0:T(8,128)S(1)} %add.84), channel_id=1, source_target_pairs={{0,24},{8,16},{16,8},{24,0},{1,25},{9,17},{17,9},{25,1},{2,26},{10... | collective-permute-start | bytes 196616 | tf_op jit(solution)/shard_map/ppermute | solution.py:332
  18.2 6.6 %collective-permute-start.7 = (f32[64,256]{1,0:T(8,128)S(1)}, f32[64,256]{1,0:T(8,128)S(1)}, u32[]{:S(2)}, u32[]{:S(2)}) collective-permute-start(f32[64,256]{1,0:T(8,128)S(1)} %add_add_fusion.5), channel_id=1, source_target_pairs={{0,6},{1,7},{2,4},{3,5},{4,2},{5,3},{6,0},{7,1},{8,14},{9,15},{10,... | collective-permute-start | bytes 196616 | tf_op jit(solution)/shard_map/ppermute | solution.py:332
  20.2 7.1 %collective-permute-start.6 = (f32[64,256]{1,0:T(8,128)S(1)}, f32[64,256]{1,0:T(8,128)S(1)}, u32[]{:S(2)}, u32[]{:S(2)}) collective-permute-start(f32[64,256]{1,0:T(8,128)S(1)} %add_add_fusion.5), channel_id=1, source_target_pairs={{0,4},{1,5},{2,6},{3,7},{4,0},{5,1},{6,2},{7,3},{8,12},{9,13},{10,... | collective-permute-start | bytes 196616 | tf_op jit(solution)/shard_map/ppermute | solution.py:332
  20.8 6.6 %collective-permute-start.5 = (f32[64,256]{1,0:T(8,128)S(1)}, f32[64,256]{1,0:T(8,128)S(1)}, u32[]{:S(2)}, u32[]{:S(2)}) collective-permute-start(f32[64,256]{1,0:T(8,128)S(1)} %add_add_fusion.5), channel_id=1, source_target_pairs={{0,2},{1,3},{2,0},{3,1},{4,6},{5,7},{6,4},{7,5},{8,10},{9,11},{10,... | collective-permute-start | bytes 196616 | tf_op jit(solution)/shard_map/ppermute | solution.py:332
  35.0 10.0 %collective-permute-start.13 = (f32[520,256]{1,0:T(8,128)S(1)}, f32[520,256]{1,0:T(8,128)S(1)}, u32[]{:S(2)}, u32[]{:S(2)}) collective-permute-start(f32[520,256]{1,0:T(8,128)S(1)} %shard_map.150), channel_id=1, source_target_pairs={{0,1},{1,2},{2,3},{3,4},{4,5},{5,6},{6,7},{7,0},{8,9},{9,10},{10,1... | collective-permute-start | bytes 1597448 | tf_op jit(solution)/shard_map/ppermute | solution.py:327
  36.9 4.4 %collective-permute-start.11 = (f32[64,256]{1,0:T(8,128)S(1)}, f32[64,256]{1,0:T(8,128)S(1)}, u32[]{:S(2)}, u32[]{:S(2)}) collective-permute-start(f32[64,256]{1,0:T(8,128)S(1)} %add.91), channel_id=1, source_target_pairs={{0,16},{8,24},{16,0},{24,8},{1,17},{9,25},{17,1},{25,9},{2,18},{10... | collective-permute-start | bytes 196616 | tf_op jit(solution)/shard_map/ppermute | solution.py:332
  41.4 7.0 %collective-permute-start.16 = (f32[64,256]{1,0:T(8,128)S(1)}, f32[64,256]{1,0:T(8,128)S(1)}, u32[]{:S(2)}, u32[]{:S(2)}) collective-permute-start(f32[64,256]{1,0:T(8,128)S(1)} %add_add_fusion.3), channel_id=1, source_target_pairs={{0,6},{1,7},{2,4},{3,5},{4,2},{5,3},{6,0},{7,1},{8,14},{9,15},{10,... | collective-permute-start | bytes 196616 | tf_op jit(solution)/shard_map/ppermute | solution.py:332
  45.0 5.9 %collective-permute-start.15 = (f32[64,256]{1,0:T(8,128)S(1)}, f32[64,256]{1,0:T(8,128)S(1)}, u32[]{:S(2)}, u32[]{:S(2)}) collective-permute-start(f32[64,256]{1,0:T(8,128)S(1)} %add_add_fusion.3), channel_id=1, source_target_pairs={{0,4},{1,5},{2,6},{3,7},{4,0},{5,1},{6,2},{7,3},{8,12},{9,13},{10,... | collective-permute-start | bytes 196616 | tf_op jit(solution)/shard_map/ppermute | solution.py:332
  45.0 5.9 %collective-permute-start.14 = (f32[64,256]{1,0:T(8,128)S(1)}, f32[64,256]{1,0:T(8,128)S(1)}, u32[]{:S(2)}, u32[]{:S(2)}) collective-permute-start(f32[64,256]{1,0:T(8,128)S(1)} %add_add_fusion.3), channel_id=1, source_target_pairs={{0,2},{1,3},{2,0},{3,1},{4,6},{5,7},{6,4},{7,5},{8,10},{9,11},{10,... | collective-permute-start | bytes 196616 | tf_op jit(solution)/shard_map/ppermute | solution.py:332
  58.5 10.3 %collective-permute-start.22 = (f32[520,256]{1,0:T(8,128)S(1)}, f32[520,256]{1,0:T(8,128)S(1)}, u32[]{:S(2)}, u32[]{:S(2)}) collective-permute-start(f32[520,256]{1,0:T(8,128)S(1)} %shard_map.153), channel_id=1, source_target_pairs={{0,1},{1,2},{2,3},{3,4},{4,5},{5,6},{6,7},{7,0},{8,9},{9,10},{10,1... | collective-permute-start | bytes 1597448 | tf_op jit(solution)/shard_map/ppermute | solution.py:327
  59.6 4.9 %collective-permute-start.21 = (f32[64,256]{1,0:T(8,128)S(1)}, f32[64,256]{1,0:T(8,128)S(1)}, u32[]{:S(2)}, u32[]{:S(2)}) collective-permute-start(f32[64,256]{1,0:T(8,128)S(1)} %add.98), channel_id=1, source_target_pairs={{0,24},{8,16},{16,8},{24,0},{1,25},{9,17},{17,9},{25,1},{2,26},{10... | collective-permute-start | bytes 196616 | tf_op jit(solution)/shard_map/ppermute | solution.py:332
  61.2 4.8 %collective-permute-start.20 = (f32[64,256]{1,0:T(8,128)S(1)}, f32[64,256]{1,0:T(8,128)S(1)}, u32[]{:S(2)}, u32[]{:S(2)}) collective-permute-start(f32[64,256]{1,0:T(8,128)S(1)} %add.98), channel_id=1, source_target_pairs={{0,16},{8,24},{16,0},{24,8},{1,17},{9,25},{17,1},{25,9},{2,18},{10... | collective-permute-start | bytes 196616 | tf_op jit(solution)/shard_map/ppermute | solution.py:332
  66.1 6.6 %collective-permute-start.25 = (f32[64,256]{1,0:T(8,128)S(1)}, f32[64,256]{1,0:T(8,128)S(1)}, u32[]{:S(2)}, u32[]{:S(2)}) collective-permute-start(f32[64,256]{1,0:T(8,128)S(1)} %add_add_fusion.1), channel_id=1, source_target_pairs={{0,6},{1,7},{2,4},{3,5},{4,2},{5,3},{6,0},{7,1},{8,14},{9,15},{10,... | collective-permute-start | bytes 196616 | tf_op jit(solution)/shard_map/ppermute | solution.py:332
  68.8 6.2 %collective-permute-start.24 = (f32[64,256]{1,0:T(8,128)S(1)}, f32[64,256]{1,0:T(8,128)S(1)}, u32[]{:S(2)}, u32[]{:S(2)}) collective-permute-start(f32[64,256]{1,0:T(8,128)S(1)} %add_add_fusion.1), channel_id=1, source_target_pairs={{0,4},{1,5},{2,6},{3,7},{4,0},{5,1},{6,2},{7,3},{8,12},{9,13},{10,... | collective-permute-start | bytes 196616 | tf_op jit(solution)/shard_map/ppermute | solution.py:332
  68.8 6.2 %collective-permute-start.23 = (f32[64,256]{1,0:T(8,128)S(1)}, f32[64,256]{1,0:T(8,128)S(1)}, u32[]{:S(2)}, u32[]{:S(2)}) collective-permute-start(f32[64,256]{1,0:T(8,128)S(1)} %add_add_fusion.1), channel_id=1, source_target_pairs={{0,2},{1,3},{2,0},{3,1},{4,6},{5,7},{6,4},{7,5},{8,10},{9,11},{10,... | collective-permute-start | bytes 196616 | tf_op jit(solution)/shard_map/ppermute | solution.py:332
  82.5 11.2 %collective-permute-start.31 = (f32[256,256]{1,0:T(8,128)S(1)}, f32[256,256]{1,0:T(8,128)S(1)}, u32[]{:S(2)}, u32[]{:S(2)}) collective-permute-start(f32[256,256]{1,0:T(8,128)S(1)} %get-tuple-element.188), channel_id=1, source_target_pairs={{0,5},{1,6},{2,7},{3,0},{4,1},{5,2},{6,3},{7,4},{8,13},{9,14},{10,... | collective-permute-start | bytes 786440 | tf_op jit(solution)/shard_map/ppermute | solution.py:327
  84.6 5.4 %collective-permute-start.29 = (f32[16,256]{1,0:T(8,128)S(1)}, f32[16,256]{1,0:T(8,128)S(1)}, u32[]{:S(2)}, u32[]{:S(2)}) collective-permute-start(f32[16,256]{1,0:T(8,128)S(1)} %get-tuple-element.200), channel_id=1, source_target_pairs={{0,16},{8,24},{16,0},{24,8},{1,17},{9,25},{17,1},{25,9},{2,18},{10... | collective-permute-start | bytes 49160 | tf_op jit(solution)/shard_map/ppermute | solution.py:332
  85.7 4.3 %collective-permute-start.30 = (f32[16,256]{1,0:T(8,128)S(1)}, f32[16,256]{1,0:T(8,128)S(1)}, u32[]{:S(2)}, u32[]{:S(2)}) collective-permute-start(f32[16,256]{1,0:T(8,128)S(1)} %get-tuple-element.201), channel_id=1, source_target_pairs={{0,24},{8,16},{16,8},{24,0},{1,25},{9,17},{17,9},{25,1},{2,26},{10... | collective-permute-start | bytes 49160 | tf_op jit(solution)/shard_map/ppermute | solution.py:332
  93.7 5.1 %collective-permute-start.34 = (f32[16,256]{1,0:T(8,128)S(1)}, f32[16,256]{1,0:T(8,128)S(1)}, u32[]{:S(2)}, u32[]{:S(2)}) collective-permute-start(f32[16,256]{1,0:T(8,128)S(1)} %slice_add_fusion), channel_id=1, source_target_pairs={{0,6},{1,7},{2,4},{3,5},{4,2},{5,3},{6,0},{7,1},{8,14},{9,15},{10,... | collective-permute-start | bytes 49160 | tf_op jit(solution)/shard_map/ppermute | solution.py:332
  97.3 11.6 %collective-permute-start.39 = (f32[264,256]{1,0:T(8,128)S(1)}, f32[264,256]{1,0:T(8,128)S(1)}, u32[]{:S(2)}, u32[]{:S(2)}) collective-permute-start(f32[264,256]{1,0:T(8,128)S(1)} %get-tuple-element.195), channel_id=1, source_target_pairs={{0,5},{1,6},{2,7},{3,0},{4,1},{5,2},{6,3},{7,4},{8,13},{9,14},{10,... | collective-permute-start | bytes 811016 | tf_op jit(solution)/shard_map/ppermute | solution.py:327
  101.6 7.3 %collective-permute-start.38 = (f32[32,256]{1,0:T(8,128)S(1)}, f32[32,256]{1,0:T(8,128)S(1)}, u32[]{:S(2)}, u32[]{:S(2)}) collective-permute-start(f32[32,256]{1,0:T(8,128)S(1)} %pad_maximum_fusion.refs_0_), channel_id=1, source_target_pairs={{0,24},{8,16},{16,8},{24,0},{1,25},{9,17},{17,9},{25,1},{2,26},{10... | collective-permute-start | bytes 98312 | tf_op jit(solution)/shard_map/ppermute | solution.py:332
  102.9 6.0 %collective-permute-start.37 = (f32[32,256]{1,0:T(8,128)S(1)}, f32[32,256]{1,0:T(8,128)S(1)}, u32[]{:S(2)}, u32[]{:S(2)}) collective-permute-start(f32[32,256]{1,0:T(8,128)S(1)} %pad_maximum_fusion.refs_0_), channel_id=1, source_target_pairs={{0,16},{8,24},{16,0},{24,8},{1,17},{9,25},{17,1},{25,9},{2,18},{10... | collective-permute-start | bytes 98312 | tf_op jit(solution)/shard_map/ppermute | solution.py:332
  103.3 5.6 %collective-permute-start.36 = (f32[32,256]{1,0:T(8,128)S(1)}, f32[32,256]{1,0:T(8,128)S(1)}, u32[]{:S(2)}, u32[]{:S(2)}) collective-permute-start(f32[32,256]{1,0:T(8,128)S(1)} %pad_maximum_fusion.refs_0_), channel_id=1, source_target_pairs={{0,8},{8,0},{16,24},{24,16},{1,9},{9,1},{17,25},{25,17},{2,10},{10... | collective-permute-start | bytes 98312 | tf_op jit(solution)/shard_map/ppermute | solution.py:332
  (16 other events, 43.9 us)

commit v4 on v3

--- a/solution.py
+++ b/solution.py
@@ -14,6 +14,7 @@
 BF16 = jnp.bfloat16
 LANES = 128
 CHUNK = 256
+QUERIES = 512
 
 
 def halves(value):
@@ -61,20 +62,27 @@
         out_ref[c * CHUNK : (c + 1) * CHUNK, :] = dot(jnp.concatenate([hot, hot], axis=1), stack)
 
 
-def write_counts(neg_ref, step, out_ref):
+def prepare(step, eds_ref, erl_ref, neg_ref, cnt_ref, hit_ref, hot_ref, hot_t_ref):
     blocks, negs = neg_ref.shape[1:]
-    rows = out_ref.shape[1]
+    rows = cnt_ref.shape[1]
+    nrel = hot_t_ref.shape[0]
     cols = columns(neg_ref[step])
-    lane = lax.broadcasted_iota(jnp.int32, (negs, rows), 1)
+    dst_cols = columns(eds_ref[step])
+    lane = lax.broadcasted_iota(jnp.int32, (LANES, rows), 1)
     for b in range(blocks):
-        hits = jnp.where(cols[:, b : b + 1] == lane, 0.5 / negs, 0.0)
-        out_ref[b : b + 1, :] = jnp.sum(hits, axis=0, keepdims=True)
+        found = jnp.where(cols[:, b : b + 1] == lane, 0.5 / negs, 0.0)
+        count = jnp.sum(found, axis=0, keepdims=True)
+        cnt_ref[b : b + 1, :] = 2.0 * count
+        own = jnp.where(dst_cols[:, b : b + 1] == lane, 0.5, 0.0)
+        hit_ref[b * LANES : (b + 1) * LANES, :] = own + count
+    hot_ref[...] = hot_columns(columns(erl_ref[step]), 0, blocks, nrel)
+    hot_t_ref[...] = hot_rows(erl_ref[step], 0, blocks, 0, nrel)
 
 
 def first_kernel(
     esr_hbm, eds_hbm, erl_hbm, neg_hbm, sac_hbm, dac_hbm, rac_hbm, rel_hbm, src_hbm, dst_hbm,
     esr_ref, eds_ref, erl_ref, neg_ref, sac_ref, rac_ref, rel_ref, src_ref, dst_ref,
-    next_ref, cnt_ref, stack_ref, src_sem, sem,
+    next_ref, cnt_ref, hit_ref, hot_ref, hot_t_ref, stack_ref, src_sem, sem,
 ):
     rows = src_ref.shape[0]
     drows, width = dst_hbm.shape
@@ -84,17 +92,17 @@
             [
                 (neg_hbm, neg_ref),
                 (esr_hbm, esr_ref),
+                (eds_hbm, eds_ref),
+                (erl_hbm, erl_ref),
                 (dac_hbm, dst_ref.at[pl.ds(drows, dac_hbm.shape[0]), pl.ds(0, LANES)]),
                 (dst_hbm, dst_ref.at[pl.ds(0, drows)]),
-                (eds_hbm, eds_ref),
-                (erl_hbm, erl_ref),
                 (sac_hbm, sac_ref),
                 (rac_hbm, rac_ref),
                 (rel_hbm, rel_ref),
             ]
         )
     ]
-    for load in small[:2]:
+    for load in small[:4]:
         load.start()
     chunks = rows // CHUNK
     loads = [
@@ -106,18 +114,18 @@
     for load in loads:
         load.start()
     dst_ref[drows : drows + 8, :] = jnp.zeros((8, width), F32)
-    for load in small[2:]:
+    for load in small[4:]:
         load.start()
-    small[0].wait()
-    write_counts(neg_ref, 0, cnt_ref)
-    small[1].wait()
+    for load in small[:4]:
+        load.wait()
+    prepare(0, eds_ref, erl_ref, neg_ref, cnt_ref, hit_ref, hot_ref, hot_t_ref)
     for m in range(chunks):
         loads[m].wait()
         high, low = halves(src_ref[m * CHUNK : (m + 1) * CHUNK, :])
         stack_ref[m * CHUNK : (m + 1) * CHUNK, :] = high
         stack_ref[rows + m * CHUNK : rows + (m + 1) * CHUNK, :] = low
     gather_rows(columns(esr_ref[0]), stack_ref[...], next_ref, next_ref.shape[0], rows)
-    for load in small[2:]:
+    for load in small[4:]:
         load.wait()
 
 
@@ -141,8 +149,8 @@
     else:
         core_ref = refs[0]
         refs = refs[1:]
-    rel_ref, src_ref, dst_ref, eds_ref, erl_ref, cnt_ref = refs[:6]
-    refs = refs[6:]
+    rel_ref, src_ref, dst_ref, cnt_ref, hit_ref, hot_ref, hot_t_ref = refs[:7]
+    refs = refs[7:]
     keep_ref, send_ref, wgt_ref, qry_ref, gsr_ref = refs[:5]
     refs = refs[5:]
     if updated:
@@ -155,45 +163,58 @@
     edges = src_ref.shape[0]
     rows = cnt_ref.shape[1]
     nrel = rel.shape[0]
-    blocks = CHUNK // LANES
+    blocks = QUERIES // LANES
     rel_stack = jnp.concatenate(halves(rel), axis=0)
     dst_high, dst_low = halves(dst_ref[0:rows, :])
-    dst_wide = 0.5 * jnp.concatenate([dst_high, dst_low, dst_high], axis=1)
-    dst_tall = jnp.concatenate([dst_high, dst_low, dst_high], axis=0)
-    rel_cols = columns(erl_ref[step])
-    dst_cols = columns(eds_ref[step])
-    lane = lax.broadcasted_iota(jnp.int32, (LANES, rows), 1)
+    half_high, half_low = 0.5 * dst_high, 0.5 * dst_low
     counts = cnt_ref[...]
-    grad = None
-    for c in range(edges // CHUNK):
-        at = slice(c * CHUNK, (c + 1) * CHUNK)
-        hot = hot_columns(rel_cols, c * blocks, blocks, nrel)
+
+    def ask(c):
+        at = slice(c * QUERIES, (c + 1) * QUERIES)
+        hot = hot_ref[at, :]
         rel_rows = dot(jnp.concatenate([hot, hot], axis=1), rel_stack)
-        src_rows = src_ref[at, :]
-        query = src_rows * rel_rows
+        query = src_ref[at, :] * rel_rows
         q_high, q_low = halves(query)
         qry_ref[0, at, :] = q_high
         qry_ref[1, at, :] = q_low
-        scores = dot(jnp.concatenate([q_high, q_high, q_low], axis=1), dst_wide, 1, 1)
-        slope = jnp.tanh(scores)
+        scores = (
+            dot(q_high, half_high, 1, 1) + dot(q_high, half_low, 1, 1) + dot(q_low, half_high, 1, 1)
+        )
+        return rel_rows, scores
+
+    def answer(c, rel_rows, scores):
+        at = slice(c * QUERIES, (c + 1) * QUERIES)
+        slope = jnp.tanh(scores) - 1.0
         parts = []
         for b in range(blocks):
             block = c * blocks + b
+            rows_at = slice(block * LANES, (block + 1) * LANES)
             part = slope[b * LANES : (b + 1) * LANES, :]
-            hit = jnp.where(dst_cols[:, block : block + 1] == lane, 0.5, 0.0)
-            count = counts[block : block + 1, :]
-            parts.append(part * (count + hit) + (count - hit))
+            parts.append(hit_ref[rows_at, :] * part + counts[block : block + 1, :])
         weight = jnp.concatenate(parts, axis=0)
         w_high, w_low = halves(weight)
         wgt_ref[0, at, :] = w_high
         wgt_ref[1, at, :] = w_low
-        grad_query = dot(jnp.concatenate([w_high, w_high, w_low], axis=1), dst_tall)
+        grad_query = dot(w_high, dst_high) + dot(w_high, dst_low) + dot(w_low, dst_high)
         gsr_ref[at, :] = grad_query * rel_rows
-        hot_t = hot_rows(erl_ref[step], c * blocks, blocks, 0, nrel)
-        part = dot(
+        return grad_query
+
+    def share(c, grad_query):
+        at = slice(c * QUERIES, (c + 1) * QUERIES)
+        hot_t = hot_t_ref[:, at]
+        return dot(
             jnp.concatenate([hot_t, hot_t], axis=1),
-            jnp.concatenate(halves(grad_query * src_rows), axis=0),
-        )
+            jnp.concatenate(halves(grad_query * src_ref[at, :]), axis=0),
+        )
+
+    count = edges // QUERIES
+    grad = None
+    asked = ask(0)
+    for c in range(count):
+        ready = asked
+        if c + 1 < count:
+            asked = ask(c + 1)
+        part = share(c, answer(c, *ready))
         grad = part if grad is None else grad + part
     first = core_ref[0] == 0
     half = nrel // 2
@@ -235,11 +256,11 @@
     )
 
 
-def src_kernel(step, last, esr_ref, neg_ref, gsr_ref, src_ref, acc_ref, *refs):
+def src_kernel(step, last, esr_ref, eds_ref, erl_ref, neg_ref, gsr_ref, src_ref, acc_ref, *refs):
     if last:
         src_out_ref, acc_out_ref = refs
     else:
-        src_out_ref, acc_out_ref, next_ref, cnt_ref, stack_ref = refs
+        src_out_ref, acc_out_ref, next_ref, *prep, stack_ref = refs
     rows = src_ref.shape[0]
     edges = gsr_ref.shape[0]
     gsr = jnp.concatenate(halves(gsr_ref[...]), axis=0)
@@ -268,7 +289,7 @@
     acc_out_ref[...] = jnp.transpose(jnp.concatenate(totals, axis=1))
     if not last:
         gather_rows(columns(esr_ref[step + 1]), stack_ref[...], next_ref, edges, rows)
-        write_counts(neg_ref, step + 1, cnt_ref)
+        prepare(step + 1, eds_ref, erl_ref, neg_ref, *prep)
 
 
 def final_kernel(core_ref, spot_ref, *refs):
@@ -364,11 +385,17 @@
     dblocks = drows // LANES
     stack = pltpu.VMEM((2 * srows, width), BF16)
     ids = (esr.shape, jnp.int32)
+    prep_shapes = [
+        ((eblocks, drows), F32),
+        ((edges, drows), F32),
+        ((edges, nrel), BF16),
+        ((nrel, edges), BF16),
+    ]
     firsts = [
         esr, eds, erl, neg, sacc, dst_acc.reshape(dblocks, LANES), rel_acc.reshape(1, nrel),
         rel_emb, src_emb, dst_emb,
     ]
-    esr, eds, erl, neg, sacc, racc, rel, src, dst, rows, counts = call(
+    esr, eds, erl, neg, sacc, racc, rel, src, dst, rows, *prep = call(
         first_kernel,
         [
             ids, ids, ids, ids,
@@ -378,7 +405,7 @@
             ((srows, width), F32),
             ((drows + 8, width), F32),
             ((edges, width), F32),
-            ((eblocks, drows), F32),
+            *prep_shapes,
         ],
         firsts,
         [stack, pltpu.SemaphoreType.DMA((srows // CHUNK,)), pltpu.SemaphoreType.DMA((len(firsts),))],
@@ -395,9 +422,9 @@
             ((edges, width), F32),
         ]
         if step == 0:
-            args = [spot, core, rel, rows, dst, eds, erl, counts]
+            args = [spot, core, rel, rows, dst, *prep]
         else:
-            args = [spot, core, half, peer, racc, rel, rows, dst, eds, erl, counts]
+            args = [spot, core, half, peer, racc, rel, rows, dst, *prep]
             outs += [((nrel, width), F32), ((1, nrel), F32)]
         res = call(functools.partial(query_kernel, step, step > 0, nsrc if last else 1), outs, args, smem=2)
         keep, send, wgt, qry, gsr = res[:5]
@@ -416,7 +443,7 @@
                 crossed(half[k * size : (k + 1) * size], "src", k) for k in range(1, nsrc)
             )
             src, sacc = call(
-                functools.partial(src_kernel, step, last), outs, [esr, neg, gsr, src, sacc]
+                functools.partial(src_kernel, step, last), outs, [esr, eds, erl, neg, gsr, src, sacc]
             )
             half, src, sacc, dst[0] = lax.optimization_barrier((half, src, sacc, dst[0]))
             half = exchanged(half, "dst", 2)
@@ -425,12 +452,12 @@
         else:
             half = exchanged(half, "src", 1)
             half, gsr = lax.optimization_barrier((half, gsr))
-            outs += [((edges, width), F32), ((eblocks, drows), F32)]
+            outs += [((edges, width), F32), *prep_shapes]
             res = call(
-                functools.partial(src_kernel, step, last), outs, [esr, neg, gsr, src, sacc], [stack]
+                functools.partial(src_kernel, step, last), outs, [esr, eds, erl, neg, gsr, src, sacc], [stack]
             )
             half, (dst,) = exchanged(half, "dst", 2, dst)
-            half, src, sacc, rows, counts = lax.optimization_barrier((half, *res))
+            half, src, sacc, rows, *prep = lax.optimization_barrier((half, *res))
             peer = crossed(half, "dst", 1)
     rel, racc, dst, dacc = call(
         final_kernel,

time: 110 us -> 106 us (0.964)
  Pallas kernels: 37.3 us -> 34.7 us
  waiting for transfers between devices: 31.8 us -> 30.4 us
    pallas_call x14, Pallas kernels: 37.3 us -> 34.7 us  [call(): pl.pallas_call(body, out_shape=tuple((jax.ShapeDtypeStruct(s, d) for s, d...]
    ppermute x35, waiting for transfers between devices: 23.4 us -> 22.1 us  [crossed(): return lax.ppermute(value, axis, [(k, k ^ bits) for k in range(count)])]
  transfers between devices with their start and end apart: 40 -> 40, of which waited for: 16 -> 16; matrix products, arithmetic and copies ran while one was open for 0% -> 0% of each run, Pallas kernels for 16% -> 18%
where the time goes in v4:
time: 106 us
  starting transfers between devices  39.8 us (38%)
  Pallas kernels  34.7 us (33%)
  waiting for transfers between devices  30.4 us (29%)
    pallas_call x14, Pallas kernels, call(): pl.pallas_call(body, out_shape=tuple((jax.ShapeDtypeStruct(s, d) for s, d...  34.7 us
    ppermute x35, starting transfers between devices, crossed(): return lax.ppermute(value, axis, [(k, k ^ bits) for k in range(count)])  32 us
    ppermute x35, waiting for transfers between devices, crossed(): return lax.ppermute(value, axis, [(k, k ^ bits) for k in range(count)])  22.1 us
    ppermute x5, waiting for transfers between devices, shifted(): lax.ppermute(value, axis, [(k, (k + steps) % count) for k in range(count)])  8.28 us
    ppermute x5, starting transfers between devices, shifted(): lax.ppermute(value, axis, [(k, (k + steps) % count) for k in range(count)])  7.78 us
  transfers between devices with their start and end apart: 40, of which 16 were waited for; matrix products, arithmetic and copies ran while one was open for 0% of the time, Pallas kernels for 18%

profile of v4, /device:TPU:1, one launch (start us, length us, event | category | flops | bytes accessed | tf_op | source)
XLA Modules:
  0.0 106.1 jit_solution(13283727137551156095)
XLA Ops:
  0.6 3.5 %shard_map.145 = (s32[4,8,128]{2,1,0:T(8,128)S(1)}, s32[4,8,128]{2,1,0:T(8,128)S(1)}, s32[4,8,128]{2,1,0:T(8,128)S(1)}, s32[4,8,128]{2,1,0:T(8,128)S(1)}, f32[8,...) custom-call(s32[4,8,128]{2,1,0:T(8,128)} %bitcast.12, ...), custom_call_target="tpu_custom_call" | custom-call | tf_op jit(solution)/shard_map/pallas_call | solution.py:336
  4.2 2.6 %shard_map.146 = (f32[64,256]{1,0:T(8,128)S(1)}, f32[64,256]{1,0:T(8,128)S(1)}, bf16[2,1024,512]{2,1,0:T(8,128)(2,1)S(1)}, bf16[2,1024,256]{2,1,0:T(8,128)(2,1)S(1)}, f32[1024,256]{1,0:T(8,128)S(1)}) custom-call(s32[1]{0:T(128)} %bitcast.refs_0_.spot_ref, s32[1]{0:T(128)} %bitcast.1.refs_1_.core_ref, f32[128,256]{1,0:T(8,128)S(1)} %get-tuple-element.124.refs_2_.refs_5_, ...), custom_call_target="tpu_custom_call" | custom-call | tf_op jit(solution)/shard_map/pallas_call | solution.py:336
  8.4 2.9 %collective-permute-start.4 = (f32[520,256]{1,0:T(8,128)S(1)}, f32[520,256]{1,0:T(8,128)S(1)}, u32[]{:S(2)}, u32[]{:S(2)}) collective-permute-start(f32[520,256]{1,0:T(8,128)S(1)} %shard_map.147), channel_id=1, source_target_pairs={{0,1},{1,2},{2,3},{3,4},{4,5},{5,6},{6,7},{7,0},{8,9},{9,10},{10,1... | collective-permute-start | bytes 1597448 | tf_op jit(solution)/shard_map/ppermute | solution.py:348
  11.3 2.2 %collective-permute-start.3 = (f32[64,256]{1,0:T(8,128)S(1)}, f32[64,256]{1,0:T(8,128)S(1)}, u32[]{:S(2)}, u32[]{:S(2)}) collective-permute-start(f32[64,256]{1,0:T(8,128)S(1)} %add.84), channel_id=1, source_target_pairs={{0,24},{8,16},{16,8},{24,0},{1,25},{9,17},{17,9},{25,1},{2,26},{10... | collective-permute-start | bytes 196616 | tf_op jit(solution)/shard_map/ppermute | solution.py:353
  15.7 1.9 %collective-permute-done.2 = f32[64,256]{1,0:T(8,128)S(1)} collective-permute-done((f32[64,256]{1,0:T(8,128)S(1)}, f32[64,256]{1,0:T(8,128)S(1)}, u32[]{:S(2)}, u32[]{:S(2)}) %collective-permute-start.2) | collective-permute-done | bytes 65568 | tf_op jit(solution)/shard_map/ppermute | solution.py:353
  17.6 2.0 %collective-permute-start.7 = (f32[64,256]{1,0:T(8,128)S(1)}, f32[64,256]{1,0:T(8,128)S(1)}, u32[]{:S(2)}, u32[]{:S(2)}) collective-permute-start(f32[64,256]{1,0:T(8,128)S(1)} %add_add_fusion.5), channel_id=1, source_target_pairs={{0,6},{1,7},{2,4},{3,5},{4,2},{5,3},{6,0},{7,1},{8,14},{9,15},{10,... | collective-permute-start | bytes 196616 | tf_op jit(solution)/shard_map/ppermute | solution.py:353
  21.3 3.4 %shard_map.148 = (f32[1024,256]{1,0:T(8,128)S(1)}, f32[8,128]{1,0:T(8,128)S(1)}, f32[1024,256]{1,0:T(8,128)S(1)}, f32[8,512]{1,0:T(8,128)S(1)}, f32[1024,512]{1,...) custom-call(s32[4,8,128]{2,1,0:T(8,128)S(1)} %get-tuple-element.140.esr_ref, ...), custom_call_target="tpu_custom_call" | custom-call | tf_op jit(solution)/shard_map/pallas_call | solution.py:336
  24.7 2.1 %collective-permute-done.6 = f32[64,256]{1,0:T(8,128)S(1)} collective-permute-done((f32[64,256]{1,0:T(8,128)S(1)}, f32[64,256]{1,0:T(8,128)S(1)}, u32[]{:S(2)}, u32[]{:S(2)}) %collective-permute-start.6) | collective-permute-done | bytes 65568 | tf_op jit(solution)/shard_map/ppermute | solution.py:353
  28.5 2.8 %shard_map.149 = (f32[64,256]{1,0:T(8,128)S(1)}, f32[64,256]{1,0:T(8,128)S(1)}, bf16[2,1024,512]{2,1,0:T(8,128)(2,1)S(1)}, bf16[2,1024,256]{2,1,0:T(8,128)(2,1)S...) custom-call(s32[1]{0:T(128)} %bitcast.refs_0_.spot_ref, s32[1]{0:T(128)} %bitcast.1.refs_1_.core_ref, ...), custom_call_target="tpu_custom_call" | custom-call | tf_op jit(solution)/shard_map/pallas_call | solution.py:336
  37.7 1.9 %collective-permute-done.11 = f32[64,256]{1,0:T(8,128)S(1)} collective-permute-done((f32[64,256]{1,0:T(8,128)S(1)}, f32[64,256]{1,0:T(8,128)S(1)}, u32[]{:S(2)}, u32[]{:S(2)}) %collective-permute-start.11) | collective-permute-done | bytes 65568 | tf_op jit(solution)/shard_map/ppermute | solution.py:353
  39.6 3.6 %collective-permute-start.16 = (f32[64,256]{1,0:T(8,128)S(1)}, f32[64,256]{1,0:T(8,128)S(1)}, u32[]{:S(2)}, u32[]{:S(2)}) collective-permute-start(f32[64,256]{1,0:T(8,128)S(1)} %add_add_fusion.3), channel_id=1, source_target_pairs={{0,6},{1,7},{2,4},{3,5},{4,2},{5,3},{6,0},{7,1},{8,14},{9,15},{10,... | collective-permute-start | bytes 196616 | tf_op jit(solution)/shard_map/ppermute | solution.py:353
  43.6 3.4 %shard_map.151 = (f32[1024,256]{1,0:T(8,128)S(1)}, f32[8,128]{1,0:T(8,128)S(1)}, f32[1024,256]{1,0:T(8,128)S(1)}, f32[8,512]{1,0:T(8,128)S(1)}, f32[1024,512]{1,...) custom-call(s32[4,8,128]{2,1,0:T(8,128)S(1)} %get-tuple-element.140.esr_ref, ...), custom_call_target="tpu_custom_call" | custom-call | tf_op jit(solution)/shard_map/pallas_call | solution.py:336
  47.1 2.1 %collective-permute-done.15 = f32[64,256]{1,0:T(8,128)S(1)} collective-permute-done((f32[64,256]{1,0:T(8,128)S(1)}, f32[64,256]{1,0:T(8,128)S(1)}, u32[]{:S(2)}, u32[]{:S(2)}) %collective-permute-start.15) | collective-permute-done | bytes 65568 | tf_op jit(solution)/shard_map/ppermute | solution.py:353
  50.9 2.8 %shard_map.152 = (f32[64,256]{1,0:T(8,128)S(1)}, f32[64,256]{1,0:T(8,128)S(1)}, bf16[2,1024,512]{2,1,0:T(8,128)(2,1)S(1)}, bf16[2,1024,256]{2,1,0:T(8,128)(2,1)S...) custom-call(s32[1]{0:T(128)} %bitcast.refs_0_.spot_ref, s32[1]{0:T(128)} %bitcast.1.refs_1_.core_ref, ...), custom_call_target="tpu_custom_call" | custom-call | tf_op jit(solution)/shard_map/pallas_call | solution.py:336
  59.5 2.2 %collective-permute-done.21 = f32[64,256]{1,0:T(8,128)S(1)} collective-permute-done((f32[64,256]{1,0:T(8,128)S(1)}, f32[64,256]{1,0:T(8,128)S(1)}, u32[]{:S(2)}, u32[]{:S(2)}) %collective-permute-start.21) | collective-permute-done | bytes 65568 | tf_op jit(solution)/shard_map/ppermute | solution.py:353
  63.2 2.7 %collective-permute-start.25 = (f32[64,256]{1,0:T(8,128)S(1)}, f32[64,256]{1,0:T(8,128)S(1)}, u32[]{:S(2)}, u32[]{:S(2)}) collective-permute-start(f32[64,256]{1,0:T(8,128)S(1)} %add_add_fusion.1), channel_id=1, source_target_pairs={{0,6},{1,7},{2,4},{3,5},{4,2},{5,3},{6,0},{7,1},{8,14},{9,15},{10,... | collective-permute-start | bytes 196616 | tf_op jit(solution)/shard_map/ppermute | solution.py:353
  66.8 3.4 %shard_map.154 = (f32[1024,256]{1,0:T(8,128)S(1)}, f32[8,128]{1,0:T(8,128)S(1)}, f32[1024,256]{1,0:T(8,128)S(1)}, f32[8,512]{1,0:T(8,128)S(1)}, f32[1024,512]{1,...) custom-call(s32[4,8,128]{2,1,0:T(8,128)S(1)} %get-tuple-element.140.esr_ref, ...), custom_call_target="tpu_custom_call" | custom-call | tf_op jit(solution)/shard_map/pallas_call | solution.py:336
  70.3 1.9 %collective-permute-done.24 = f32[64,256]{1,0:T(8,128)S(1)} collective-permute-done((f32[64,256]{1,0:T(8,128)S(1)}, f32[64,256]{1,0:T(8,128)S(1)}, u32[]{:S(2)}, u32[]{:S(2)}) %collective-permute-start.24) | collective-permute-done | bytes 65568 | tf_op jit(solution)/shard_map/ppermute | solution.py:353
  73.7 2.7 %shard_map.155 = (f32[64,256]{1,0:T(8,128)S(1)}, f32[64,256]{1,0:T(8,128)S(1)}, bf16[2,1024,512]{2,1,0:T(8,128)(2,1)S(1)}, bf16[2,1024,256]{2,1,0:T(8,128)(2,1)S...) custom-call(s32[1]{0:T(128)} %bitcast.refs_0_.spot_ref, s32[1]{0:T(128)} %bitcast.1.refs_1_.core_ref, ...), custom_call_target="tpu_custom_call" | custom-call | tf_op jit(solution)/shard_map/pallas_call | solution.py:336
  78.5 2.1 %collective-permute-start.31 = (f32[256,256]{1,0:T(8,128)S(1)}, f32[256,256]{1,0:T(8,128)S(1)}, u32[]{:S(2)}, u32[]{:S(2)}) collective-permute-start(f32[256,256]{1,0:T(8,128)S(1)} %get-tuple-element.230), channel_id=1, source_target_pairs={{0,5},{1,6},{2,7},{3,0},{4,1},{5,2},{6,3},{7,4},{8,13},{9,14},{10,... | collective-permute-start | bytes 786440 | tf_op jit(solution)/shard_map/ppermute | solution.py:348
  83.3 2.7 %shard_map.157 = (f32[1024,256]{1,0:T(8,128)}, f32[8,128]{1,0:T(8,128)}) custom-call(s32[4,8,128]{2,1,0:T(8,128)S(1)} %get-tuple-element.140.esr_ref, s32[4,8,128]{2,1,0:T(8,128)S(1)} %get-tuple-element.141.eds_ref, s32[4,8,128]{2,1,0:T(8,128)S(1)} %get-tuple-element.142.erl_ref, s32[4,8,128]{2,1,0:T(8,128)S(1)} %get-tuple-element.143.neg_ref, ...), custom_call_target="tpu_custom_call" | custom-call | tf_op jit(solution)/shard_map/pallas_call | solution.py:336
  86.1 3.6 %collective-permute-done.31.refs_6_ = f32[256,256]{1,0:T(8,128)S(1)} collective-permute-done((f32[256,256]{1,0:T(8,128)S(1)}, f32[256,256]{1,0:T(8,128)S(1)}, u32[]{:S(2)}, u32[]{:S(2)}) %collective-permute-start.31) | collective-permute-done | bytes 262176 | tf_op jit(solution)/shard_map/ppermute | solution.py:348
  89.7 3.0 %collective-permute-start.34 = (f32[16,256]{1,0:T(8,128)S(1)}, f32[16,256]{1,0:T(8,128)S(1)}, u32[]{:S(2)}, u32[]{:S(2)}) collective-permute-start(f32[16,256]{1,0:T(8,128)S(1)} %slice_add_fusion), channel_id=1, source_target_pairs={{0,6},{1,7},{2,4},{3,5},{4,2},{5,3},{6,0},{7,1},{8,14},{9,15},{10,... | collective-permute-start | bytes 49160 | tf_op jit(solution)/shard_map/ppermute | solution.py:353
  100.2 4.7 %collective-permute-done.39.refs_7_ = f32[264,256]{1,0:T(8,128)S(1)} collective-permute-done((f32[264,256]{1,0:T(8,128)S(1)}, f32[264,256]{1,0:T(8,128)S(1)}, u32[]{:S(2)}, u32[]{:S(2)}) %collective-permute-start.39) | collective-permute-done | bytes 270368 | tf_op jit(solution)/shard_map/ppermute | solution.py:348
  (84 shorter events, 38.9 us)
Async XLA Ops:
  8.4 11.7 %collective-permute-start.4 = (f32[520,256]{1,0:T(8,128)S(1)}, f32[520,256]{1,0:T(8,128)S(1)}, u32[]{:S(2)}, u32[]{:S(2)}) collective-permute-start(f32[520,256]{1,0:T(8,128)S(1)} %shard_map.147), channel_id=1, source_target_pairs={{0,1},{1,2},{2,3},{3,4},{4,5},{5,6},{6,7},{7,0},{8,9},{9,10},{10,1... | collective-permute-start | bytes 1597448 | tf_op jit(solution)/shard_map/ppermute | solution.py:348
  11.3 4.4 %collective-permute-start.3 = (f32[64,256]{1,0:T(8,128)S(1)}, f32[64,256]{1,0:T(8,128)S(1)}, u32[]{:S(2)}, u32[]{:S(2)}) collective-permute-start(f32[64,256]{1,0:T(8,128)S(1)} %add.84), channel_id=1, source_target_pairs={{0,24},{8,16},{16,8},{24,0},{1,25},{9,17},{17,9},{25,1},{2,26},{10... | collective-permute-start | bytes 196616 | tf_op jit(solution)/shard_map/ppermute | solution.py:353
  17.6 7.0 %collective-permute-start.7 = (f32[64,256]{1,0:T(8,128)S(1)}, f32[64,256]{1,0:T(8,128)S(1)}, u32[]{:S(2)}, u32[]{:S(2)}) collective-permute-start(f32[64,256]{1,0:T(8,128)S(1)} %add_add_fusion.5), channel_id=1, source_target_pairs={{0,6},{1,7},{2,4},{3,5},{4,2},{5,3},{6,0},{7,1},{8,14},{9,15},{10,... | collective-permute-start | bytes 196616 | tf_op jit(solution)/shard_map/ppermute | solution.py:353
  19.6 7.1 %collective-permute-start.6 = (f32[64,256]{1,0:T(8,128)S(1)}, f32[64,256]{1,0:T(8,128)S(1)}, u32[]{:S(2)}, u32[]{:S(2)}) collective-permute-start(f32[64,256]{1,0:T(8,128)S(1)} %add_add_fusion.5), channel_id=1, source_target_pairs={{0,4},{1,5},{2,6},{3,7},{4,0},{5,1},{6,2},{7,3},{8,12},{9,13},{10,... | collective-permute-start | bytes 196616 | tf_op jit(solution)/shard_map/ppermute | solution.py:353
  20.2 6.6 %collective-permute-start.5 = (f32[64,256]{1,0:T(8,128)S(1)}, f32[64,256]{1,0:T(8,128)S(1)}, u32[]{:S(2)}, u32[]{:S(2)}) collective-permute-start(f32[64,256]{1,0:T(8,128)S(1)} %add_add_fusion.5), channel_id=1, source_target_pairs={{0,2},{1,3},{2,0},{3,1},{4,6},{5,7},{6,4},{7,5},{8,10},{9,11},{10,... | collective-permute-start | bytes 196616 | tf_op jit(solution)/shard_map/ppermute | solution.py:353
  33.3 10.0 %collective-permute-start.13 = (f32[520,256]{1,0:T(8,128)S(1)}, f32[520,256]{1,0:T(8,128)S(1)}, u32[]{:S(2)}, u32[]{:S(2)}) collective-permute-start(f32[520,256]{1,0:T(8,128)S(1)} %shard_map.150), channel_id=1, source_target_pairs={{0,1},{1,2},{2,3},{3,4},{4,5},{5,6},{6,7},{7,0},{8,9},{9,10},{10,1... | collective-permute-start | bytes 1597448 | tf_op jit(solution)/shard_map/ppermute | solution.py:348
  35.1 4.4 %collective-permute-start.11 = (f32[64,256]{1,0:T(8,128)S(1)}, f32[64,256]{1,0:T(8,128)S(1)}, u32[]{:S(2)}, u32[]{:S(2)}) collective-permute-start(f32[64,256]{1,0:T(8,128)S(1)} %add.91), channel_id=1, source_target_pairs={{0,16},{8,24},{16,0},{24,8},{1,17},{9,25},{17,1},{25,9},{2,18},{10... | collective-permute-start | bytes 196616 | tf_op jit(solution)/shard_map/ppermute | solution.py:353
  39.6 7.4 %collective-permute-start.16 = (f32[64,256]{1,0:T(8,128)S(1)}, f32[64,256]{1,0:T(8,128)S(1)}, u32[]{:S(2)}, u32[]{:S(2)}) collective-permute-start(f32[64,256]{1,0:T(8,128)S(1)} %add_add_fusion.3), channel_id=1, source_target_pairs={{0,6},{1,7},{2,4},{3,5},{4,2},{5,3},{6,0},{7,1},{8,14},{9,15},{10,... | collective-permute-start | bytes 196616 | tf_op jit(solution)/shard_map/ppermute | solution.py:353
  43.3 5.9 %collective-permute-start.15 = (f32[64,256]{1,0:T(8,128)S(1)}, f32[64,256]{1,0:T(8,128)S(1)}, u32[]{:S(2)}, u32[]{:S(2)}) collective-permute-start(f32[64,256]{1,0:T(8,128)S(1)} %add_add_fusion.3), channel_id=1, source_target_pairs={{0,4},{1,5},{2,6},{3,7},{4,0},{5,1},{6,2},{7,3},{8,12},{9,13},{10,... | collective-permute-start | bytes 196616 | tf_op jit(solution)/shard_map/ppermute | solution.py:353
  43.3 5.9 %collective-permute-start.14 = (f32[64,256]{1,0:T(8,128)S(1)}, f32[64,256]{1,0:T(8,128)S(1)}, u32[]{:S(2)}, u32[]{:S(2)}) collective-permute-start(f32[64,256]{1,0:T(8,128)S(1)} %add_add_fusion.3), channel_id=1, source_target_pairs={{0,2},{1,3},{2,0},{3,1},{4,6},{5,7},{6,4},{7,5},{8,10},{9,11},{10,... | collective-permute-start | bytes 196616 | tf_op jit(solution)/shard_map/ppermute | solution.py:353
  55.7 10.3 %collective-permute-start.22 = (f32[520,256]{1,0:T(8,128)S(1)}, f32[520,256]{1,0:T(8,128)S(1)}, u32[]{:S(2)}, u32[]{:S(2)}) collective-permute-start(f32[520,256]{1,0:T(8,128)S(1)} %shard_map.153), channel_id=1, source_target_pairs={{0,1},{1,2},{2,3},{3,4},{4,5},{5,6},{6,7},{7,0},{8,9},{9,10},{10,1... | collective-permute-start | bytes 1597448 | tf_op jit(solution)/shard_map/ppermute | solution.py:348
  56.7 4.9 %collective-permute-start.21 = (f32[64,256]{1,0:T(8,128)S(1)}, f32[64,256]{1,0:T(8,128)S(1)}, u32[]{:S(2)}, u32[]{:S(2)}) collective-permute-start(f32[64,256]{1,0:T(8,128)S(1)} %add.98), channel_id=1, source_target_pairs={{0,24},{8,16},{16,8},{24,0},{1,25},{9,17},{17,9},{25,1},{2,26},{10... | collective-permute-start | bytes 196616 | tf_op jit(solution)/shard_map/ppermute | solution.py:353
  58.3 4.8 %collective-permute-start.20 = (f32[64,256]{1,0:T(8,128)S(1)}, f32[64,256]{1,0:T(8,128)S(1)}, u32[]{:S(2)}, u32[]{:S(2)}) collective-permute-start(f32[64,256]{1,0:T(8,128)S(1)} %add.98), channel_id=1, source_target_pairs={{0,16},{8,24},{16,0},{24,8},{1,17},{9,25},{17,1},{25,9},{2,18},{10... | collective-permute-start | bytes 196616 | tf_op jit(solution)/shard_map/ppermute | solution.py:353
  63.2 7.1 %collective-permute-start.25 = (f32[64,256]{1,0:T(8,128)S(1)}, f32[64,256]{1,0:T(8,128)S(1)}, u32[]{:S(2)}, u32[]{:S(2)}) collective-permute-start(f32[64,256]{1,0:T(8,128)S(1)} %add_add_fusion.1), channel_id=1, source_target_pairs={{0,6},{1,7},{2,4},{3,5},{4,2},{5,3},{6,0},{7,1},{8,14},{9,15},{10,... | collective-permute-start | bytes 196616 | tf_op jit(solution)/shard_map/ppermute | solution.py:353
  65.9 6.2 %collective-permute-start.24 = (f32[64,256]{1,0:T(8,128)S(1)}, f32[64,256]{1,0:T(8,128)S(1)}, u32[]{:S(2)}, u32[]{:S(2)}) collective-permute-start(f32[64,256]{1,0:T(8,128)S(1)} %add_add_fusion.1), channel_id=1, source_target_pairs={{0,4},{1,5},{2,6},{3,7},{4,0},{5,1},{6,2},{7,3},{8,12},{9,13},{10,... | collective-permute-start | bytes 196616 | tf_op jit(solution)/shard_map/ppermute | solution.py:353
  66.0 6.2 %collective-permute-start.23 = (f32[64,256]{1,0:T(8,128)S(1)}, f32[64,256]{1,0:T(8,128)S(1)}, u32[]{:S(2)}, u32[]{:S(2)}) collective-permute-start(f32[64,256]{1,0:T(8,128)S(1)} %add_add_fusion.1), channel_id=1, source_target_pairs={{0,2},{1,3},{2,0},{3,1},{4,6},{5,7},{6,4},{7,5},{8,10},{9,11},{10,... | collective-permute-start | bytes 196616 | tf_op jit(solution)/shard_map/ppermute | solution.py:353
  78.5 11.2 %collective-permute-start.31 = (f32[256,256]{1,0:T(8,128)S(1)}, f32[256,256]{1,0:T(8,128)S(1)}, u32[]{:S(2)}, u32[]{:S(2)}) collective-permute-start(f32[256,256]{1,0:T(8,128)S(1)} %get-tuple-element.230), channel_id=1, source_target_pairs={{0,5},{1,6},{2,7},{3,0},{4,1},{5,2},{6,3},{7,4},{8,13},{9,14},{10,... | collective-permute-start | bytes 786440 | tf_op jit(solution)/shard_map/ppermute | solution.py:348
  80.6 5.5 %collective-permute-start.29 = (f32[16,256]{1,0:T(8,128)S(1)}, f32[16,256]{1,0:T(8,128)S(1)}, u32[]{:S(2)}, u32[]{:S(2)}) collective-permute-start(f32[16,256]{1,0:T(8,128)S(1)} %get-tuple-element.242), channel_id=1, source_target_pairs={{0,16},{8,24},{16,0},{24,8},{1,17},{9,25},{17,1},{25,9},{2,18},{10... | collective-permute-start | bytes 49160 | tf_op jit(solution)/shard_map/ppermute | solution.py:353
  81.7 4.4 %collective-permute-start.30 = (f32[16,256]{1,0:T(8,128)S(1)}, f32[16,256]{1,0:T(8,128)S(1)}, u32[]{:S(2)}, u32[]{:S(2)}) collective-permute-start(f32[16,256]{1,0:T(8,128)S(1)} %get-tuple-element.243), channel_id=1, source_target_pairs={{0,24},{8,16},{16,8},{24,0},{1,25},{9,17},{17,9},{25,1},{2,26},{10... | collective-permute-start | bytes 49160 | tf_op jit(solution)/shard_map/ppermute | solution.py:353
  89.7 5.1 %collective-permute-start.34 = (f32[16,256]{1,0:T(8,128)S(1)}, f32[16,256]{1,0:T(8,128)S(1)}, u32[]{:S(2)}, u32[]{:S(2)}) collective-permute-start(f32[16,256]{1,0:T(8,128)S(1)} %slice_add_fusion), channel_id=1, source_target_pairs={{0,6},{1,7},{2,4},{3,5},{4,2},{5,3},{6,0},{7,1},{8,14},{9,15},{10,... | collective-permute-start | bytes 49160 | tf_op jit(solution)/shard_map/ppermute | solution.py:353
  93.2 11.6 %collective-permute-start.39 = (f32[264,256]{1,0:T(8,128)S(1)}, f32[264,256]{1,0:T(8,128)S(1)}, u32[]{:S(2)}, u32[]{:S(2)}) collective-permute-start(f32[264,256]{1,0:T(8,128)S(1)} %get-tuple-element.237), channel_id=1, source_target_pairs={{0,5},{1,6},{2,7},{3,0},{4,1},{5,2},{6,3},{7,4},{8,13},{9,14},{10,... | collective-permute-start | bytes 811016 | tf_op jit(solution)/shard_map/ppermute | solution.py:348
  97.5 7.3 %collective-permute-start.38 = (f32[32,256]{1,0:T(8,128)S(1)}, f32[32,256]{1,0:T(8,128)S(1)}, u32[]{:S(2)}, u32[]{:S(2)}) collective-permute-start(f32[32,256]{1,0:T(8,128)S(1)} %pad_maximum_fusion.refs_0_), channel_id=1, source_target_pairs={{0,24},{8,16},{16,8},{24,0},{1,25},{9,17},{17,9},{25,1},{2,26},{10... | collective-permute-start | bytes 98312 | tf_op jit(solution)/shard_map/ppermute | solution.py:353
  98.8 6.0 %collective-permute-start.37 = (f32[32,256]{1,0:T(8,128)S(1)}, f32[32,256]{1,0:T(8,128)S(1)}, u32[]{:S(2)}, u32[]{:S(2)}) collective-permute-start(f32[32,256]{1,0:T(8,128)S(1)} %pad_maximum_fusion.refs_0_), channel_id=1, source_target_pairs={{0,16},{8,24},{16,0},{24,8},{1,17},{9,25},{17,1},{25,9},{2,18},{10... | collective-permute-start | bytes 98312 | tf_op jit(solution)/shard_map/ppermute | solution.py:353
  99.3 5.6 %collective-permute-start.36 = (f32[32,256]{1,0:T(8,128)S(1)}, f32[32,256]{1,0:T(8,128)S(1)}, u32[]{:S(2)}, u32[]{:S(2)}) collective-permute-start(f32[32,256]{1,0:T(8,128)S(1)} %pad_maximum_fusion.refs_0_), channel_id=1, source_target_pairs={{0,8},{8,0},{16,24},{24,16},{1,9},{9,1},{17,25},{25,17},{2,10},{10... | collective-permute-start | bytes 98312 | tf_op jit(solution)/shard_map/ppermute | solution.py:353
  (16 other events, 44.0 us)

commit v5 on v4

--- a/solution.py
+++ b/solution.py
@@ -445,19 +445,19 @@
             src, sacc = call(
                 functools.partial(src_kernel, step, last), outs, [esr, eds, erl, neg, gsr, src, sacc]
             )
-            half, src, sacc, dst[0] = lax.optimization_barrier((half, src, sacc, dst[0]))
-            half = exchanged(half, "dst", 2)
+            half, src, sacc = lax.optimization_barrier((half, src, sacc))
+            half, dst[:1] = exchanged(half, "dst", 2, dst[:1])
             pair = jnp.concatenate([half, crossed(half, "dst", 1)], axis=0)
             pairs = [pair] + [crossed(pair, "src", k) for k in range(1, nsrc)]
         else:
             half = exchanged(half, "src", 1)
-            half, gsr = lax.optimization_barrier((half, gsr))
             outs += [((edges, width), F32), *prep_shapes]
             res = call(
                 functools.partial(src_kernel, step, last), outs, [esr, eds, erl, neg, gsr, src, sacc], [stack]
             )
+            half, *res = lax.optimization_barrier((half, *res))
             half, (dst,) = exchanged(half, "dst", 2, dst)
-            half, src, sacc, rows, *prep = lax.optimization_barrier((half, *res))
+            src, sacc, rows, *prep = res
             peer = crossed(half, "dst", 1)
     rel, racc, dst, dacc = call(
         final_kernel,

time: 106 us -> 103 us (0.972)
  waiting for transfers between devices: 30.4 us -> 27.1 us
    ppermute x5, waiting for transfers between devices: 8.28 us -> 6.37 us  [shifted(): lax.ppermute(value, axis, [(k, (k + steps) % count) for k in range(count)])]
    ppermute x35, waiting for transfers between devices: 22.1 us -> 20.7 us  [crossed(): return lax.ppermute(value, axis, [(k, k ^ bits) for k in range(count)])]
    ppermute x35, starting transfers between devices: 32 us -> 30.8 us  [crossed(): return lax.ppermute(value, axis, [(k, k ^ bits) for k in range(count)])]
  transfers between devices with their start and end apart: 40 -> 40, of which waited for: 16 -> 15; matrix products, arithmetic and copies ran while one was open for 0% -> 0% of each run, Pallas kernels for 18% -> 19%
where the time goes in v5:
time: 103 us; the launch traced here: 102 us
  starting transfers between devices  39.5 us (38%)
  Pallas kernels  34.6 us (34%)
  waiting for transfers between devices  27.1 us (26%)
  between operations  1.04 us (1%)
    pallas_call x14, Pallas kernels, call(): pl.pallas_call(body, out_shape=tuple((jax.ShapeDtypeStruct(s, d) for s, d...  34.6 us
    ppermute x35, starting transfers between devices, crossed(): return lax.ppermute(value, axis, [(k, k ^ bits) for k in range(count)])  30.8 us
    ppermute x35, waiting for transfers between devices, crossed(): return lax.ppermute(value, axis, [(k, k ^ bits) for k in range(count)])  20.7 us
    ppermute x5, starting transfers between devices, shifted(): lax.ppermute(value, axis, [(k, (k + steps) % count) for k in range(count)])  8.68 us
    ppermute x5, waiting for transfers between devices, shifted(): lax.ppermute(value, axis, [(k, (k + steps) % count) for k in range(count)])  6.37 us
  transfers between devices with their start and end apart: 40, of which 15 were waited for; matrix products, arithmetic and copies ran while one was open for 0% of the time, Pallas kernels for 19%

profile of v5, /device:TPU:1, one launch (start us, length us, event | category | flops | bytes accessed | tf_op | source)
XLA Modules:
  0.0 102.5 jit_solution(5373209915530475623)
XLA Ops:
  0.6 3.5 %shard_map.145 = (s32[4,8,128]{2,1,0:T(8,128)S(1)}, s32[4,8,128]{2,1,0:T(8,128)S(1)}, s32[4,8,128]{2,1,0:T(8,128)S(1)}, s32[4,8,128]{2,1,0:T(8,128)S(1)}, f32[8,...) custom-call(s32[4,8,128]{2,1,0:T(8,128)} %bitcast.12, ...), custom_call_target="tpu_custom_call" | custom-call | tf_op jit(solution)/shard_map/pallas_call | solution.py:336
  4.2 2.6 %shard_map.146 = (f32[64,256]{1,0:T(8,128)S(1)}, f32[64,256]{1,0:T(8,128)S(1)}, bf16[2,1024,512]{2,1,0:T(8,128)(2,1)S(1)}, bf16[2,1024,256]{2,1,0:T(8,128)(2,1)S(1)}, f32[1024,256]{1,0:T(8,128)S(1)}) custom-call(s32[1]{0:T(128)} %bitcast.refs_0_.spot_ref, s32[1]{0:T(128)} %bitcast.1.refs_1_.core_ref, f32[128,256]{1,0:T(8,128)S(1)} %get-tuple-element.119.refs_2_.refs_5_, ...), custom_call_target="tpu_custom_call" | custom-call | tf_op jit(solution)/shard_map/pallas_call | solution.py:336
  8.4 2.9 %collective-permute-start.4 = (f32[520,256]{1,0:T(8,128)S(1)}, f32[520,256]{1,0:T(8,128)S(1)}, u32[]{:S(2)}, u32[]{:S(2)}) collective-permute-start(f32[520,256]{1,0:T(8,128)S(1)} %shard_map.147), channel_id=1, source_target_pairs={{0,1},{1,2},{2,3},{3,4},{4,5},{5,6},{6,7},{7,0},{8,9},{9,10},{10,1... | collective-permute-start | bytes 1597448 | tf_op jit(solution)/shard_map/ppermute | solution.py:348
  11.3 2.2 %collective-permute-start.3 = (f32[64,256]{1,0:T(8,128)S(1)}, f32[64,256]{1,0:T(8,128)S(1)}, u32[]{:S(2)}, u32[]{:S(2)}) collective-permute-start(f32[64,256]{1,0:T(8,128)S(1)} %add.84), channel_id=1, source_target_pairs={{0,24},{8,16},{16,8},{24,0},{1,25},{9,17},{17,9},{25,1},{2,26},{10... | collective-permute-start | bytes 196616 | tf_op jit(solution)/shard_map/ppermute | solution.py:353
  14.0 3.4 %shard_map.148 = (f32[1024,256]{1,0:T(8,128)S(1)}, f32[8,128]{1,0:T(8,128)S(1)}, f32[1024,256]{1,0:T(8,128)S(1)}, f32[8,512]{1,0:T(8,128)S(1)}, f32[1024,512]{1,...) custom-call(s32[4,8,128]{2,1,0:T(8,128)S(1)} %get-tuple-element.131.esr_ref, ...), custom_call_target="tpu_custom_call" | custom-call | tf_op jit(solution)/shard_map/pallas_call | solution.py:336
  17.6 2.1 %collective-permute-start.7 = (f32[64,256]{1,0:T(8,128)S(1)}, f32[64,256]{1,0:T(8,128)S(1)}, u32[]{:S(2)}, u32[]{:S(2)}) collective-permute-start(f32[64,256]{1,0:T(8,128)S(1)} %add_add_fusion.5), channel_id=1, source_target_pairs={{0,6},{1,7},{2,4},{3,5},{4,2},{5,3},{6,0},{7,1},{8,14},{9,15},{10,... | collective-permute-start | bytes 196616 | tf_op jit(solution)/shard_map/ppermute | solution.py:353
  22.7 3.9 %collective-permute-done.6 = f32[64,256]{1,0:T(8,128)S(1)} collective-permute-done((f32[64,256]{1,0:T(8,128)S(1)}, f32[64,256]{1,0:T(8,128)S(1)}, u32[]{:S(2)}, u32[]{:S(2)}) %collective-permute-start.6) | collective-permute-done | bytes 65568 | tf_op jit(solution)/shard_map/ppermute | solution.py:353
  28.5 2.8 %shard_map.149 = (f32[64,256]{1,0:T(8,128)S(1)}, f32[64,256]{1,0:T(8,128)S(1)}, bf16[2,1024,512]{2,1,0:T(8,128)(2,1)S(1)}, bf16[2,1024,256]{2,1,0:T(8,128)(2,1)S...) custom-call(s32[1]{0:T(128)} %bitcast.refs_0_.spot_ref, s32[1]{0:T(128)} %bitcast.1.refs_1_.core_ref, ...), custom_call_target="tpu_custom_call" | custom-call | tf_op jit(solution)/shard_map/pallas_call | solution.py:336
  33.6 2.0 %collective-permute-start.12 = (f32[64,256]{1,0:T(8,128)S(1)}, f32[64,256]{1,0:T(8,128)S(1)}, u32[]{:S(2)}, u32[]{:S(2)}) collective-permute-start(f32[64,256]{1,0:T(8,128)S(1)} %add.91), channel_id=1, source_target_pairs={{0,24},{8,16},{16,8},{24,0},{1,25},{9,17},{17,9},{25,1},{2,26},{10... | collective-permute-start | bytes 196616 | tf_op jit(solution)/shard_map/ppermute | solution.py:353
  36.3 3.4 %shard_map.151 = (f32[1024,256]{1,0:T(8,128)S(1)}, f32[8,128]{1,0:T(8,128)S(1)}, f32[1024,256]{1,0:T(8,128)S(1)}, f32[8,512]{1,0:T(8,128)S(1)}, f32[1024,512]{1,...) custom-call(s32[4,8,128]{2,1,0:T(8,128)S(1)} %get-tuple-element.131.esr_ref, ...), custom_call_target="tpu_custom_call" | custom-call | tf_op jit(solution)/shard_map/pallas_call | solution.py:336
  39.8 3.5 %collective-permute-start.16 = (f32[64,256]{1,0:T(8,128)S(1)}, f32[64,256]{1,0:T(8,128)S(1)}, u32[]{:S(2)}, u32[]{:S(2)}) collective-permute-start(f32[64,256]{1,0:T(8,128)S(1)} %add_add_fusion.3), channel_id=1, source_target_pairs={{0,6},{1,7},{2,4},{3,5},{4,2},{5,3},{6,0},{7,1},{8,14},{9,15},{10,... | collective-permute-start | bytes 196616 | tf_op jit(solution)/shard_map/ppermute | solution.py:353
  45.0 4.4 %collective-permute-done.15 = f32[64,256]{1,0:T(8,128)S(1)} collective-permute-done((f32[64,256]{1,0:T(8,128)S(1)}, f32[64,256]{1,0:T(8,128)S(1)}, u32[]{:S(2)}, u32[]{:S(2)}) %collective-permute-start.15) | collective-permute-done | bytes 65568 | tf_op jit(solution)/shard_map/ppermute | solution.py:353
  50.9 2.8 %shard_map.152 = (f32[64,256]{1,0:T(8,128)S(1)}, f32[64,256]{1,0:T(8,128)S(1)}, bf16[2,1024,512]{2,1,0:T(8,128)(2,1)S(1)}, bf16[2,1024,256]{2,1,0:T(8,128)(2,1)S...) custom-call(s32[1]{0:T(128)} %bitcast.refs_0_.spot_ref, s32[1]{0:T(128)} %bitcast.1.refs_1_.core_ref, ...), custom_call_target="tpu_custom_call" | custom-call | tf_op jit(solution)/shard_map/pallas_call | solution.py:336
  56.7 1.9 %collective-permute-start.21 = (f32[64,256]{1,0:T(8,128)S(1)}, f32[64,256]{1,0:T(8,128)S(1)}, u32[]{:S(2)}, u32[]{:S(2)}) collective-permute-start(f32[64,256]{1,0:T(8,128)S(1)} %add.98), channel_id=1, source_target_pairs={{0,24},{8,16},{16,8},{24,0},{1,25},{9,17},{17,9},{25,1},{2,26},{10... | collective-permute-start | bytes 196616 | tf_op jit(solution)/shard_map/ppermute | solution.py:353
  59.5 3.4 %shard_map.154 = (f32[1024,256]{1,0:T(8,128)S(1)}, f32[8,128]{1,0:T(8,128)S(1)}, f32[1024,256]{1,0:T(8,128)S(1)}, f32[8,512]{1,0:T(8,128)S(1)}, f32[1024,512]{1,...) custom-call(s32[4,8,128]{2,1,0:T(8,128)S(1)} %get-tuple-element.131.esr_ref, ...), custom_call_target="tpu_custom_call" | custom-call | tf_op jit(solution)/shard_map/pallas_call | solution.py:336
  63.1 2.5 %collective-permute-start.25 = (f32[64,256]{1,0:T(8,128)S(1)}, f32[64,256]{1,0:T(8,128)S(1)}, u32[]{:S(2)}, u32[]{:S(2)}) collective-permute-start(f32[64,256]{1,0:T(8,128)S(1)} %add_add_fusion.1), channel_id=1, source_target_pairs={{0,6},{1,7},{2,4},{3,5},{4,2},{5,3},{6,0},{7,1},{8,14},{9,15},{10,... | collective-permute-start | bytes 196616 | tf_op jit(solution)/shard_map/ppermute | solution.py:353
  68.2 3.8 %collective-permute-done.24 = f32[64,256]{1,0:T(8,128)S(1)} collective-permute-done((f32[64,256]{1,0:T(8,128)S(1)}, f32[64,256]{1,0:T(8,128)S(1)}, u32[]{:S(2)}, u32[]{:S(2)}) %collective-permute-start.24) | collective-permute-done | bytes 65568 | tf_op jit(solution)/shard_map/ppermute | solution.py:353
  73.8 2.7 %shard_map.155 = (f32[64,256]{1,0:T(8,128)S(1)}, f32[64,256]{1,0:T(8,128)S(1)}, bf16[2,1024,512]{2,1,0:T(8,128)(2,1)S(1)}, bf16[2,1024,256]{2,1,0:T(8,128)(2,1)S...) custom-call(s32[1]{0:T(128)} %bitcast.refs_0_.spot_ref, s32[1]{0:T(128)} %bitcast.1.refs_1_.core_ref, ...), custom_call_target="tpu_custom_call" | custom-call | tf_op jit(solution)/shard_map/pallas_call | solution.py:336
  78.5 2.1 %collective-permute-start.31 = (f32[256,256]{1,0:T(8,128)S(1)}, f32[256,256]{1,0:T(8,128)S(1)}, u32[]{:S(2)}, u32[]{:S(2)}) collective-permute-start(f32[256,256]{1,0:T(8,128)S(1)} %get-tuple-element.222), channel_id=1, source_target_pairs={{0,5},{1,6},{2,7},{3,0},{4,1},{5,2},{6,3},{7,4},{8,13},{9,14},{10,... | collective-permute-start | bytes 786440 | tf_op jit(solution)/shard_map/ppermute | solution.py:348
  83.3 2.7 %shard_map.157 = (f32[1024,256]{1,0:T(8,128)}, f32[8,128]{1,0:T(8,128)}) custom-call(s32[4,8,128]{2,1,0:T(8,128)S(1)} %get-tuple-element.131.esr_ref, s32[4,8,128]{2,1,0:T(8,128)S(1)} %get-tuple-element.132.eds_ref, s32[4,8,128]{2,1,0:T(8,128)S(1)} %get-tuple-element.133.erl_ref, s32[4,8,128]{2,1,0:T(8,128)S(1)} %get-tuple-element.134.neg_ref, ...), custom_call_target="tpu_custom_call" | custom-call | tf_op jit(solution)/shard_map/pallas_call | solution.py:336
  86.8 2.8 %collective-permute-done.31.refs_6_ = f32[256,256]{1,0:T(8,128)S(1)} collective-permute-done((f32[256,256]{1,0:T(8,128)S(1)}, f32[256,256]{1,0:T(8,128)S(1)}, u32[]{:S(2)}, u32[]{:S(2)}) %collective-permute-start.31) | collective-permute-done | bytes 262176 | tf_op jit(solution)/shard_map/ppermute | solution.py:348
  89.7 2.5 %collective-permute-start.39 = (f32[264,256]{1,0:T(8,128)S(1)}, f32[264,256]{1,0:T(8,128)S(1)}, u32[]{:S(2)}, u32[]{:S(2)}) collective-permute-start(f32[264,256]{1,0:T(8,128)S(1)} %get-tuple-element.227), channel_id=1, source_target_pairs={{0,5},{1,6},{2,7},{3,0},{4,1},{5,2},{6,3},{7,4},{8,13},{9,14},{10,... | collective-permute-start | bytes 811016 | tf_op jit(solution)/shard_map/ppermute | solution.py:348
  92.5 1.7 %collective-permute-start.35 = (f32[16,256]{1,0:T(8,128)S(1)}, f32[16,256]{1,0:T(8,128)S(1)}, u32[]{:S(2)}, u32[]{:S(2)}) collective-permute-start(f32[16,256]{1,0:T(8,128)S(1)} %add_add_fusion.6), channel_id=1, source_target_pairs={{0,1},{1,0},{2,3},{3,2},{4,5},{5,4},{6,7},{7,6},{8,9},{9,8},{10,11... | collective-permute-start | bytes 49160 | tf_op jit(solution)/shard_map/ppermute | solution.py:353
  97.6 3.6 %collective-permute-done.39.refs_7_ = f32[264,256]{1,0:T(8,128)S(1)} collective-permute-done((f32[264,256]{1,0:T(8,128)S(1)}, f32[264,256]{1,0:T(8,128)S(1)}, u32[]{:S(2)}, u32[]{:S(2)}) %collective-permute-start.39) | collective-permute-done | bytes 270368 | tf_op jit(solution)/shard_map/ppermute | solution.py:348
  (84 shorter events, 32.3 us)
Async XLA Ops:
  8.4 11.7 %collective-permute-start.4 = (f32[520,256]{1,0:T(8,128)S(1)}, f32[520,256]{1,0:T(8,128)S(1)}, u32[]{:S(2)}, u32[]{:S(2)}) collective-permute-start(f32[520,256]{1,0:T(8,128)S(1)} %shard_map.147), channel_id=1, source_target_pairs={{0,1},{1,2},{2,3},{3,4},{4,5},{5,6},{6,7},{7,0},{8,9},{9,10},{10,1... | collective-permute-start | bytes 1597448 | tf_op jit(solution)/shard_map/ppermute | solution.py:348
  11.3 6.1 %collective-permute-start.3 = (f32[64,256]{1,0:T(8,128)S(1)}, f32[64,256]{1,0:T(8,128)S(1)}, u32[]{:S(2)}, u32[]{:S(2)}) collective-permute-start(f32[64,256]{1,0:T(8,128)S(1)} %add.84), channel_id=1, source_target_pairs={{0,24},{8,16},{16,8},{24,0},{1,25},{9,17},{17,9},{25,1},{2,26},{10... | collective-permute-start | bytes 196616 | tf_op jit(solution)/shard_map/ppermute | solution.py:353
  17.6 5.1 %collective-permute-start.7 = (f32[64,256]{1,0:T(8,128)S(1)}, f32[64,256]{1,0:T(8,128)S(1)}, u32[]{:S(2)}, u32[]{:S(2)}) collective-permute-start(f32[64,256]{1,0:T(8,128)S(1)} %add_add_fusion.5), channel_id=1, source_target_pairs={{0,6},{1,7},{2,4},{3,5},{4,2},{5,3},{6,0},{7,1},{8,14},{9,15},{10,... | collective-permute-start | bytes 196616 | tf_op jit(solution)/shard_map/ppermute | solution.py:353
  19.7 7.0 %collective-permute-start.6 = (f32[64,256]{1,0:T(8,128)S(1)}, f32[64,256]{1,0:T(8,128)S(1)}, u32[]{:S(2)}, u32[]{:S(2)}) collective-permute-start(f32[64,256]{1,0:T(8,128)S(1)} %add_add_fusion.5), channel_id=1, source_target_pairs={{0,4},{1,5},{2,6},{3,7},{4,0},{5,1},{6,2},{7,3},{8,12},{9,13},{10,... | collective-permute-start | bytes 196616 | tf_op jit(solution)/shard_map/ppermute | solution.py:353
  20.2 6.5 %collective-permute-start.5 = (f32[64,256]{1,0:T(8,128)S(1)}, f32[64,256]{1,0:T(8,128)S(1)}, u32[]{:S(2)}, u32[]{:S(2)}) collective-permute-start(f32[64,256]{1,0:T(8,128)S(1)} %add_add_fusion.5), channel_id=1, source_target_pairs={{0,2},{1,3},{2,0},{3,1},{4,6},{5,7},{6,4},{7,5},{8,10},{9,11},{10,... | collective-permute-start | bytes 196616 | tf_op jit(solution)/shard_map/ppermute | solution.py:353
  33.3 10.0 %collective-permute-start.13 = (f32[520,256]{1,0:T(8,128)S(1)}, f32[520,256]{1,0:T(8,128)S(1)}, u32[]{:S(2)}, u32[]{:S(2)}) collective-permute-start(f32[520,256]{1,0:T(8,128)S(1)} %shard_map.150), channel_id=1, source_target_pairs={{0,1},{1,2},{2,3},{3,4},{4,5},{5,6},{6,7},{7,0},{8,9},{9,10},{10,1... | collective-permute-start | bytes 1597448 | tf_op jit(solution)/shard_map/ppermute | solution.py:348
  33.6 6.1 %collective-permute-start.12 = (f32[64,256]{1,0:T(8,128)S(1)}, f32[64,256]{1,0:T(8,128)S(1)}, u32[]{:S(2)}, u32[]{:S(2)}) collective-permute-start(f32[64,256]{1,0:T(8,128)S(1)} %add.91), channel_id=1, source_target_pairs={{0,24},{8,16},{16,8},{24,0},{1,25},{9,17},{17,9},{25,1},{2,26},{10... | collective-permute-start | bytes 196616 | tf_op jit(solution)/shard_map/ppermute | solution.py:353
  39.8 5.2 %collective-permute-start.16 = (f32[64,256]{1,0:T(8,128)S(1)}, f32[64,256]{1,0:T(8,128)S(1)}, u32[]{:S(2)}, u32[]{:S(2)}) collective-permute-start(f32[64,256]{1,0:T(8,128)S(1)} %add_add_fusion.3), channel_id=1, source_target_pairs={{0,6},{1,7},{2,4},{3,5},{4,2},{5,3},{6,0},{7,1},{8,14},{9,15},{10,... | collective-permute-start | bytes 196616 | tf_op jit(solution)/shard_map/ppermute | solution.py:353
  43.3 6.2 %collective-permute-start.15 = (f32[64,256]{1,0:T(8,128)S(1)}, f32[64,256]{1,0:T(8,128)S(1)}, u32[]{:S(2)}, u32[]{:S(2)}) collective-permute-start(f32[64,256]{1,0:T(8,128)S(1)} %add_add_fusion.3), channel_id=1, source_target_pairs={{0,4},{1,5},{2,6},{3,7},{4,0},{5,1},{6,2},{7,3},{8,12},{9,13},{10,... | collective-permute-start | bytes 196616 | tf_op jit(solution)/shard_map/ppermute | solution.py:353
  43.3 6.2 %collective-permute-start.14 = (f32[64,256]{1,0:T(8,128)S(1)}, f32[64,256]{1,0:T(8,128)S(1)}, u32[]{:S(2)}, u32[]{:S(2)}) collective-permute-start(f32[64,256]{1,0:T(8,128)S(1)} %add_add_fusion.3), channel_id=1, source_target_pairs={{0,2},{1,3},{2,0},{3,1},{4,6},{5,7},{6,4},{7,5},{8,10},{9,11},{10,... | collective-permute-start | bytes 196616 | tf_op jit(solution)/shard_map/ppermute | solution.py:353
  55.7 10.0 %collective-permute-start.22 = (f32[520,256]{1,0:T(8,128)S(1)}, f32[520,256]{1,0:T(8,128)S(1)}, u32[]{:S(2)}, u32[]{:S(2)}) collective-permute-start(f32[520,256]{1,0:T(8,128)S(1)} %shard_map.153), channel_id=1, source_target_pairs={{0,1},{1,2},{2,3},{3,4},{4,5},{5,6},{6,7},{7,0},{8,9},{9,10},{10,1... | collective-permute-start | bytes 1597448 | tf_op jit(solution)/shard_map/ppermute | solution.py:348
  56.7 6.2 %collective-permute-start.21 = (f32[64,256]{1,0:T(8,128)S(1)}, f32[64,256]{1,0:T(8,128)S(1)}, u32[]{:S(2)}, u32[]{:S(2)}) collective-permute-start(f32[64,256]{1,0:T(8,128)S(1)} %add.98), channel_id=1, source_target_pairs={{0,24},{8,16},{16,8},{24,0},{1,25},{9,17},{17,9},{25,1},{2,26},{10... | collective-permute-start | bytes 196616 | tf_op jit(solution)/shard_map/ppermute | solution.py:353
  58.6 4.5 %collective-permute-start.20 = (f32[64,256]{1,0:T(8,128)S(1)}, f32[64,256]{1,0:T(8,128)S(1)}, u32[]{:S(2)}, u32[]{:S(2)}) collective-permute-start(f32[64,256]{1,0:T(8,128)S(1)} %add.98), channel_id=1, source_target_pairs={{0,16},{8,24},{16,0},{24,8},{1,17},{9,25},{17,1},{25,9},{2,18},{10... | collective-permute-start | bytes 196616 | tf_op jit(solution)/shard_map/ppermute | solution.py:353
  63.1 5.1 %collective-permute-start.25 = (f32[64,256]{1,0:T(8,128)S(1)}, f32[64,256]{1,0:T(8,128)S(1)}, u32[]{:S(2)}, u32[]{:S(2)}) collective-permute-start(f32[64,256]{1,0:T(8,128)S(1)} %add_add_fusion.1), channel_id=1, source_target_pairs={{0,6},{1,7},{2,4},{3,5},{4,2},{5,3},{6,0},{7,1},{8,14},{9,15},{10,... | collective-permute-start | bytes 196616 | tf_op jit(solution)/shard_map/ppermute | solution.py:353
  65.7 6.3 %collective-permute-start.24 = (f32[64,256]{1,0:T(8,128)S(1)}, f32[64,256]{1,0:T(8,128)S(1)}, u32[]{:S(2)}, u32[]{:S(2)}) collective-permute-start(f32[64,256]{1,0:T(8,128)S(1)} %add_add_fusion.1), channel_id=1, source_target_pairs={{0,4},{1,5},{2,6},{3,7},{4,0},{5,1},{6,2},{7,3},{8,12},{9,13},{10,... | collective-permute-start | bytes 196616 | tf_op jit(solution)/shard_map/ppermute | solution.py:353
  65.7 6.3 %collective-permute-start.23 = (f32[64,256]{1,0:T(8,128)S(1)}, f32[64,256]{1,0:T(8,128)S(1)}, u32[]{:S(2)}, u32[]{:S(2)}) collective-permute-start(f32[64,256]{1,0:T(8,128)S(1)} %add_add_fusion.1), channel_id=1, source_target_pairs={{0,2},{1,3},{2,0},{3,1},{4,6},{5,7},{6,4},{7,5},{8,10},{9,11},{10,... | collective-permute-start | bytes 196616 | tf_op jit(solution)/shard_map/ppermute | solution.py:353
  78.5 11.1 %collective-permute-start.31 = (f32[256,256]{1,0:T(8,128)S(1)}, f32[256,256]{1,0:T(8,128)S(1)}, u32[]{:S(2)}, u32[]{:S(2)}) collective-permute-start(f32[256,256]{1,0:T(8,128)S(1)} %get-tuple-element.222), channel_id=1, source_target_pairs={{0,5},{1,6},{2,7},{3,0},{4,1},{5,2},{6,3},{7,4},{8,13},{9,14},{10,... | collective-permute-start | bytes 786440 | tf_op jit(solution)/shard_map/ppermute | solution.py:348
  80.6 5.5 %collective-permute-start.29 = (f32[16,256]{1,0:T(8,128)S(1)}, f32[16,256]{1,0:T(8,128)S(1)}, u32[]{:S(2)}, u32[]{:S(2)}) collective-permute-start(f32[16,256]{1,0:T(8,128)S(1)} %get-tuple-element.232), channel_id=1, source_target_pairs={{0,16},{8,24},{16,0},{24,8},{1,17},{9,25},{17,1},{25,9},{2,18},{10... | collective-permute-start | bytes 49160 | tf_op jit(solution)/shard_map/ppermute | solution.py:353
  86.1 6.1 %collective-permute-start.34 = (f32[16,256]{1,0:T(8,128)S(1)}, f32[16,256]{1,0:T(8,128)S(1)}, u32[]{:S(2)}, u32[]{:S(2)}) collective-permute-start(f32[16,256]{1,0:T(8,128)S(1)} %slice_add_fusion), channel_id=1, source_target_pairs={{0,6},{1,7},{2,4},{3,5},{4,2},{5,3},{6,0},{7,1},{8,14},{9,15},{10,... | collective-permute-start | bytes 49160 | tf_op jit(solution)/shard_map/ppermute | solution.py:353
  86.1 6.1 %collective-permute-start.33 = (f32[16,256]{1,0:T(8,128)S(1)}, f32[16,256]{1,0:T(8,128)S(1)}, u32[]{:S(2)}, u32[]{:S(2)}) collective-permute-start(f32[16,256]{1,0:T(8,128)S(1)} %slice_add_fusion), channel_id=1, source_target_pairs={{0,4},{1,5},{2,6},{3,7},{4,0},{5,1},{6,2},{7,3},{8,12},{9,13},{10,... | collective-permute-start | bytes 49160 | tf_op jit(solution)/shard_map/ppermute | solution.py:353
  89.7 11.5 %collective-permute-start.39 = (f32[264,256]{1,0:T(8,128)S(1)}, f32[264,256]{1,0:T(8,128)S(1)}, u32[]{:S(2)}, u32[]{:S(2)}) collective-permute-start(f32[264,256]{1,0:T(8,128)S(1)} %get-tuple-element.227), channel_id=1, source_target_pairs={{0,5},{1,6},{2,7},{3,0},{4,1},{5,2},{6,3},{7,4},{8,13},{9,14},{10,... | collective-permute-start | bytes 811016 | tf_op jit(solution)/shard_map/ppermute | solution.py:348
  95.0 6.2 %collective-permute-start.38 = (f32[32,256]{1,0:T(8,128)S(1)}, f32[32,256]{1,0:T(8,128)S(1)}, u32[]{:S(2)}, u32[]{:S(2)}) collective-permute-start(f32[32,256]{1,0:T(8,128)S(1)} %pad_maximum_fusion.refs_0_), channel_id=1, source_target_pairs={{0,24},{8,16},{16,8},{24,0},{1,25},{9,17},{17,9},{25,1},{2,26},{10... | collective-permute-start | bytes 98312 | tf_op jit(solution)/shard_map/ppermute | solution.py:353
  96.5 4.8 %collective-permute-start.37 = (f32[32,256]{1,0:T(8,128)S(1)}, f32[32,256]{1,0:T(8,128)S(1)}, u32[]{:S(2)}, u32[]{:S(2)}) collective-permute-start(f32[32,256]{1,0:T(8,128)S(1)} %pad_maximum_fusion.refs_0_), channel_id=1, source_target_pairs={{0,16},{8,24},{16,0},{24,8},{1,17},{9,25},{17,1},{25,9},{2,18},{10... | collective-permute-start | bytes 98312 | tf_op jit(solution)/shard_map/ppermute | solution.py:353
  97.0 4.3 %collective-permute-start.36 = (f32[32,256]{1,0:T(8,128)S(1)}, f32[32,256]{1,0:T(8,128)S(1)}, u32[]{:S(2)}, u32[]{:S(2)}) collective-permute-start(f32[32,256]{1,0:T(8,128)S(1)} %pad_maximum_fusion.refs_0_), channel_id=1, source_target_pairs={{0,8},{8,0},{16,24},{24,16},{1,9},{9,1},{17,25},{25,17},{2,10},{10... | collective-permute-start | bytes 98312 | tf_op jit(solution)/shard_map/ppermute | solution.py:353
  (16 other events, 45.1 us)

commit v6 on v5

--- a/solution.py
+++ b/solution.py
@@ -233,11 +233,8 @@
     width = dst_ref.shape[1]
     head = 0 if len(outs) == 1 else outs[0].shape[0]
     tail_ref = outs[-1]
-    grad = (
-        dot(wgt_ref[0], qry_ref[0], 0, 0)
-        + dot(wgt_ref[0], qry_ref[1], 0, 0)
-        + dot(wgt_ref[1], qry_ref[0], 0, 0)
-    )
+    wide = dot(wgt_ref[0], jnp.concatenate([qry_ref[0], qry_ref[1]], axis=1), 0, 0)
+    grad = wide[:, :width] + wide[:, width:] + dot(wgt_ref[1], qry_ref[0], 0, 0)
     blocks = rows // LANES
     cols = columns(dst_ref[rows : rows + 8, 0:LANES])
     totals = []

time: 103 us -> 103 us (level)
  no operation moved by 1% of the time
where the time goes in v6:
time: 103 us; the launch traced here: 102 us
  starting transfers between devices  39.5 us (38%)
  Pallas kernels  34.7 us (34%)
  waiting for transfers between devices  27.1 us (26%)
  between operations  1.04 us (1%)
    pallas_call x14, Pallas kernels, call(): pl.pallas_call(body, out_shape=tuple((jax.ShapeDtypeStruct(s, d) for s, d...  34.7 us
    ppermute x35, starting transfers between devices, crossed(): return lax.ppermute(value, axis, [(k, k ^ bits) for k in range(count)])  30.8 us
    ppermute x35, waiting for transfers between devices, crossed(): return lax.ppermute(value, axis, [(k, k ^ bits) for k in range(count)])  20.7 us
    ppermute x5, starting transfers between devices, shifted(): lax.ppermute(value, axis, [(k, (k + steps) % count) for k in range(count)])  8.68 us
    ppermute x5, waiting for transfers between devices, shifted(): lax.ppermute(value, axis, [(k, (k + steps) % count) for k in range(count)])  6.38 us
  transfers between devices with their start and end apart: 40, of which 15 were waited for; matrix products, arithmetic and copies ran while one was open for 0% of the time, Pallas kernels for 19%

profile of v6, /device:TPU:1, one launch (start us, length us, event | category | flops | bytes accessed | tf_op | source)
XLA Modules:
  0.0 102.5 jit_solution(10228285201894318790)
XLA Ops:
  0.6 3.5 %shard_map.145 = (s32[4,8,128]{2,1,0:T(8,128)S(1)}, s32[4,8,128]{2,1,0:T(8,128)S(1)}, s32[4,8,128]{2,1,0:T(8,128)S(1)}, s32[4,8,128]{2,1,0:T(8,128)S(1)}, f32[8,...) custom-call(s32[4,8,128]{2,1,0:T(8,128)} %bitcast.12, ...), custom_call_target="tpu_custom_call" | custom-call | tf_op jit(solution)/shard_map/pallas_call | solution.py:333
  4.2 2.6 %shard_map.146 = (f32[64,256]{1,0:T(8,128)S(1)}, f32[64,256]{1,0:T(8,128)S(1)}, bf16[2,1024,512]{2,1,0:T(8,128)(2,1)S(1)}, bf16[2,1024,256]{2,1,0:T(8,128)(2,1)S(1)}, f32[1024,256]{1,0:T(8,128)S(1)}) custom-call(s32[1]{0:T(128)} %bitcast.refs_0_.spot_ref, s32[1]{0:T(128)} %bitcast.1.refs_1_.core_ref, f32[128,256]{1,0:T(8,128)S(1)} %get-tuple-element.119.refs_2_.refs_5_, ...), custom_call_target="tpu_custom_call" | custom-call | tf_op jit(solution)/shard_map/pallas_call | solution.py:333
  8.4 2.9 %collective-permute-start.4 = (f32[520,256]{1,0:T(8,128)S(1)}, f32[520,256]{1,0:T(8,128)S(1)}, u32[]{:S(2)}, u32[]{:S(2)}) collective-permute-start(f32[520,256]{1,0:T(8,128)S(1)} %shard_map.147), channel_id=1, source_target_pairs={{0,1},{1,2},{2,3},{3,4},{4,5},{5,6},{6,7},{7,0},{8,9},{9,10},{10,1... | collective-permute-start | bytes 1597448 | tf_op jit(solution)/shard_map/ppermute | solution.py:345
  11.3 2.2 %collective-permute-start.3 = (f32[64,256]{1,0:T(8,128)S(1)}, f32[64,256]{1,0:T(8,128)S(1)}, u32[]{:S(2)}, u32[]{:S(2)}) collective-permute-start(f32[64,256]{1,0:T(8,128)S(1)} %add.84), channel_id=1, source_target_pairs={{0,24},{8,16},{16,8},{24,0},{1,25},{9,17},{17,9},{25,1},{2,26},{10... | collective-permute-start | bytes 196616 | tf_op jit(solution)/shard_map/ppermute | solution.py:350
  14.0 3.4 %shard_map.148 = (f32[1024,256]{1,0:T(8,128)S(1)}, f32[8,128]{1,0:T(8,128)S(1)}, f32[1024,256]{1,0:T(8,128)S(1)}, f32[8,512]{1,0:T(8,128)S(1)}, f32[1024,512]{1,...) custom-call(s32[4,8,128]{2,1,0:T(8,128)S(1)} %get-tuple-element.131.esr_ref, ...), custom_call_target="tpu_custom_call" | custom-call | tf_op jit(solution)/shard_map/pallas_call | solution.py:333
  17.6 2.1 %collective-permute-start.7 = (f32[64,256]{1,0:T(8,128)S(1)}, f32[64,256]{1,0:T(8,128)S(1)}, u32[]{:S(2)}, u32[]{:S(2)}) collective-permute-start(f32[64,256]{1,0:T(8,128)S(1)} %add_add_fusion.5), channel_id=1, source_target_pairs={{0,6},{1,7},{2,4},{3,5},{4,2},{5,3},{6,0},{7,1},{8,14},{9,15},{10,... | collective-permute-start | bytes 196616 | tf_op jit(solution)/shard_map/ppermute | solution.py:350
  22.7 3.9 %collective-permute-done.6 = f32[64,256]{1,0:T(8,128)S(1)} collective-permute-done((f32[64,256]{1,0:T(8,128)S(1)}, f32[64,256]{1,0:T(8,128)S(1)}, u32[]{:S(2)}, u32[]{:S(2)}) %collective-permute-start.6) | collective-permute-done | bytes 65568 | tf_op jit(solution)/shard_map/ppermute | solution.py:350
  28.5 2.8 %shard_map.149 = (f32[64,256]{1,0:T(8,128)S(1)}, f32[64,256]{1,0:T(8,128)S(1)}, bf16[2,1024,512]{2,1,0:T(8,128)(2,1)S(1)}, bf16[2,1024,256]{2,1,0:T(8,128)(2,1)S...) custom-call(s32[1]{0:T(128)} %bitcast.refs_0_.spot_ref, s32[1]{0:T(128)} %bitcast.1.refs_1_.core_ref, ...), custom_call_target="tpu_custom_call" | custom-call | tf_op jit(solution)/shard_map/pallas_call | solution.py:333
  33.6 2.0 %collective-permute-start.12 = (f32[64,256]{1,0:T(8,128)S(1)}, f32[64,256]{1,0:T(8,128)S(1)}, u32[]{:S(2)}, u32[]{:S(2)}) collective-permute-start(f32[64,256]{1,0:T(8,128)S(1)} %add.91), channel_id=1, source_target_pairs={{0,24},{8,16},{16,8},{24,0},{1,25},{9,17},{17,9},{25,1},{2,26},{10... | collective-permute-start | bytes 196616 | tf_op jit(solution)/shard_map/ppermute | solution.py:350
  36.3 3.4 %shard_map.151 = (f32[1024,256]{1,0:T(8,128)S(1)}, f32[8,128]{1,0:T(8,128)S(1)}, f32[1024,256]{1,0:T(8,128)S(1)}, f32[8,512]{1,0:T(8,128)S(1)}, f32[1024,512]{1,...) custom-call(s32[4,8,128]{2,1,0:T(8,128)S(1)} %get-tuple-element.131.esr_ref, ...), custom_call_target="tpu_custom_call" | custom-call | tf_op jit(solution)/shard_map/pallas_call | solution.py:333
  39.8 3.5 %collective-permute-start.16 = (f32[64,256]{1,0:T(8,128)S(1)}, f32[64,256]{1,0:T(8,128)S(1)}, u32[]{:S(2)}, u32[]{:S(2)}) collective-permute-start(f32[64,256]{1,0:T(8,128)S(1)} %add_add_fusion.3), channel_id=1, source_target_pairs={{0,6},{1,7},{2,4},{3,5},{4,2},{5,3},{6,0},{7,1},{8,14},{9,15},{10,... | collective-permute-start | bytes 196616 | tf_op jit(solution)/shard_map/ppermute | solution.py:350
  45.0 4.4 %collective-permute-done.15 = f32[64,256]{1,0:T(8,128)S(1)} collective-permute-done((f32[64,256]{1,0:T(8,128)S(1)}, f32[64,256]{1,0:T(8,128)S(1)}, u32[]{:S(2)}, u32[]{:S(2)}) %collective-permute-start.15) | collective-permute-done | bytes 65568 | tf_op jit(solution)/shard_map/ppermute | solution.py:350
  50.9 2.8 %shard_map.152 = (f32[64,256]{1,0:T(8,128)S(1)}, f32[64,256]{1,0:T(8,128)S(1)}, bf16[2,1024,512]{2,1,0:T(8,128)(2,1)S(1)}, bf16[2,1024,256]{2,1,0:T(8,128)(2,1)S...) custom-call(s32[1]{0:T(128)} %bitcast.refs_0_.spot_ref, s32[1]{0:T(128)} %bitcast.1.refs_1_.core_ref, ...), custom_call_target="tpu_custom_call" | custom-call | tf_op jit(solution)/shard_map/pallas_call | solution.py:333
  56.7 1.9 %collective-permute-start.21 = (f32[64,256]{1,0:T(8,128)S(1)}, f32[64,256]{1,0:T(8,128)S(1)}, u32[]{:S(2)}, u32[]{:S(2)}) collective-permute-start(f32[64,256]{1,0:T(8,128)S(1)} %add.98), channel_id=1, source_target_pairs={{0,24},{8,16},{16,8},{24,0},{1,25},{9,17},{17,9},{25,1},{2,26},{10... | collective-permute-start | bytes 196616 | tf_op jit(solution)/shard_map/ppermute | solution.py:350
  59.5 3.4 %shard_map.154 = (f32[1024,256]{1,0:T(8,128)S(1)}, f32[8,128]{1,0:T(8,128)S(1)}, f32[1024,256]{1,0:T(8,128)S(1)}, f32[8,512]{1,0:T(8,128)S(1)}, f32[1024,512]{1,...) custom-call(s32[4,8,128]{2,1,0:T(8,128)S(1)} %get-tuple-element.131.esr_ref, ...), custom_call_target="tpu_custom_call" | custom-call | tf_op jit(solution)/shard_map/pallas_call | solution.py:333
  63.1 2.5 %collective-permute-start.25 = (f32[64,256]{1,0:T(8,128)S(1)}, f32[64,256]{1,0:T(8,128)S(1)}, u32[]{:S(2)}, u32[]{:S(2)}) collective-permute-start(f32[64,256]{1,0:T(8,128)S(1)} %add_add_fusion.1), channel_id=1, source_target_pairs={{0,6},{1,7},{2,4},{3,5},{4,2},{5,3},{6,0},{7,1},{8,14},{9,15},{10,... | collective-permute-start | bytes 196616 | tf_op jit(solution)/shard_map/ppermute | solution.py:350
  68.2 3.8 %collective-permute-done.24 = f32[64,256]{1,0:T(8,128)S(1)} collective-permute-done((f32[64,256]{1,0:T(8,128)S(1)}, f32[64,256]{1,0:T(8,128)S(1)}, u32[]{:S(2)}, u32[]{:S(2)}) %collective-permute-start.24) | collective-permute-done | bytes 65568 | tf_op jit(solution)/shard_map/ppermute | solution.py:350
  73.8 2.7 %shard_map.155 = (f32[64,256]{1,0:T(8,128)S(1)}, f32[64,256]{1,0:T(8,128)S(1)}, bf16[2,1024,512]{2,1,0:T(8,128)(2,1)S(1)}, bf16[2,1024,256]{2,1,0:T(8,128)(2,1)S...) custom-call(s32[1]{0:T(128)} %bitcast.refs_0_.spot_ref, s32[1]{0:T(128)} %bitcast.1.refs_1_.core_ref, ...), custom_call_target="tpu_custom_call" | custom-call | tf_op jit(solution)/shard_map/pallas_call | solution.py:333
  78.5 2.1 %collective-permute-start.31 = (f32[256,256]{1,0:T(8,128)S(1)}, f32[256,256]{1,0:T(8,128)S(1)}, u32[]{:S(2)}, u32[]{:S(2)}) collective-permute-start(f32[256,256]{1,0:T(8,128)S(1)} %get-tuple-element.222), channel_id=1, source_target_pairs={{0,5},{1,6},{2,7},{3,0},{4,1},{5,2},{6,3},{7,4},{8,13},{9,14},{10,... | collective-permute-start | bytes 786440 | tf_op jit(solution)/shard_map/ppermute | solution.py:345
  83.3 2.7 %shard_map.157 = (f32[1024,256]{1,0:T(8,128)}, f32[8,128]{1,0:T(8,128)}) custom-call(s32[4,8,128]{2,1,0:T(8,128)S(1)} %get-tuple-element.131.esr_ref, s32[4,8,128]{2,1,0:T(8,128)S(1)} %get-tuple-element.132.eds_ref, s32[4,8,128]{2,1,0:T(8,128)S(1)} %get-tuple-element.133.erl_ref, s32[4,8,128]{2,1,0:T(8,128)S(1)} %get-tuple-element.134.neg_ref, ...), custom_call_target="tpu_custom_call" | custom-call | tf_op jit(solution)/shard_map/pallas_call | solution.py:333
  86.8 2.8 %collective-permute-done.31.refs_6_ = f32[256,256]{1,0:T(8,128)S(1)} collective-permute-done((f32[256,256]{1,0:T(8,128)S(1)}, f32[256,256]{1,0:T(8,128)S(1)}, u32[]{:S(2)}, u32[]{:S(2)}) %collective-permute-start.31) | collective-permute-done | bytes 262176 | tf_op jit(solution)/shard_map/ppermute | solution.py:345
  89.7 2.5 %collective-permute-start.39 = (f32[264,256]{1,0:T(8,128)S(1)}, f32[264,256]{1,0:T(8,128)S(1)}, u32[]{:S(2)}, u32[]{:S(2)}) collective-permute-start(f32[264,256]{1,0:T(8,128)S(1)} %get-tuple-element.227), channel_id=1, source_target_pairs={{0,5},{1,6},{2,7},{3,0},{4,1},{5,2},{6,3},{7,4},{8,13},{9,14},{10,... | collective-permute-start | bytes 811016 | tf_op jit(solution)/shard_map/ppermute | solution.py:345
  92.5 1.7 %collective-permute-start.35 = (f32[16,256]{1,0:T(8,128)S(1)}, f32[16,256]{1,0:T(8,128)S(1)}, u32[]{:S(2)}, u32[]{:S(2)}) collective-permute-start(f32[16,256]{1,0:T(8,128)S(1)} %add_add_fusion.6), channel_id=1, source_target_pairs={{0,1},{1,0},{2,3},{3,2},{4,5},{5,4},{6,7},{7,6},{8,9},{9,8},{10,11... | collective-permute-start | bytes 49160 | tf_op jit(solution)/shard_map/ppermute | solution.py:350
  97.6 3.6 %collective-permute-done.39.refs_7_ = f32[264,256]{1,0:T(8,128)S(1)} collective-permute-done((f32[264,256]{1,0:T(8,128)S(1)}, f32[264,256]{1,0:T(8,128)S(1)}, u32[]{:S(2)}, u32[]{:S(2)}) %collective-permute-start.39) | collective-permute-done | bytes 270368 | tf_op jit(solution)/shard_map/ppermute | solution.py:345
  (84 shorter events, 32.3 us)
Async XLA Ops:
  8.4 11.7 %collective-permute-start.4 = (f32[520,256]{1,0:T(8,128)S(1)}, f32[520,256]{1,0:T(8,128)S(1)}, u32[]{:S(2)}, u32[]{:S(2)}) collective-permute-start(f32[520,256]{1,0:T(8,128)S(1)} %shard_map.147), channel_id=1, source_target_pairs={{0,1},{1,2},{2,3},{3,4},{4,5},{5,6},{6,7},{7,0},{8,9},{9,10},{10,1... | collective-permute-start | bytes 1597448 | tf_op jit(solution)/shard_map/ppermute | solution.py:345
  11.3 6.1 %collective-permute-start.3 = (f32[64,256]{1,0:T(8,128)S(1)}, f32[64,256]{1,0:T(8,128)S(1)}, u32[]{:S(2)}, u32[]{:S(2)}) collective-permute-start(f32[64,256]{1,0:T(8,128)S(1)} %add.84), channel_id=1, source_target_pairs={{0,24},{8,16},{16,8},{24,0},{1,25},{9,17},{17,9},{25,1},{2,26},{10... | collective-permute-start | bytes 196616 | tf_op jit(solution)/shard_map/ppermute | solution.py:350
  17.6 5.1 %collective-permute-start.7 = (f32[64,256]{1,0:T(8,128)S(1)}, f32[64,256]{1,0:T(8,128)S(1)}, u32[]{:S(2)}, u32[]{:S(2)}) collective-permute-start(f32[64,256]{1,0:T(8,128)S(1)} %add_add_fusion.5), channel_id=1, source_target_pairs={{0,6},{1,7},{2,4},{3,5},{4,2},{5,3},{6,0},{7,1},{8,14},{9,15},{10,... | collective-permute-start | bytes 196616 | tf_op jit(solution)/shard_map/ppermute | solution.py:350
  19.7 7.0 %collective-permute-start.6 = (f32[64,256]{1,0:T(8,128)S(1)}, f32[64,256]{1,0:T(8,128)S(1)}, u32[]{:S(2)}, u32[]{:S(2)}) collective-permute-start(f32[64,256]{1,0:T(8,128)S(1)} %add_add_fusion.5), channel_id=1, source_target_pairs={{0,4},{1,5},{2,6},{3,7},{4,0},{5,1},{6,2},{7,3},{8,12},{9,13},{10,... | collective-permute-start | bytes 196616 | tf_op jit(solution)/shard_map/ppermute | solution.py:350
  20.2 6.5 %collective-permute-start.5 = (f32[64,256]{1,0:T(8,128)S(1)}, f32[64,256]{1,0:T(8,128)S(1)}, u32[]{:S(2)}, u32[]{:S(2)}) collective-permute-start(f32[64,256]{1,0:T(8,128)S(1)} %add_add_fusion.5), channel_id=1, source_target_pairs={{0,2},{1,3},{2,0},{3,1},{4,6},{5,7},{6,4},{7,5},{8,10},{9,11},{10,... | collective-permute-start | bytes 196616 | tf_op jit(solution)/shard_map/ppermute | solution.py:350
  33.3 10.0 %collective-permute-start.13 = (f32[520,256]{1,0:T(8,128)S(1)}, f32[520,256]{1,0:T(8,128)S(1)}, u32[]{:S(2)}, u32[]{:S(2)}) collective-permute-start(f32[520,256]{1,0:T(8,128)S(1)} %shard_map.150), channel_id=1, source_target_pairs={{0,1},{1,2},{2,3},{3,4},{4,5},{5,6},{6,7},{7,0},{8,9},{9,10},{10,1... | collective-permute-start | bytes 1597448 | tf_op jit(solution)/shard_map/ppermute | solution.py:345
  33.6 6.1 %collective-permute-start.12 = (f32[64,256]{1,0:T(8,128)S(1)}, f32[64,256]{1,0:T(8,128)S(1)}, u32[]{:S(2)}, u32[]{:S(2)}) collective-permute-start(f32[64,256]{1,0:T(8,128)S(1)} %add.91), channel_id=1, source_target_pairs={{0,24},{8,16},{16,8},{24,0},{1,25},{9,17},{17,9},{25,1},{2,26},{10... | collective-permute-start | bytes 196616 | tf_op jit(solution)/shard_map/ppermute | solution.py:350
  39.8 5.2 %collective-permute-start.16 = (f32[64,256]{1,0:T(8,128)S(1)}, f32[64,256]{1,0:T(8,128)S(1)}, u32[]{:S(2)}, u32[]{:S(2)}) collective-permute-start(f32[64,256]{1,0:T(8,128)S(1)} %add_add_fusion.3), channel_id=1, source_target_pairs={{0,6},{1,7},{2,4},{3,5},{4,2},{5,3},{6,0},{7,1},{8,14},{9,15},{10,... | collective-permute-start | bytes 196616 | tf_op jit(solution)/shard_map/ppermute | solution.py:350
  43.3 6.2 %collective-permute-start.15 = (f32[64,256]{1,0:T(8,128)S(1)}, f32[64,256]{1,0:T(8,128)S(1)}, u32[]{:S(2)}, u32[]{:S(2)}) collective-permute-start(f32[64,256]{1,0:T(8,128)S(1)} %add_add_fusion.3), channel_id=1, source_target_pairs={{0,4},{1,5},{2,6},{3,7},{4,0},{5,1},{6,2},{7,3},{8,12},{9,13},{10,... | collective-permute-start | bytes 196616 | tf_op jit(solution)/shard_map/ppermute | solution.py:350
  43.3 6.2 %collective-permute-start.14 = (f32[64,256]{1,0:T(8,128)S(1)}, f32[64,256]{1,0:T(8,128)S(1)}, u32[]{:S(2)}, u32[]{:S(2)}) collective-permute-start(f32[64,256]{1,0:T(8,128)S(1)} %add_add_fusion.3), channel_id=1, source_target_pairs={{0,2},{1,3},{2,0},{3,1},{4,6},{5,7},{6,4},{7,5},{8,10},{9,11},{10,... | collective-permute-start | bytes 196616 | tf_op jit(solution)/shard_map/ppermute | solution.py:350
  55.7 10.0 %collective-permute-start.22 = (f32[520,256]{1,0:T(8,128)S(1)}, f32[520,256]{1,0:T(8,128)S(1)}, u32[]{:S(2)}, u32[]{:S(2)}) collective-permute-start(f32[520,256]{1,0:T(8,128)S(1)} %shard_map.153), channel_id=1, source_target_pairs={{0,1},{1,2},{2,3},{3,4},{4,5},{5,6},{6,7},{7,0},{8,9},{9,10},{10,1... | collective-permute-start | bytes 1597448 | tf_op jit(solution)/shard_map/ppermute | solution.py:345
  56.7 6.2 %collective-permute-start.21 = (f32[64,256]{1,0:T(8,128)S(1)}, f32[64,256]{1,0:T(8,128)S(1)}, u32[]{:S(2)}, u32[]{:S(2)}) collective-permute-start(f32[64,256]{1,0:T(8,128)S(1)} %add.98), channel_id=1, source_target_pairs={{0,24},{8,16},{16,8},{24,0},{1,25},{9,17},{17,9},{25,1},{2,26},{10... | collective-permute-start | bytes 196616 | tf_op jit(solution)/shard_map/ppermute | solution.py:350
  58.6 4.5 %collective-permute-start.20 = (f32[64,256]{1,0:T(8,128)S(1)}, f32[64,256]{1,0:T(8,128)S(1)}, u32[]{:S(2)}, u32[]{:S(2)}) collective-permute-start(f32[64,256]{1,0:T(8,128)S(1)} %add.98), channel_id=1, source_target_pairs={{0,16},{8,24},{16,0},{24,8},{1,17},{9,25},{17,1},{25,9},{2,18},{10... | collective-permute-start | bytes 196616 | tf_op jit(solution)/shard_map/ppermute | solution.py:350
  63.1 5.1 %collective-permute-start.25 = (f32[64,256]{1,0:T(8,128)S(1)}, f32[64,256]{1,0:T(8,128)S(1)}, u32[]{:S(2)}, u32[]{:S(2)}) collective-permute-start(f32[64,256]{1,0:T(8,128)S(1)} %add_add_fusion.1), channel_id=1, source_target_pairs={{0,6},{1,7},{2,4},{3,5},{4,2},{5,3},{6,0},{7,1},{8,14},{9,15},{10,... | collective-permute-start | bytes 196616 | tf_op jit(solution)/shard_map/ppermute | solution.py:350
  65.7 6.3 %collective-permute-start.24 = (f32[64,256]{1,0:T(8,128)S(1)}, f32[64,256]{1,0:T(8,128)S(1)}, u32[]{:S(2)}, u32[]{:S(2)}) collective-permute-start(f32[64,256]{1,0:T(8,128)S(1)} %add_add_fusion.1), channel_id=1, source_target_pairs={{0,4},{1,5},{2,6},{3,7},{4,0},{5,1},{6,2},{7,3},{8,12},{9,13},{10,... | collective-permute-start | bytes 196616 | tf_op jit(solution)/shard_map/ppermute | solution.py:350
  65.7 6.3 %collective-permute-start.23 = (f32[64,256]{1,0:T(8,128)S(1)}, f32[64,256]{1,0:T(8,128)S(1)}, u32[]{:S(2)}, u32[]{:S(2)}) collective-permute-start(f32[64,256]{1,0:T(8,128)S(1)} %add_add_fusion.1), channel_id=1, source_target_pairs={{0,2},{1,3},{2,0},{3,1},{4,6},{5,7},{6,4},{7,5},{8,10},{9,11},{10,... | collective-permute-start | bytes 196616 | tf_op jit(solution)/shard_map/ppermute | solution.py:350
  78.5 11.1 %collective-permute-start.31 = (f32[256,256]{1,0:T(8,128)S(1)}, f32[256,256]{1,0:T(8,128)S(1)}, u32[]{:S(2)}, u32[]{:S(2)}) collective-permute-start(f32[256,256]{1,0:T(8,128)S(1)} %get-tuple-element.222), channel_id=1, source_target_pairs={{0,5},{1,6},{2,7},{3,0},{4,1},{5,2},{6,3},{7,4},{8,13},{9,14},{10,... | collective-permute-start | bytes 786440 | tf_op jit(solution)/shard_map/ppermute | solution.py:345
  80.6 5.5 %collective-permute-start.29 = (f32[16,256]{1,0:T(8,128)S(1)}, f32[16,256]{1,0:T(8,128)S(1)}, u32[]{:S(2)}, u32[]{:S(2)}) collective-permute-start(f32[16,256]{1,0:T(8,128)S(1)} %get-tuple-element.232), channel_id=1, source_target_pairs={{0,16},{8,24},{16,0},{24,8},{1,17},{9,25},{17,1},{25,9},{2,18},{10... | collective-permute-start | bytes 49160 | tf_op jit(solution)/shard_map/ppermute | solution.py:350
  86.1 6.1 %collective-permute-start.34 = (f32[16,256]{1,0:T(8,128)S(1)}, f32[16,256]{1,0:T(8,128)S(1)}, u32[]{:S(2)}, u32[]{:S(2)}) collective-permute-start(f32[16,256]{1,0:T(8,128)S(1)} %slice_add_fusion), channel_id=1, source_target_pairs={{0,6},{1,7},{2,4},{3,5},{4,2},{5,3},{6,0},{7,1},{8,14},{9,15},{10,... | collective-permute-start | bytes 49160 | tf_op jit(solution)/shard_map/ppermute | solution.py:350
  86.2 6.1 %collective-permute-start.33 = (f32[16,256]{1,0:T(8,128)S(1)}, f32[16,256]{1,0:T(8,128)S(1)}, u32[]{:S(2)}, u32[]{:S(2)}) collective-permute-start(f32[16,256]{1,0:T(8,128)S(1)} %slice_add_fusion), channel_id=1, source_target_pairs={{0,4},{1,5},{2,6},{3,7},{4,0},{5,1},{6,2},{7,3},{8,12},{9,13},{10,... | collective-permute-start | bytes 49160 | tf_op jit(solution)/shard_map/ppermute | solution.py:350
  89.7 11.5 %collective-permute-start.39 = (f32[264,256]{1,0:T(8,128)S(1)}, f32[264,256]{1,0:T(8,128)S(1)}, u32[]{:S(2)}, u32[]{:S(2)}) collective-permute-start(f32[264,256]{1,0:T(8,128)S(1)} %get-tuple-element.227), channel_id=1, source_target_pairs={{0,5},{1,6},{2,7},{3,0},{4,1},{5,2},{6,3},{7,4},{8,13},{9,14},{10,... | collective-permute-start | bytes 811016 | tf_op jit(solution)/shard_map/ppermute | solution.py:345
  95.0 6.2 %collective-permute-start.38 = (f32[32,256]{1,0:T(8,128)S(1)}, f32[32,256]{1,0:T(8,128)S(1)}, u32[]{:S(2)}, u32[]{:S(2)}) collective-permute-start(f32[32,256]{1,0:T(8,128)S(1)} %pad_maximum_fusion.refs_0_), channel_id=1, source_target_pairs={{0,24},{8,16},{16,8},{24,0},{1,25},{9,17},{17,9},{25,1},{2,26},{10... | collective-permute-start | bytes 98312 | tf_op jit(solution)/shard_map/ppermute | solution.py:350
  96.5 4.8 %collective-permute-start.37 = (f32[32,256]{1,0:T(8,128)S(1)}, f32[32,256]{1,0:T(8,128)S(1)}, u32[]{:S(2)}, u32[]{:S(2)}) collective-permute-start(f32[32,256]{1,0:T(8,128)S(1)} %pad_maximum_fusion.refs_0_), channel_id=1, source_target_pairs={{0,16},{8,24},{16,0},{24,8},{1,17},{9,25},{17,1},{25,9},{2,18},{10... | collective-permute-start | bytes 98312 | tf_op jit(solution)/shard_map/ppermute | solution.py:350
  96.9 4.3 %collective-permute-start.36 = (f32[32,256]{1,0:T(8,128)S(1)}, f32[32,256]{1,0:T(8,128)S(1)}, u32[]{:S(2)}, u32[]{:S(2)}) collective-permute-start(f32[32,256]{1,0:T(8,128)S(1)} %pad_maximum_fusion.refs_0_), channel_id=1, source_target_pairs={{0,8},{8,0},{16,24},{24,16},{1,9},{9,1},{17,25},{25,17},{2,10},{10... | collective-permute-start | bytes 98312 | tf_op jit(solution)/shard_map/ppermute | solution.py:350
  (16 other events, 45.1 us)
